TPU v7x, 256 devices: a whole 4x4x8 slice. The times are simulated.
256 devices in a mesh: ctx: 32 (over z, x), batch: 8 (over y, core).
Axes of the slice: x: 4, y: 4, z: 8, core: 2. Of those that a mesh axis runs over, the one named last changes fastest.
Arguments:
- kda_query: bfloat16 [32768, 2048], P(('batch', 'ctx')), parts along dimension 0, may hold values from -6 to 6
- kda_key: bfloat16 [32768, 2048], P(('batch', 'ctx')), parts along dimension 0, may hold values from -6 to 6
- kda_value: bfloat16 [32768, 2048], P(('batch', 'ctx')), parts along dimension 0, may hold values from -6 to 6
- log_decay: bfloat16 [32768, 2048], P(('batch', 'ctx')), parts along dimension 0, may hold values from -2 to 0
- write_rate: float32 [32768, 16], P(('batch', 'ctx')), parts along dimension 0, may hold values from 0.01 to 0.9
- mla_query: bfloat16 [32768, 3072], P(('batch', 'ctx')), parts along dimension 0, may hold values from -8 to 8
- latents: bfloat16 [32768, 576], P(('batch', 'ctx')), parts along dimension 0, may hold values from -8 to 8
- key_up: bfloat16 [512, 2048], replicated, may hold values from -0.25 to 0.25
- value_up: bfloat16 [512, 2048], replicated, may hold values from -0.25 to 0.25
- doc_lengths: int32 [64], P('batch'), parts along dimension 0, may hold values from 1 to 2048, 4096 in all
Outputs:
- kda_out: bfloat16 [32768, 2048], P(('batch', 'ctx')), parts along dimension 0
- mla_out: bfloat16 [32768, 2048], P(('batch', 'ctx')), parts along dimension 0
There are 8 independent parts, one for each index of `batch`. A program takes and returns all parts, laid end to end along the dimension named above; an argument that names none is the same for every part. Nothing has to cross between parts.
Inputs may be any that keep to these rules, and one draw needn't show every extreme that they name: `doc_lengths`: 8 lengths of the documents of one context in order; they sum to 4096 and the longest is exactly 2048.
All inputs are finite; a program needn't handle non-finite values.
Results may differ from a plain program's by a relative error of at most 0.009.
Values may be sent and summed in bfloat16 or wider, within the bound.
A program may use at most 192 MiB of HBM per device.

v0:
```python
import math

import jax
import jax.numpy as jnp
from jax import lax
from jax.sharding import PartitionSpec as P

NOPE = 128
ROPE = 64
LATENT = 512
BLOCK = 64


PRECISE_PRODUCT = lax.Precision.HIGHEST


def prefix(array, axis, join, neutral):
    place = lax.axis_index(axis)
    gathered = jax.tree.map(
        lambda a, kind: lax.all_gather(a.astype(kind), axis),
        array,
        jax.tree.map(lambda a: jnp.bfloat16 if a.dtype == jnp.float32 else a.dtype, array),
    )
    state = jax.tree.map(lambda a, e: jnp.zeros_like(a) + jnp.asarray(e, a.dtype), array, neutral)

    def one(step, state):
        return join(
            state,
            jax.tree.map(
                lambda a, own: lax.dynamic_index_in_dim(a, step, 0, False).astype(own.dtype),
                gathered,
                array,
            ),
        )

    return lax.fori_loop(0, place, one, state)


def shifted(block, axis, distance):
    devices = range(lax.axis_size(axis))
    route = [(i - distance, i) for i in devices if i - distance in devices]
    return lax.ppermute(block, axis, route)


def unit_rows(values):
    return values * lax.rsqrt(jnp.sum(values * values, axis=-1, keepdims=True) + 1e-06)


def doc_of(positions, doc_starts):
    match_count = (doc_starts[None, :] <= positions[:, None]).astype(jnp.int32)
    return jnp.sum(match_count, axis=1) - 1


def unit_lower_inverse(strictly_lower):
    length = strictly_lower.shape[-1]
    identity = jnp.eye(length, dtype=jnp.float32)[None]
    result = identity - strictly_lower
    power_term = strictly_lower
    for level_index in range(length.bit_length() - 2):
        power_term = jnp.einsum("hij,hjk->hik", power_term, power_term, precision=PRECISE_PRODUCT)
        result = jnp.einsum(
            "hij,hjk->hik", result, identity + power_term, precision=PRECISE_PRODUCT
        )
    return result


def block_terms(query_unit, keyvec, valvec, logarithm_decay, write_gain, docids, prevdoc):
    length = docids.shape[0]
    cumulative = jnp.cumsum(logarithm_decay, axis=0)
    growth = jnp.exp(cumulative)
    key_plus = keyvec * growth
    key_minus = keyvec * jnp.exp(-cumulative)
    query_plus = query_unit * growth
    places = jnp.arange(length)
    same_doc = docids[:, None] == docids[None, :]
    strict = (places[:, None] > places[None, :]) & same_doc
    causal = (places[:, None] >= places[None, :]) & same_doc
    follow = (docids == prevdoc).astype(jnp.float32)
    inner_prod = jnp.einsum("thk,shk->hts", key_plus, key_minus, precision=PRECISE_PRODUCT)
    strictly_lower = (
        jnp.where(strict[None], inner_prod, 0.0) * jnp.transpose(write_gain)[:, :, None]
    )
    inverse = unit_lower_inverse(strictly_lower)
    value_rhs = jnp.transpose(valvec * write_gain[:, :, None], (1, 0, 2))
    key_rhs = jnp.transpose(key_plus * (write_gain * follow[:, None])[:, :, None], (1, 0, 2))
    value_solution = jnp.einsum("hts,hsv->htv", inverse, value_rhs, precision=PRECISE_PRODUCT)
    solved_key = jnp.einsum("hts,hsk->htk", inverse, key_rhs, precision=PRECISE_PRODUCT)
    mixing = jnp.where(
        causal[None],
        jnp.einsum("thk,shk->hts", query_plus, key_minus, precision=PRECISE_PRODUCT),
        0.0,
    )
    local_output = jnp.einsum("hts,hsv->htv", mixing, value_solution, precision=PRECISE_PRODUCT)
    query_effective = jnp.transpose(query_plus * follow[:, None, None], (1, 0, 2)) - jnp.einsum(
        "hts,hsk->htk", mixing, solved_key, precision=PRECISE_PRODUCT
    )
    last_doc = (docids == docids[length - 1]).astype(jnp.float32)
    key_trailing = (
        keyvec * jnp.exp(cumulative[length - 1][None] - cumulative) * last_doc[:, None, None]
    )
    growth_last = growth[length - 1]
    diagonal_map = growth_last[:, :, None] * jnp.eye(keyvec.shape[2], dtype=jnp.float32)[None]
    handed_operator = follow[length - 1] * diagonal_map - jnp.einsum(
        "shk,hsj->hkj", key_trailing, solved_key, precision=PRECISE_PRODUCT
    )
    handed_update = jnp.einsum(
        "omt,mor->mtr", key_trailing, value_solution, precision=PRECISE_PRODUCT
    )
    return (local_output, query_effective, handed_operator, handed_update)


def compose(prior_slab, successor_slab):
    joined_map = jnp.einsum(
        "hkj,hjl->hkl", successor_slab[0], prior_slab[0], precision=PRECISE_PRODUCT
    )
    combined_increment = (
        jnp.einsum("ytn,yne->yte", successor_slab[0], prior_slab[1], precision=PRECISE_PRODUCT)
        + successor_slab[1]
    )
    return (joined_map, combined_increment)


def local(
    kda_query,
    kda_key,
    kda_value,
    log_decay,
    write_rate,
    mla_query,
    latents,
    key_up,
    value_up,
    doc_lengths,
):
    slab_rows = latents.shape[0]
    head_count = write_rate.shape[1]
    first_row = lax.axis_index("ctx") * slab_rows
    doc_starts = jnp.cumsum(doc_lengths) - doc_lengths
    positions = first_row + jnp.arange(slab_rows, dtype=jnp.int32)
    docids = doc_of(positions, doc_starts)
    query_unit = unit_rows(kda_query.astype(jnp.float32).reshape(slab_rows, head_count, -1))
    keyvec = unit_rows(kda_key.astype(jnp.float32).reshape(slab_rows, head_count, -1))
    valvec = kda_value.astype(jnp.float32).reshape(slab_rows, head_count, -1)
    logarithm_decay = log_decay.astype(jnp.float32).reshape(slab_rows, head_count, -1)
    block_count = slab_rows // BLOCK
    prevdocs = doc_of(first_row + jnp.arange(block_count, dtype=jnp.int32) * BLOCK - 1, doc_starts)

    def shaped(values):
        return values.reshape((block_count, BLOCK) + values.shape[1:])

    block_outs = jax.vmap(block_terms)(
        shaped(query_unit),
        shaped(keyvec),
        shaped(valvec),
        shaped(logarithm_decay),
        shaped(write_rate),
        shaped(docids),
        prevdocs,
    )
    key_dim = keyvec.shape[2]
    value_dim = valvec.shape[2]
    identity_map = jnp.broadcast_to(
        jnp.eye(key_dim, dtype=jnp.float32)[None], (head_count, key_dim, key_dim)
    )
    zero_add = jnp.zeros((head_count, key_dim, value_dim), jnp.float32)

    def advance_block(prefix_pair, block_item):
        map_before, update_from_prior = prefix_pair
        local_output, query_effective, handed_operator, handed_update = block_item
        eff_now = jnp.einsum("htk,hkj->htj", query_effective, map_before, precision=PRECISE_PRODUCT)
        output_current = local_output + jnp.einsum(
            "cor,crm->com", query_effective, update_from_prior, precision=PRECISE_PRODUCT
        )
        map_after = jnp.einsum(
            "hkj,hjl->hkl", handed_operator, map_before, precision=PRECISE_PRODUCT
        )
        increment_later = (
            jnp.einsum(
                "ytn,yne->yte", handed_operator, update_from_prior, precision=PRECISE_PRODUCT
            )
            + handed_update
        )
        return ((map_after, increment_later), (eff_now, output_current))

    slab_pair, per_block = lax.scan(advance_block, (identity_map, zero_add), block_outs)
    effective_everything, output_everything = per_block
    leading_part = prefix(slab_pair, "ctx", compose, (identity_map, zero_add))
    delta_attention_complete = output_everything + jnp.einsum(
        "enzx,nxu->enzu", effective_everything, leading_part[1], precision=PRECISE_PRODUCT
    )
    kda_out = (
        jnp.transpose(delta_attention_complete, (0, 2, 1, 3))
        .reshape(slab_rows, -1)
        .astype(jnp.bfloat16)
    )
    queries = mla_query.reshape(slab_rows, head_count, NOPE + ROPE)
    query_nope = queries[:, :, :NOPE]
    query_rope = queries[:, :, NOPE:]
    score_scale = 1.0 / math.sqrt(NOPE + ROPE)
    last_place = positions[slab_rows - 1]
    first_doc_start = jnp.sum(
        jnp.where(jnp.arange(doc_starts.shape[0]) == docids[0], doc_starts, 0)
    )

    def attend_rows(softmax_state, key_rows, key_first):
        running_max, running_sum, accumulated = softmax_state
        row_count = key_rows.shape[0]
        latent_part = key_rows[:, :LATENT]
        keys_nope = (
            jnp.dot(latent_part, key_up, preferred_element_type=jnp.float32)
            .astype(jnp.bfloat16)
            .reshape(row_count, head_count, NOPE)
        )
        values = (
            jnp.dot(latent_part, value_up, preferred_element_type=jnp.float32)
            .astype(jnp.bfloat16)
            .reshape(row_count, head_count, -1)
        )
        scores = jnp.einsum(
            "thd,shd->hts", query_nope, keys_nope, preferred_element_type=jnp.float32
        )
        scores = (
            scores
            + jnp.einsum(
                "thr,sr->hts", query_rope, key_rows[:, LATENT:], preferred_element_type=jnp.float32
            )
        ) * score_scale
        key_places = key_first + jnp.arange(row_count, dtype=jnp.int32)
        key_docs = doc_of(key_places, doc_starts)
        allowed = (key_places[None, :] <= positions[:, None]) & (
            key_docs[None, :] == docids[:, None]
        )
        masked = jnp.where(allowed[None], scores, -1e30)
        new_max = jnp.maximum(running_max, jnp.max(masked, axis=2))
        weights = jnp.where(allowed[None], jnp.exp(masked - new_max[:, :, None]), 0.0)
        factor = jnp.exp(running_max - new_max)
        running_sum = running_sum * factor + jnp.sum(weights, axis=2)
        product = jnp.einsum(
            "hts,shv->thv", weights.astype(jnp.bfloat16), values, preferred_element_type=jnp.float32
        )
        accumulated = accumulated * jnp.transpose(factor)[:, :, None] + product
        return (new_max, running_sum, accumulated)

    def guarded(softmax_state, key_rows, key_first):
        row_count = key_rows.shape[0]
        needed = (key_first <= last_place) & (key_first + row_count - 1 >= first_doc_start)
        return lax.cond(
            needed, lambda: attend_rows(softmax_state, key_rows, key_first), lambda: softmax_state
        )

    value_width = value_up.shape[1] // head_count
    initial_state = (
        jnp.full((head_count, slab_rows), -1e30, jnp.float32),
        jnp.zeros((head_count, slab_rows), jnp.float32),
        jnp.zeros((slab_rows, head_count, value_width), jnp.float32),
    )
    own_state = guarded(initial_state, latents, first_row)

    def advance_window(step_index, window_pair):
        carried_state, moving = window_pair
        moving = shifted(moving, "ctx", 1)
        carried_state = guarded(carried_state, moving, first_row - (step_index + 1) * slab_rows)
        return (carried_state, moving)

    softmax_state, _ = lax.fori_loop(
        0, lax.axis_size("ctx") // 2, advance_window, (own_state, latents)
    )
    running_sum = softmax_state[1]
    accumulated = softmax_state[2]
    mla_out = (
        (accumulated / jnp.transpose(running_sum)[:, :, None])
        .astype(jnp.bfloat16)
        .reshape(slab_rows, -1)
    )
    return (kda_out, mla_out)


def solution(mesh):
    in_specs = (
        P(("batch", "ctx"), None),
        P(("batch", "ctx"), None),
        P(("batch", "ctx"), None),
        P(("batch", "ctx"), None),
        P(("batch", "ctx"), None),
        P(("batch", "ctx"), None),
        P(("batch", "ctx"), None),
        P(),
        P(),
        P("batch"),
    )
    out_specs = (P(("batch", "ctx"), None), P(("batch", "ctx"), None))
    return jax.shard_map(local, mesh=mesh, in_specs=in_specs, out_specs=out_specs, check_vma=False)
```

profile of v0, /device:TPU:144, one launch (start us, length us, event | category | flops | bytes accessed | tf_op | source)
XLA Modules:
  0.0 551.0 jit_solution(9183807061820889483)
XLA Ops:
  69.6 23.3 %while.55 = (s32[]{:T(128)}, f32[16,128,128]{2,1,0:T(8,128)}, f32[16,128,128]{2,1,0:T(8,128)}, f32[2,16,64,128]{3,2,0,1:T(8,128)}, f32[2,16,64,128]{3,2,0,1:T(8,...) while((s32[]{:T(128)}, f32[16,128,128]{2,1,0:T(8,128)}, ...), condition=%wide.region_7.8_spmd.clone, body=%wide.region_6.7_spmd.clone.sunk | while | flops 1208877056 | bytes 41423116 | solution.py:185
  104.7 12.8 %conditional.2 = (f32[16,128]{1,0:T(8,128)}, f32[16,128]{1,0:T(8,128)}, f32[128,16,128]{0,2,1:T(8,128)}) conditional(s32[]{:T(128)} %convert_element_type.143, () %tuple.66, (s32[]{:T(128)}, s32[128]{0:T(128)}, s32[8]{0:T(128)}, s32[128]{0:T(128)}, bf16[128,576]{0,1:T(8,128)(2,1)}, /*index=5*/bf16[512,2048]{1,0:T(8,128)(2,1)S(1)}, ...), branch_computations={%region_11.12_spmd, %region_12.16_spmd} | conditional | flops 708111488 | bytes 26002304 | solution.py:247
  117.5 388.1 %while.56 = (s32[]{:T(128)}, f32[16,128]{1,0:T(8,128)}, f32[16,128]{1,0:T(8,128)}, f32[128,16,128]{0,2,1:T(8,128)}, bf16[128,576]{0,1:T(8,128)(2,1)}, /*index=5*...) while((s32[]{:T(128)}, f32[16,128]{1,0:T(8,128)}, ...), condition=%wide.region_22.23_spmd.clone.clone, body=%wide.region_16.22_spmd.clone.clone.sunk | while | flops 708371712 | bytes 27419380 | solution.py:265
  131.7 11.1 %conditional.6 = ((f32[16,128]{1,0:T(8,128)}, f32[16,128]{1,0:T(8,128)}, f32[128,16,128]{0,2,1:T(8,128)})) conditional(s32[]{:T(128)} %convert_element_type.183, (f32[16,128]{1,0:T(8,128)}, f32[16,128]{1,0:T(8,128)}, f32[128,16,128]{0,2,1:T(8,128)}) %tuple.130, (s32[]{:T(128)}, s32[]{:T(128)}, s32[8]{0:T(128)}, s32[128]{0:T(128)}, ...), branch_computations={%region_17.17_spmd, %region_18.21_spmd} | conditional | flops 708371712 | bytes 26533744 | solution.py:247
  154.1 11.2 %conditional.6 = ((f32[16,128]{1,0:T(8,128)}, f32[16,128]{1,0:T(8,128)}, f32[128,16,128]{0,2,1:T(8,128)})) conditional(s32[]{:T(128)} %convert_element_type.183, (f32[16,128]{1,0:T(8,128)}, f32[16,128]{1,0:T(8,128)}, f32[128,16,128]{0,2,1:T(8,128)}) %tuple.130, (s32[]{:T(128)}, s32[]{:T(128)}, s32[8]{0:T(128)}, s32[128]{0:T(128)}, ...), branch_computations={%region_17.17_spmd, %region_18.21_spmd} | conditional | flops 708371712 | bytes 26533744 | solution.py:247
  169.1 10.5 %collective-permute-done = bf16[128,576]{0,1:T(8,128)(2,1)S(1)} collective-permute-done((bf16[128,576]{0,1:T(8,128)(2,1)}, bf16[128,576]{0,1:T(8,128)(2,1)S(1)}, u32[]{:S(2)}, u32[]{:S(2)}) %collective-permute-start) | collective-permute-done | bytes 147488 | tf_op jit(solution)/shard_map/while/body/eval_jaxpr/ppermute | solution.py:42
  179.6 11.1 %conditional.6 = ((f32[16,128]{1,0:T(8,128)}, f32[16,128]{1,0:T(8,128)}, f32[128,16,128]{0,2,1:T(8,128)})) conditional(s32[]{:T(128)} %convert_element_type.183, (f32[16,128]{1,0:T(8,128)}, f32[16,128]{1,0:T(8,128)}, f32[128,16,128]{0,2,1:T(8,128)}) %tuple.130, (s32[]{:T(128)}, s32[]{:T(128)}, s32[8]{0:T(128)}, s32[128]{0:T(128)}, ...), branch_computations={%region_17.17_spmd, %region_18.21_spmd} | conditional | flops 708371712 | bytes 26533744 | solution.py:247
  194.6 10.8 %collective-permute-done = bf16[128,576]{0,1:T(8,128)(2,1)S(1)} collective-permute-done((bf16[128,576]{0,1:T(8,128)(2,1)}, bf16[128,576]{0,1:T(8,128)(2,1)S(1)}, u32[]{:S(2)}, u32[]{:S(2)}) %collective-permute-start) | collective-permute-done | bytes 147488 | tf_op jit(solution)/shard_map/while/body/eval_jaxpr/ppermute | solution.py:42
  205.5 11.1 %conditional.6 = ((f32[16,128]{1,0:T(8,128)}, f32[16,128]{1,0:T(8,128)}, f32[128,16,128]{0,2,1:T(8,128)})) conditional(s32[]{:T(128)} %convert_element_type.183, (f32[16,128]{1,0:T(8,128)}, f32[16,128]{1,0:T(8,128)}, f32[128,16,128]{0,2,1:T(8,128)}) %tuple.130, (s32[]{:T(128)}, s32[]{:T(128)}, s32[8]{0:T(128)}, s32[128]{0:T(128)}, ...), branch_computations={%region_17.17_spmd, %region_18.21_spmd} | conditional | flops 708371712 | bytes 26533744 | solution.py:247
  220.5 10.5 %collective-permute-done = bf16[128,576]{0,1:T(8,128)(2,1)S(1)} collective-permute-done((bf16[128,576]{0,1:T(8,128)(2,1)}, bf16[128,576]{0,1:T(8,128)(2,1)S(1)}, u32[]{:S(2)}, u32[]{:S(2)}) %collective-permute-start) | collective-permute-done | bytes 147488 | tf_op jit(solution)/shard_map/while/body/eval_jaxpr/ppermute | solution.py:42
  231.0 11.1 %conditional.6 = ((f32[16,128]{1,0:T(8,128)}, f32[16,128]{1,0:T(8,128)}, f32[128,16,128]{0,2,1:T(8,128)})) conditional(s32[]{:T(128)} %convert_element_type.183, (f32[16,128]{1,0:T(8,128)}, f32[16,128]{1,0:T(8,128)}, f32[128,16,128]{0,2,1:T(8,128)}) %tuple.130, (s32[]{:T(128)}, s32[]{:T(128)}, s32[8]{0:T(128)}, s32[128]{0:T(128)}, ...), branch_computations={%region_17.17_spmd, %region_18.21_spmd} | conditional | flops 708371712 | bytes 26533744 | solution.py:247
  253.4 11.1 %conditional.6 = ((f32[16,128]{1,0:T(8,128)}, f32[16,128]{1,0:T(8,128)}, f32[128,16,128]{0,2,1:T(8,128)})) conditional(s32[]{:T(128)} %convert_element_type.183, (f32[16,128]{1,0:T(8,128)}, f32[16,128]{1,0:T(8,128)}, f32[128,16,128]{0,2,1:T(8,128)}) %tuple.130, (s32[]{:T(128)}, s32[]{:T(128)}, s32[8]{0:T(128)}, s32[128]{0:T(128)}, ...), branch_computations={%region_17.17_spmd, %region_18.21_spmd} | conditional | flops 708371712 | bytes 26533744 | solution.py:247
  278.6 11.1 %conditional.6 = ((f32[16,128]{1,0:T(8,128)}, f32[16,128]{1,0:T(8,128)}, f32[128,16,128]{0,2,1:T(8,128)})) conditional(s32[]{:T(128)} %convert_element_type.183, (f32[16,128]{1,0:T(8,128)}, f32[16,128]{1,0:T(8,128)}, f32[128,16,128]{0,2,1:T(8,128)}) %tuple.130, (s32[]{:T(128)}, s32[]{:T(128)}, s32[8]{0:T(128)}, s32[128]{0:T(128)}, ...), branch_computations={%region_17.17_spmd, %region_18.21_spmd} | conditional | flops 708371712 | bytes 26533744 | solution.py:247
  301.8 11.1 %conditional.6 = ((f32[16,128]{1,0:T(8,128)}, f32[16,128]{1,0:T(8,128)}, f32[128,16,128]{0,2,1:T(8,128)})) conditional(s32[]{:T(128)} %convert_element_type.183, (f32[16,128]{1,0:T(8,128)}, f32[16,128]{1,0:T(8,128)}, f32[128,16,128]{0,2,1:T(8,128)}) %tuple.130, (s32[]{:T(128)}, s32[]{:T(128)}, s32[8]{0:T(128)}, s32[128]{0:T(128)}, ...), branch_computations={%region_17.17_spmd, %region_18.21_spmd} | conditional | flops 708371712 | bytes 26533744 | solution.py:247
  327.2 11.2 %conditional.6 = ((f32[16,128]{1,0:T(8,128)}, f32[16,128]{1,0:T(8,128)}, f32[128,16,128]{0,2,1:T(8,128)})) conditional(s32[]{:T(128)} %convert_element_type.183, (f32[16,128]{1,0:T(8,128)}, f32[16,128]{1,0:T(8,128)}, f32[128,16,128]{0,2,1:T(8,128)}) %tuple.130, (s32[]{:T(128)}, s32[]{:T(128)}, s32[8]{0:T(128)}, s32[128]{0:T(128)}, ...), branch_computations={%region_17.17_spmd, %region_18.21_spmd} | conditional | flops 708371712 | bytes 26533744 | solution.py:247
  352.7 11.1 %conditional.6 = ((f32[16,128]{1,0:T(8,128)}, f32[16,128]{1,0:T(8,128)}, f32[128,16,128]{0,2,1:T(8,128)})) conditional(s32[]{:T(128)} %convert_element_type.183, (f32[16,128]{1,0:T(8,128)}, f32[16,128]{1,0:T(8,128)}, f32[128,16,128]{0,2,1:T(8,128)}) %tuple.130, (s32[]{:T(128)}, s32[]{:T(128)}, s32[8]{0:T(128)}, s32[128]{0:T(128)}, ...), branch_computations={%region_17.17_spmd, %region_18.21_spmd} | conditional | flops 708371712 | bytes 26533744 | solution.py:247
  367.7 11.5 %collective-permute-done = bf16[128,576]{0,1:T(8,128)(2,1)S(1)} collective-permute-done((bf16[128,576]{0,1:T(8,128)(2,1)}, bf16[128,576]{0,1:T(8,128)(2,1)S(1)}, u32[]{:S(2)}, u32[]{:S(2)}) %collective-permute-start) | collective-permute-done | bytes 147488 | tf_op jit(solution)/shard_map/while/body/eval_jaxpr/ppermute | solution.py:42
  379.2 11.1 %conditional.6 = ((f32[16,128]{1,0:T(8,128)}, f32[16,128]{1,0:T(8,128)}, f32[128,16,128]{0,2,1:T(8,128)})) conditional(s32[]{:T(128)} %convert_element_type.183, (f32[16,128]{1,0:T(8,128)}, f32[16,128]{1,0:T(8,128)}, f32[128,16,128]{0,2,1:T(8,128)}) %tuple.130, (s32[]{:T(128)}, s32[]{:T(128)}, s32[8]{0:T(128)}, s32[128]{0:T(128)}, ...), branch_computations={%region_17.17_spmd, %region_18.21_spmd} | conditional | flops 708371712 | bytes 26533744 | solution.py:247
  404.7 11.1 %conditional.6 = ((f32[16,128]{1,0:T(8,128)}, f32[16,128]{1,0:T(8,128)}, f32[128,16,128]{0,2,1:T(8,128)})) conditional(s32[]{:T(128)} %convert_element_type.183, (f32[16,128]{1,0:T(8,128)}, f32[16,128]{1,0:T(8,128)}, f32[128,16,128]{0,2,1:T(8,128)}) %tuple.130, (s32[]{:T(128)}, s32[]{:T(128)}, s32[8]{0:T(128)}, s32[128]{0:T(128)}, ...), branch_computations={%region_17.17_spmd, %region_18.21_spmd} | conditional | flops 708371712 | bytes 26533744 | solution.py:247
  427.0 11.1 %conditional.6 = ((f32[16,128]{1,0:T(8,128)}, f32[16,128]{1,0:T(8,128)}, f32[128,16,128]{0,2,1:T(8,128)})) conditional(s32[]{:T(128)} %convert_element_type.183, (f32[16,128]{1,0:T(8,128)}, f32[16,128]{1,0:T(8,128)}, f32[128,16,128]{0,2,1:T(8,128)}) %tuple.130, (s32[]{:T(128)}, s32[]{:T(128)}, s32[8]{0:T(128)}, s32[128]{0:T(128)}, ...), branch_computations={%region_17.17_spmd, %region_18.21_spmd} | conditional | flops 708371712 | bytes 26533744 | solution.py:247
  449.3 11.1 %conditional.6 = ((f32[16,128]{1,0:T(8,128)}, f32[16,128]{1,0:T(8,128)}, f32[128,16,128]{0,2,1:T(8,128)})) conditional(s32[]{:T(128)} %convert_element_type.183, (f32[16,128]{1,0:T(8,128)}, f32[16,128]{1,0:T(8,128)}, f32[128,16,128]{0,2,1:T(8,128)}) %tuple.130, (s32[]{:T(128)}, s32[]{:T(128)}, s32[8]{0:T(128)}, s32[128]{0:T(128)}, ...), branch_computations={%region_17.17_spmd, %region_18.21_spmd} | conditional | flops 708371712 | bytes 26533744 | solution.py:247
  471.6 11.1 %conditional.6 = ((f32[16,128]{1,0:T(8,128)}, f32[16,128]{1,0:T(8,128)}, f32[128,16,128]{0,2,1:T(8,128)})) conditional(s32[]{:T(128)} %convert_element_type.183, (f32[16,128]{1,0:T(8,128)}, f32[16,128]{1,0:T(8,128)}, f32[128,16,128]{0,2,1:T(8,128)}) %tuple.130, (s32[]{:T(128)}, s32[]{:T(128)}, s32[8]{0:T(128)}, s32[128]{0:T(128)}, ...), branch_computations={%region_17.17_spmd, %region_18.21_spmd} | conditional | flops 708371712 | bytes 26533744 | solution.py:247
  493.9 11.1 %conditional.6 = ((f32[16,128]{1,0:T(8,128)}, f32[16,128]{1,0:T(8,128)}, f32[128,16,128]{0,2,1:T(8,128)})) conditional(s32[]{:T(128)} %convert_element_type.183, (f32[16,128]{1,0:T(8,128)}, f32[16,128]{1,0:T(8,128)}, f32[128,16,128]{0,2,1:T(8,128)}) %tuple.130, (s32[]{:T(128)}, s32[]{:T(128)}, s32[8]{0:T(128)}, s32[128]{0:T(128)}, ...), branch_computations={%region_17.17_spmd, %region_18.21_spmd} | conditional | flops 708371712 | bytes 26533744 | solution.py:247
  508.1 32.3 %while.54 = (s32[]{:T(128)}, f32[16,128,128]{2,1,0:T(8,128)S(1)}, s32[]{:T(128)}, bf16[32,16,128,128]{3,2,1,0:T(8,128)(2,1)}, bf16[32,16,128,128]{3,2,1,0:T(8,128)(2,1)}, /*index=5*/s32[]{:T(128)}, s32[]{:T(128)}, s32[]{:T(128)}) while((s32[]{:T(128)}, f32[16,128,128]{2,1,0:T(8,128)S(1)}, s32[]{:T(128)}, ...), condition=%wide.region_9.10_spmd, body=%wide.region_8.9_spmd.sunk | while | flops 403177472 | bytes 5244031 | solution.py:36
  (688 shorter events, 468.2 us)
Async XLA Ops:
  7.2 500.8 %all-gather.5.cloned.1.call-start = ((), (), s32[]{:S(2)}) async-start(), calls=%async_computation | async-start | bytes 17301504 | tf_op jit(solution)/shard_map/all_gather | solution.py:20
  8.9 87.1 %copy-start.29 = (s32[128]{0:T(128)}, s32[128]{0:T(128)S(1)}, u32[]{:S(2)}) copy-start(s32[128]{0:T(128)S(1)} %iota_add_fusion.2) | copy-start | bytes 1540
  17.7 39.3 %copy-start.3 = (f32[16,8,16,128]{3,2,1,0:T(8,128)}, f32[16,8,16,128]{3,2,1,0:T(8,128)S(1)}, u32[]{:S(2)}) copy-start(f32[16,8,16,128]{3,2,1,0:T(8,128)S(1)} %copy.150) | copy-start | bytes 3145732
  95.1 412.9 %all-gather.7.cloned.1.call-start = ((), (), s32[]{:S(2)}) async-start(), calls=%async_computation.1 | async-start | bytes 17301504 | tf_op jit(solution)/shard_map/all_gather | solution.py:20
  96.7 7.9 %copy-start = (bf16[512,2048]{1,0:T(8,128)(2,1)S(1)}, bf16[512,2048]{1,0:T(8,128)(2,1)}, u32[]{:S(2)}) copy-start(bf16[512,2048]{1,0:T(8,128)(2,1)} %param.27) | copy-start | bytes 6291460
  107.4 4.4 copy-start.1
  107.4 4.4 copy-start.18
  117.5 14.3 %collective-permute-start = (bf16[128,576]{0,1:T(8,128)(2,1)}, bf16[128,576]{0,1:T(8,128)(2,1)S(1)}, u32[]{:S(2)}, u32[]{:S(2)}) collective-permute-start(bf16[128,576]{0,1:T(8,128)(2,1)} %get-tuple-element.1228), channel_id=1, source_target_pairs={{0,8},{8,16},{16,24},{24,32},{32,40},{40,48},{48,56},{56,64},{64,7... | collective-permute-start | bytes 442376 | tf_op jit(solution)/shard_map/while/body/eval_jaxpr/ppermute | solution.py:42
  143.5 10.6 %collective-permute-start = (bf16[128,576]{0,1:T(8,128)(2,1)}, bf16[128,576]{0,1:T(8,128)(2,1)S(1)}, u32[]{:S(2)}, u32[]{:S(2)}) collective-permute-start(bf16[128,576]{0,1:T(8,128)(2,1)} %get-tuple-element.1228), channel_id=1, source_target_pairs={{0,8},{8,16},{16,24},{24,32},{32,40},{40,48},{48,56},{56,64},{64,7... | collective-permute-start | bytes 442376 | tf_op jit(solution)/shard_map/while/body/eval_jaxpr/ppermute | solution.py:42
  165.9 13.8 %collective-permute-start = (bf16[128,576]{0,1:T(8,128)(2,1)}, bf16[128,576]{0,1:T(8,128)(2,1)S(1)}, u32[]{:S(2)}, u32[]{:S(2)}) collective-permute-start(bf16[128,576]{0,1:T(8,128)(2,1)} %get-tuple-element.1228), channel_id=1, source_target_pairs={{0,8},{8,16},{16,24},{24,32},{32,40},{40,48},{48,56},{56,64},{64,7... | collective-permute-start | bytes 442376 | tf_op jit(solution)/shard_map/while/body/eval_jaxpr/ppermute | solution.py:42
  191.4 14.1 %collective-permute-start = (bf16[128,576]{0,1:T(8,128)(2,1)}, bf16[128,576]{0,1:T(8,128)(2,1)S(1)}, u32[]{:S(2)}, u32[]{:S(2)}) collective-permute-start(bf16[128,576]{0,1:T(8,128)(2,1)} %get-tuple-element.1228), channel_id=1, source_target_pairs={{0,8},{8,16},{16,24},{24,32},{32,40},{40,48},{48,56},{56,64},{64,7... | collective-permute-start | bytes 442376 | tf_op jit(solution)/shard_map/while/body/eval_jaxpr/ppermute | solution.py:42
  217.3 13.8 %collective-permute-start = (bf16[128,576]{0,1:T(8,128)(2,1)}, bf16[128,576]{0,1:T(8,128)(2,1)S(1)}, u32[]{:S(2)}, u32[]{:S(2)}) collective-permute-start(bf16[128,576]{0,1:T(8,128)(2,1)} %get-tuple-element.1228), channel_id=1, source_target_pairs={{0,8},{8,16},{16,24},{24,32},{32,40},{40,48},{48,56},{56,64},{64,7... | collective-permute-start | bytes 442376 | tf_op jit(solution)/shard_map/while/body/eval_jaxpr/ppermute | solution.py:42
  242.8 10.6 %collective-permute-start = (bf16[128,576]{0,1:T(8,128)(2,1)}, bf16[128,576]{0,1:T(8,128)(2,1)S(1)}, u32[]{:S(2)}, u32[]{:S(2)}) collective-permute-start(bf16[128,576]{0,1:T(8,128)(2,1)} %get-tuple-element.1228), channel_id=1, source_target_pairs={{0,8},{8,16},{16,24},{24,32},{32,40},{40,48},{48,56},{56,64},{64,7... | collective-permute-start | bytes 442376 | tf_op jit(solution)/shard_map/while/body/eval_jaxpr/ppermute | solution.py:42
  265.1 13.5 %collective-permute-start = (bf16[128,576]{0,1:T(8,128)(2,1)}, bf16[128,576]{0,1:T(8,128)(2,1)S(1)}, u32[]{:S(2)}, u32[]{:S(2)}) collective-permute-start(bf16[128,576]{0,1:T(8,128)(2,1)} %get-tuple-element.1228), channel_id=1, source_target_pairs={{0,8},{8,16},{16,24},{24,32},{32,40},{40,48},{48,56},{56,64},{64,7... | collective-permute-start | bytes 442376 | tf_op jit(solution)/shard_map/while/body/eval_jaxpr/ppermute | solution.py:42
  290.4 11.4 %collective-permute-start = (bf16[128,576]{0,1:T(8,128)(2,1)}, bf16[128,576]{0,1:T(8,128)(2,1)S(1)}, u32[]{:S(2)}, u32[]{:S(2)}) collective-permute-start(bf16[128,576]{0,1:T(8,128)(2,1)} %get-tuple-element.1228), channel_id=1, source_target_pairs={{0,8},{8,16},{16,24},{24,32},{32,40},{40,48},{48,56},{56,64},{64,7... | collective-permute-start | bytes 442376 | tf_op jit(solution)/shard_map/while/body/eval_jaxpr/ppermute | solution.py:42
  313.6 13.7 %collective-permute-start = (bf16[128,576]{0,1:T(8,128)(2,1)}, bf16[128,576]{0,1:T(8,128)(2,1)S(1)}, u32[]{:S(2)}, u32[]{:S(2)}) collective-permute-start(bf16[128,576]{0,1:T(8,128)(2,1)} %get-tuple-element.1228), channel_id=1, source_target_pairs={{0,8},{8,16},{16,24},{24,32},{32,40},{40,48},{48,56},{56,64},{64,7... | collective-permute-start | bytes 442376 | tf_op jit(solution)/shard_map/while/body/eval_jaxpr/ppermute | solution.py:42
  339.0 13.7 %collective-permute-start = (bf16[128,576]{0,1:T(8,128)(2,1)}, bf16[128,576]{0,1:T(8,128)(2,1)S(1)}, u32[]{:S(2)}, u32[]{:S(2)}) collective-permute-start(bf16[128,576]{0,1:T(8,128)(2,1)} %get-tuple-element.1228), channel_id=1, source_target_pairs={{0,8},{8,16},{16,24},{24,32},{32,40},{40,48},{48,56},{56,64},{64,7... | collective-permute-start | bytes 442376 | tf_op jit(solution)/shard_map/while/body/eval_jaxpr/ppermute | solution.py:42
  364.5 14.8 %collective-permute-start = (bf16[128,576]{0,1:T(8,128)(2,1)}, bf16[128,576]{0,1:T(8,128)(2,1)S(1)}, u32[]{:S(2)}, u32[]{:S(2)}) collective-permute-start(bf16[128,576]{0,1:T(8,128)(2,1)} %get-tuple-element.1228), channel_id=1, source_target_pairs={{0,8},{8,16},{16,24},{24,32},{32,40},{40,48},{48,56},{56,64},{64,7... | collective-permute-start | bytes 442376 | tf_op jit(solution)/shard_map/while/body/eval_jaxpr/ppermute | solution.py:42
  391.0 13.7 %collective-permute-start = (bf16[128,576]{0,1:T(8,128)(2,1)}, bf16[128,576]{0,1:T(8,128)(2,1)S(1)}, u32[]{:S(2)}, u32[]{:S(2)}) collective-permute-start(bf16[128,576]{0,1:T(8,128)(2,1)} %get-tuple-element.1228), channel_id=1, source_target_pairs={{0,8},{8,16},{16,24},{24,32},{32,40},{40,48},{48,56},{56,64},{64,7... | collective-permute-start | bytes 442376 | tf_op jit(solution)/shard_map/while/body/eval_jaxpr/ppermute | solution.py:42
  416.4 10.6 %collective-permute-start = (bf16[128,576]{0,1:T(8,128)(2,1)}, bf16[128,576]{0,1:T(8,128)(2,1)S(1)}, u32[]{:S(2)}, u32[]{:S(2)}) collective-permute-start(bf16[128,576]{0,1:T(8,128)(2,1)} %get-tuple-element.1228), channel_id=1, source_target_pairs={{0,8},{8,16},{16,24},{24,32},{32,40},{40,48},{48,56},{56,64},{64,7... | collective-permute-start | bytes 442376 | tf_op jit(solution)/shard_map/while/body/eval_jaxpr/ppermute | solution.py:42
  438.7 10.6 %collective-permute-start = (bf16[128,576]{0,1:T(8,128)(2,1)}, bf16[128,576]{0,1:T(8,128)(2,1)S(1)}, u32[]{:S(2)}, u32[]{:S(2)}) collective-permute-start(bf16[128,576]{0,1:T(8,128)(2,1)} %get-tuple-element.1228), channel_id=1, source_target_pairs={{0,8},{8,16},{16,24},{24,32},{32,40},{40,48},{48,56},{56,64},{64,7... | collective-permute-start | bytes 442376 | tf_op jit(solution)/shard_map/while/body/eval_jaxpr/ppermute | solution.py:42
  461.0 10.6 %collective-permute-start = (bf16[128,576]{0,1:T(8,128)(2,1)}, bf16[128,576]{0,1:T(8,128)(2,1)S(1)}, u32[]{:S(2)}, u32[]{:S(2)}) collective-permute-start(bf16[128,576]{0,1:T(8,128)(2,1)} %get-tuple-element.1228), channel_id=1, source_target_pairs={{0,8},{8,16},{16,24},{24,32},{32,40},{40,48},{48,56},{56,64},{64,7... | collective-permute-start | bytes 442376 | tf_op jit(solution)/shard_map/while/body/eval_jaxpr/ppermute | solution.py:42
  483.3 10.6 %collective-permute-start = (bf16[128,576]{0,1:T(8,128)(2,1)}, bf16[128,576]{0,1:T(8,128)(2,1)S(1)}, u32[]{:S(2)}, u32[]{:S(2)}) collective-permute-start(bf16[128,576]{0,1:T(8,128)(2,1)} %get-tuple-element.1228), channel_id=1, source_target_pairs={{0,8},{8,16},{16,24},{24,32},{32,40},{40,48},{48,56},{56,64},{64,7... | collective-permute-start | bytes 442376 | tf_op jit(solution)/shard_map/while/body/eval_jaxpr/ppermute | solution.py:42
  508.1 32.3 %copy-start.21 = (f32[2,16,64,128]{3,2,0,1:T(8,128)S(1)}, f32[2,16,64,128]{3,2,0,1:T(8,128)}, u32[]{:S(2)}) copy-start(f32[2,16,64,128]{3,2,0,1:T(8,128)} %get-tuple-element.660) | copy-start | bytes 3145732
  (124 other events, 235.4 us)
Sparse Core Ops, SparseCore 0:
  95.2 153.5 all-gather.4
  251.4 158.4 all-gather.6
where the time goes:
time: 559 us; the launch traced here: 551 us
  matrix products  182 us (33%)
  waiting for transfers between devices  147 us (26%)
  local copies, waits for them, and re-layouts  81.8 us (15%)
  other arithmetic  68.7 us (12%)
  starting transfers between devices  32.1 us (6%)
  loops' own time  23.5 us (4%)
  between operations  16 us (3%)
    ppermute x16, waiting for transfers between devices, shifted(): return lax.ppermute(block, axis, route)  147 us
    dot_general x17, matrix products, attend_rows(): jnp.einsum('hts,shv->thv', weights.astype(jnp.bfloat16), values, preferre...  44.9 us
    reshape x17, local copies, waits for them, and re-layouts, attend_rows(): values = jnp.dot(latent_part, value_up, preferred_element_type=jnp.float3...  34.6 us
    ppermute x16, starting transfers between devices, shifted(): return lax.ppermute(block, axis, route)  32 us
    dot_general x16, matrix products, compose(): jnp.einsum('ytn,yne->yte', successor_slab[0], prior_slab[1], precision=PR...  30.2 us
    transpose x16, other arithmetic, attend_rows(): accumulated = accumulated * jnp.transpose(factor)[:, :, None] + product  23 us
    add x17, other arithmetic, attend_rows(): running_sum = running_sum * factor + jnp.sum(weights, axis=2)  22.5 us
    dot_general x17, matrix products, attend_rows(): jnp.dot(latent_part, value_up, preferred_element_type=jnp.float32)  21.5 us
  transfers between devices with their start and end apart: 18, of which 16 were waited for; matrix products, arithmetic and copies ran while one was open for 38% of the time, Pallas kernels for 0%

commit v1 on v0

--- a/solution.py
+++ b/solution.py
@@ -184,95 +184,101 @@
 
     slab_pair, per_block = lax.scan(advance_block, (identity_map, zero_add), block_outs)
     effective_everything, output_everything = per_block
-    leading_part = prefix(slab_pair, "ctx", compose, (identity_map, zero_add))
+    carried_in = incoming_state(slab_pair, slab_rows)
     delta_attention_complete = output_everything + jnp.einsum(
-        "enzx,nxu->enzu", effective_everything, leading_part[1], precision=PRECISE_PRODUCT
+        "enzx,nxu->enzu", effective_everything, carried_in, precision=PRECISE_PRODUCT
     )
     kda_out = (
         jnp.transpose(delta_attention_complete, (0, 2, 1, 3))
         .reshape(slab_rows, -1)
         .astype(jnp.bfloat16)
     )
+    mla_out = latent_attention(
+        mla_query, latents, key_up, value_up, positions, docids, doc_starts, head_count
+    )
+    return (kda_out, mla_out)
+
+
+def window_slabs_of(slab_rows):
+    longest = lax.axis_size("ctx") * slab_rows // 2
+    return -(-longest // slab_rows)
+
+
+def incoming_state(slab_pair, slab_rows):
+    map_now, add_now = slab_pair
+    window = window_slabs_of(slab_rows)
+
+    def received(value, distance):
+        return shifted(value.astype(jnp.bfloat16), "ctx", distance).astype(jnp.float32)
+
+    def product(left, right):
+        return jnp.einsum("hkj,hjl->hkl", left, right, precision=PRECISE_PRODUCT)
+
+    distance = 1
+    while 2 * distance < window:
+        map_before = received(map_now, distance)
+        add_before = received(add_now, distance)
+        add_now = product(map_now, add_before) + add_now
+        map_now = product(map_now, map_before)
+        distance *= 2
+    map_last = received(map_now, 1)
+    add_last = received(add_now, 1)
+    add_far = received(add_now, distance + 1)
+    return product(map_last, add_far) + add_last
+
+
+def latent_attention(
+    mla_query, latents, key_up, value_up, positions, docids, doc_starts, head_count
+):
+    slab_rows = latents.shape[0]
+    slabs = lax.axis_size("ctx")
+    reach = window_slabs_of(slab_rows)
+    window_slabs = min(reach + 1, slabs)
+    window_rows = window_slabs * slab_rows
+    everything = lax.all_gather(latents, "ctx", tiled=True)
+    first_slab = jnp.clip(lax.axis_index("ctx") - reach, 0, slabs - window_slabs)
+    key_first = first_slab * slab_rows
+    key_rows = lax.dynamic_slice_in_dim(everything, key_first, window_rows, 0)
+    latent_part = key_rows[:, :LATENT]
+    keys_nope = (
+        jnp.dot(latent_part, key_up, preferred_element_type=jnp.float32)
+        .astype(jnp.bfloat16)
+        .reshape(window_rows, head_count, NOPE)
+    )
+    values = (
+        jnp.dot(latent_part, value_up, preferred_element_type=jnp.float32)
+        .astype(jnp.bfloat16)
+        .reshape(window_rows, head_count, -1)
+    )
     queries = mla_query.reshape(slab_rows, head_count, NOPE + ROPE)
-    query_nope = queries[:, :, :NOPE]
-    query_rope = queries[:, :, NOPE:]
     score_scale = 1.0 / math.sqrt(NOPE + ROPE)
-    last_place = positions[slab_rows - 1]
-    first_doc_start = jnp.sum(
-        jnp.where(jnp.arange(doc_starts.shape[0]) == docids[0], doc_starts, 0)
-    )
-
-    def attend_rows(softmax_state, key_rows, key_first):
-        running_max, running_sum, accumulated = softmax_state
-        row_count = key_rows.shape[0]
-        latent_part = key_rows[:, :LATENT]
-        keys_nope = (
-            jnp.dot(latent_part, key_up, preferred_element_type=jnp.float32)
-            .astype(jnp.bfloat16)
-            .reshape(row_count, head_count, NOPE)
-        )
-        values = (
-            jnp.dot(latent_part, value_up, preferred_element_type=jnp.float32)
-            .astype(jnp.bfloat16)
-            .reshape(row_count, head_count, -1)
-        )
-        scores = jnp.einsum(
-            "thd,shd->hts", query_nope, keys_nope, preferred_element_type=jnp.float32
-        )
-        scores = (
-            scores
-            + jnp.einsum(
-                "thr,sr->hts", query_rope, key_rows[:, LATENT:], preferred_element_type=jnp.float32
-            )
-        ) * score_scale
-        key_places = key_first + jnp.arange(row_count, dtype=jnp.int32)
-        key_docs = doc_of(key_places, doc_starts)
-        allowed = (key_places[None, :] <= positions[:, None]) & (
-            key_docs[None, :] == docids[:, None]
-        )
-        masked = jnp.where(allowed[None], scores, -1e30)
-        new_max = jnp.maximum(running_max, jnp.max(masked, axis=2))
-        weights = jnp.where(allowed[None], jnp.exp(masked - new_max[:, :, None]), 0.0)
-        factor = jnp.exp(running_max - new_max)
-        running_sum = running_sum * factor + jnp.sum(weights, axis=2)
-        product = jnp.einsum(
-            "hts,shv->thv", weights.astype(jnp.bfloat16), values, preferred_element_type=jnp.float32
-        )
-        accumulated = accumulated * jnp.transpose(factor)[:, :, None] + product
-        return (new_max, running_sum, accumulated)
-
-    def guarded(softmax_state, key_rows, key_first):
-        row_count = key_rows.shape[0]
-        needed = (key_first <= last_place) & (key_first + row_count - 1 >= first_doc_start)
-        return lax.cond(
-            needed, lambda: attend_rows(softmax_state, key_rows, key_first), lambda: softmax_state
-        )
-
-    value_width = value_up.shape[1] // head_count
-    initial_state = (
-        jnp.full((head_count, slab_rows), -1e30, jnp.float32),
-        jnp.zeros((head_count, slab_rows), jnp.float32),
-        jnp.zeros((slab_rows, head_count, value_width), jnp.float32),
-    )
-    own_state = guarded(initial_state, latents, first_row)
-
-    def advance_window(step_index, window_pair):
-        carried_state, moving = window_pair
-        moving = shifted(moving, "ctx", 1)
-        carried_state = guarded(carried_state, moving, first_row - (step_index + 1) * slab_rows)
-        return (carried_state, moving)
-
-    softmax_state, _ = lax.fori_loop(
-        0, lax.axis_size("ctx") // 2, advance_window, (own_state, latents)
-    )
-    running_sum = softmax_state[1]
-    accumulated = softmax_state[2]
-    mla_out = (
-        (accumulated / jnp.transpose(running_sum)[:, :, None])
-        .astype(jnp.bfloat16)
-        .reshape(slab_rows, -1)
-    )
-    return (kda_out, mla_out)
+    scores = jnp.einsum(
+        "thd,shd->hts", queries[:, :, :NOPE], keys_nope, preferred_element_type=jnp.float32
+    )
+    scores = (
+        scores
+        + jnp.einsum(
+            "thr,sr->hts",
+            queries[:, :, NOPE:],
+            key_rows[:, LATENT:],
+            preferred_element_type=jnp.float32,
+        )
+    ) * score_scale
+    key_places = key_first + jnp.arange(window_rows, dtype=jnp.int32)
+    key_docs = doc_of(key_places, doc_starts)
+    allowed = (key_places[None, :] <= positions[:, None]) & (
+        key_docs[None, :] == docids[:, None]
+    )
+    masked = jnp.where(allowed[None], scores, -1e30)
+    row_max = jnp.max(masked, axis=2, keepdims=True)
+    weights = jnp.where(allowed[None], jnp.exp(masked - row_max), 0.0)
+    row_total = jnp.sum(weights, axis=2)
+    summed = jnp.einsum(
+        "hts,shv->thv", weights.astype(jnp.bfloat16), values, preferred_element_type=jnp.float32
+    )
+    return (
+        (summed / jnp.transpose(row_total)[:, :, None]).astype(jnp.bfloat16).reshape(slab_rows, -1)
+    )
 
 
 def solution(mesh):

time: 559 us -> 295 us (0.53)
  the two profiles are of different devices: /device:TPU:144 before, /device:TPU:120 now
where the time goes in v1:
time: 295 us; the launch traced here: 290 us
  matrix products  116 us (39%)
  waiting for transfers between devices  71.8 us (24%)
  starting transfers between devices  51 us (17%)
  local copies, waits for them, and re-layouts  20.9 us (7%)
  other arithmetic  15.1 us (5%)
  between operations  14.8 us (5%)
    ppermute x9, waiting for transfers between devices, shifted(): return lax.ppermute(block, axis, route)  71.1 us
    ppermute x9, starting transfers between devices, shifted(): return lax.ppermute(block, axis, route)  51 us
    unnamed x33, local copies, waits for them, and re-layouts  14.3 us
    sub x1, matrix products, latent_attention(): weights = jnp.where(allowed[None], jnp.exp(masked - row_max), 0.0)  14.2 us
    dot_general x1, matrix products, latent_attention(): jnp.einsum('thd,shd->hts', queries[:, :, :NOPE], keys_nope, preferred_ele...  12.4 us
    dot_general x1, matrix products, latent_attention(): jnp.dot(latent_part, key_up, preferred_element_type=jnp.float32)  9.13 us
    dot_general x1, matrix products, latent_attention(): jnp.dot(latent_part, value_up, preferred_element_type=jnp.float32)  9.05 us
    dot_general x1, matrix products, latent_attention(): jnp.einsum('hts,shv->thv', weights.astype(jnp.bfloat16), values, preferre...  8.69 us
  transfers between devices with their start and end apart: 10, of which 5 were waited for; matrix products, arithmetic and copies ran while one was open for 34% of the time, Pallas kernels for 0%

profile of v1, /device:TPU:120, one launch (start us, length us, event | category | flops | bytes accessed | tf_op | source)
XLA Modules:
  0.0 290.2 jit_solution(5549372973234512374)
XLA Ops:
  31.9 3.1 %fusion.36 = f32[2,16,64,64]{3,2,1,0:T(8,128)S(1)} fusion(f32[2,16,64]{2,1,0:T(8,128)S(1)} %get-tuple-element.115, pred[2,64,64]{2,1,0:T(8,128)(4,1)S(1)} %get-tuple-element.118, f32[2,64,16,128]{3,2,1,0:T(8,128)S(1)} %bitcast.185, f32[2,64,16]{1,2,0:T(8,128)S(1)} %copy.88, f32[2,64,16,128]{3,2,1,0:T(8,128)S(1)} %fusion.42), kind=kOutput, calls=%fused_computation.51 | convolution fusion | flops 202899456 | bytes 2646016 | tf_op jit(solution)/shard_map/vmap(thk,shk->hts)/dot_general | solution.py:79
  55.8 3.0 %convolution_subtract_fusion = f32[2,16,64,128]{3,2,1,0:T(8,128)} fusion(f32[2,16,64,64]{3,2,1,0:T(8,128)S(1)} %convolution_select_fusion, f32[2,16,64,128]{3,2,1,0:T(8,128)S(1)} %fusion.46, f32[2,64]{1,0:T(2,128)S(1)} %get-tuple-element.120, f32[2,64,16]{1,2,0:T(8,128)S(1)} %copy.97, f32[2,64,16,128]{3,2,1,0:T(8,128)S(1)} %bitcast.191, ...), kind=kOutput, calls=%fused_computation.47 | convolution fusion | flops 202375168 | bytes 4727296 | tf_op jit(solution)/shard_map/vmap(hts,hsk->htk)/dot_general | solution.py:94
  58.8 5.6 %fusion.74 = f32[2,16,128,128]{3,2,1,0:T(8,128)} fusion(f32[2,16,64,128]{3,2,1,0:T(8,128)S(1)} %fusion.44, f32[2,64,16,128]{3,2,1,0:T(8,128)S(1)} %fusion.42, f32[2,64,16,128]{3,2,1,0:T(8,128)S(1)} %bitcast.188, f32[2,64]{1,0:T(2,128)S(1)} %get-tuple-element.119, f32[2,16,128]{2,1,0:T(8,128)S(1)} %slice_bitcast_fusion, f32[2,64,16]{1,2,0:T(8,128)S(1)} %copy.88), kind=kOutput, calls=%fused_computation.103 | convolution fusion | flops 403701760 | bytes 5267968 | tf_op jit(solution)/shard_map/vmap(omt,mor->mtr)/dot_general | solution.py:106
  64.4 6.2 %multiply_subtract_fusion = f32[2,16,128,128]{3,2,1,0:T(8,128)} fusion(f32[2,16,64,128]{3,2,1,0:T(8,128)S(1)} %fusion.46, f32[128,128]{1,0:T(8,128)S(1)} %fusion.75, f32[2,16,128]{2,1,0:T(8,128)S(1)} %bitcast.202, f32[2]{0:T(128)S(1)} %slice_reduce_fusion.1, f32[2,64,16,128]{3,2,1,0:T(8,128)S(1)} %fusion.42, f32[2,64,16,128]{3,2,1,0:T(8,128)S(1)} %bitcast.189, ...), kind=kOutput, calls=%fused_computation.36 | convolution fusion | flops 405274624 | bytes 5349896 | tf_op jit(solution)/shard_map/vmap(shk,hsj->hkj)/dot_general | solution.py:103
  70.7 19.7 %while.17 = (s32[]{:T(128)}, f32[16,128,128]{2,1,0:T(8,128)S(1)}, f32[16,128,128]{2,1,0:T(8,128)}, f32[2,16,64,128]{3,2,0,1:T(8,128)}, f32[2,16,64,128]{3,2,0,1:...) while((s32[]{:T(128)}, f32[16,128,128]{2,1,0:T(8,128)S(1)}, ...), condition=%wide.region_7.8_spmd.clone, body=%wide.region_6.7_spmd.clone.sunk | while | flops 1208877056 | bytes 49811752 | solution.py:185
  72.2 3.9 %fusion.160 = f32[2,16,64,128]{3,2,0,1:T(8,128)} fusion(f32[2,16,64,128]{3,2,0,1:T(8,128)} %get-tuple-element.204, s32[]{:T(128)S(6)} %copy.181, f32[16,128,128]{2,1,0:T(8,128)S(1)} %copy.193, f32[2,16,64,128]{3,2,1,0:T(8,128)} %get-tuple-element.219), kind=kOutput, calls=%fused_computation.5.clone.1 | convolution fusion | flops 201326592 | bytes 2098176 | tf_op jit(solution)/shard_map/while/body/eval_jaxpr/htk,hkj->htj/dot_general | solution.py:170
  82.1 3.8 %fusion.160 = f32[2,16,64,128]{3,2,0,1:T(8,128)} fusion(f32[2,16,64,128]{3,2,0,1:T(8,128)} %get-tuple-element.204, s32[]{:T(128)S(6)} %copy.181, f32[16,128,128]{2,1,0:T(8,128)S(1)} %copy.193, f32[2,16,64,128]{3,2,1,0:T(8,128)} %get-tuple-element.219), kind=kOutput, calls=%fused_computation.5.clone.1 | convolution fusion | flops 201326592 | bytes 2098176 | tf_op jit(solution)/shard_map/while/body/eval_jaxpr/htk,hkj->htj/dot_general | solution.py:170
  92.5 3.3 %collective-permute-start.4 = (bf16[16,128,128]{2,1,0:T(8,128)(2,1)}, bf16[16,128,128]{2,1,0:T(8,128)(2,1)}, u32[]{:S(2)}, u32[]{:S(2)}) collective-permute-start(bf16[16,128,128]{2,1,0:T(8,128)(2,1)} %convert_element_type.135), channel_id=1, source_target_pairs={{0,8},{8,16},{16,24},{24,32},{32,40},{40,48},{48,56},{56,64},{64,7... | collective-permute-start | bytes 1572872 | tf_op jit(solution)/shard_map/ppermute | solution.py:42
  96.7 3.3 %collective-permute-start = (bf16[16,128,128]{2,1,0:T(8,128)(2,1)}, bf16[16,128,128]{2,1,0:T(8,128)(2,1)}, u32[]{:S(2)}, u32[]{:S(2)}) collective-permute-start(bf16[16,128,128]{2,1,0:T(8,128)(2,1)} %convert_element_type.131), channel_id=1, source_target_pairs={{0,8},{8,16},{16,24},{24,32},{32,40},{40,48},{48,56},{56,64},{64,7... | collective-permute-start | bytes 1572872 | tf_op jit(solution)/shard_map/ppermute | solution.py:42
  102.4 9.3 %collective-permute-done.4 = bf16[16,128,128]{2,1,0:T(8,128)(2,1)} collective-permute-done((bf16[16,128,128]{2,1,0:T(8,128)(2,1)}, bf16[16,128,128]{2,1,0:T(8,128)(2,1)}, u32[]{:S(2)}, u32[]{:S(2)}) %collective-permute-start.4) | collective-permute-done | bytes 524320 | tf_op jit(solution)/shard_map/ppermute | solution.py:42
  116.4 8.9 %collective-permute-done = bf16[16,128,128]{2,1,0:T(8,128)(2,1)} collective-permute-done((bf16[16,128,128]{2,1,0:T(8,128)(2,1)}, bf16[16,128,128]{2,1,0:T(8,128)(2,1)}, u32[]{:S(2)}, u32[]{:S(2)}) %collective-permute-start) | collective-permute-done | bytes 524320 | tf_op jit(solution)/shard_map/ppermute | solution.py:42
  129.1 5.2 %collective-permute-done.5 = bf16[16,128,128]{2,1,0:T(8,128)(2,1)S(1)} collective-permute-done((bf16[16,128,128]{2,1,0:T(8,128)(2,1)S(1)}, bf16[16,128,128]{2,1,0:T(8,128)(2,1)S(1)}, u32[]{:S(2)}, u32[]{:S(2)}) %collective-permute-start.5) | collective-permute-done | bytes 524320 | tf_op jit(solution)/shard_map/ppermute | solution.py:42
  135.0 6.5 %collective-permute-start.6 = (bf16[16,128,128]{2,1,0:T(8,128)(2,1)S(1)}, bf16[16,128,128]{2,1,0:T(8,128)(2,1)S(1)}, u32[]{:S(2)}, u32[]{:S(2)}) collective-permute-start(bf16[16,128,128]{2,1,0:T(8,128)(2,1)S(1)} %get-tuple-element.127), channel_id=1, source_target_pairs={{0,32},{8,40},{16,48},{24,56},{32,64},{40,72},{48,80},{56,88},{64,... | collective-permute-start | bytes 1572872 | tf_op jit(solution)/shard_map/ppermute | solution.py:42
  141.5 4.7 %collective-permute-done.1 = bf16[16,128,128]{2,1,0:T(8,128)(2,1)S(1)} collective-permute-done((bf16[16,128,128]{2,1,0:T(8,128)(2,1)S(1)}, bf16[16,128,128]{2,1,0:T(8,128)(2,1)S(1)}, u32[]{:S(2)}, u32[]{:S(2)}) %collective-permute-start.1) | collective-permute-done | bytes 524320 | tf_op jit(solution)/shard_map/ppermute | solution.py:42
  146.9 6.4 %collective-permute-start.2 = (bf16[16,128,128]{2,1,0:T(8,128)(2,1)S(1)}, bf16[16,128,128]{2,1,0:T(8,128)(2,1)S(1)}, u32[]{:S(2)}, u32[]{:S(2)}) collective-permute-start(bf16[16,128,128]{2,1,0:T(8,128)(2,1)S(1)} %get-tuple-element.123), channel_id=1, source_target_pairs={{0,32},{8,40},{16,48},{24,56},{32,64},{40,72},{48,80},{56,88},{64,... | collective-permute-start | bytes 1572872 | tf_op jit(solution)/shard_map/ppermute | solution.py:42
  154.0 8.9 %collective-permute-start.8 = (bf16[16,128,128]{2,1,0:T(8,128)(2,1)S(1)}, bf16[16,128,128]{2,1,0:T(8,128)(2,1)S(1)}, u32[]{:S(2)}, u32[]{:S(2)}) collective-permute-start(bf16[16,128,128]{2,1,0:T(8,128)(2,1)S(1)} %fusion.37), channel_id=1, source_target_pairs={{0,8},{8,16},{16,24},{24,32},{32,40},{40,48},{48,56},{56,64},{64,7... | collective-permute-start | bytes 1572872 | tf_op jit(solution)/shard_map/ppermute | solution.py:42
  162.9 7.5 %collective-permute-start.7 = (bf16[16,128,128]{2,1,0:T(8,128)(2,1)S(1)}, bf16[16,128,128]{2,1,0:T(8,128)(2,1)S(1)}, u32[]{:S(2)}, u32[]{:S(2)}) collective-permute-start(bf16[16,128,128]{2,1,0:T(8,128)(2,1)S(1)} %fusion.37), channel_id=1, source_target_pairs={{0,72},{8,80},{16,88},{24,96},{32,104},{40,112},{48,120},{56,128},... | collective-permute-start | bytes 1572872 | tf_op jit(solution)/shard_map/ppermute | solution.py:42
  171.0 10.5 %collective-permute-start.3 = (bf16[16,128,128]{2,1,0:T(8,128)(2,1)S(1)}, bf16[16,128,128]{2,1,0:T(8,128)(2,1)S(1)}, u32[]{:S(2)}, u32[]{:S(2)}) collective-permute-start(bf16[16,128,128]{2,1,0:T(8,128)(2,1)S(1)} %convolution_convert_fusion.2), channel_id=1, source_target_pairs={{0,8},{8,16},{16,24},{24,32},{32,40},{40,48},{48,56},{56,64},{64,7... | collective-permute-start | bytes 1572872 | tf_op jit(solution)/shard_map/ppermute | solution.py:42
  182.9 43.0 %collective-permute-done.3 = bf16[16,128,128]{2,1,0:T(8,128)(2,1)S(1)} collective-permute-done((bf16[16,128,128]{2,1,0:T(8,128)(2,1)S(1)}, bf16[16,128,128]{2,1,0:T(8,128)(2,1)S(1)}, u32[]{:S(2)}, u32[]{:S(2)}) %collective-permute-start.3) | collective-permute-done | bytes 524320 | tf_op jit(solution)/shard_map/ppermute | solution.py:42
  228.7 9.1 %convolution_convert_fusion = bf16[2176,2048]{0,1:T(8,128)(2,1)} fusion(bf16[512,2048]{1,0:T(8,128)(2,1)S(1)} %copy-done, bf16[4096,576]{0,1:T(8,128)(2,1)} %all-gather.2.cloned.1.call-done, s32[]{:T(128)S(6)} %select_n.19), kind=kOutput, calls=%fused_computation.32 | convolution fusion | flops 4567859200 | bytes 13238276 | tf_op jit(solution)/shard_map/dot_general | solution.py:244
  237.8 12.4 %fusion.62 = f32[16,2176,128]{2,1,0:T(8,128)} fusion(bf16[2176,16,128]{0,2,1:T(8,128)(2,1)} %bitcast.192, bf16[128,16,192]{0,2,1:T(8,128)(2,1)S(1)} %bitcast.197), kind=kOutput, calls=%fused_computation.91 | convolution fusion | flops 1140850688 | bytes 27262976 | tf_op jit(solution)/shard_map/thd,shd->hts/dot_general | solution.py:255
  250.2 9.0 %convolution_convert_fusion.1 = bf16[2176,2048]{0,1:T(8,128)(2,1)} fusion(bf16[512,2048]{1,0:T(8,128)(2,1)S(1)} %copy-done.16, bf16[4096,576]{0,1:T(8,128)(2,1)} %all-gather.2.cloned.1.call-done, s32[]{:T(128)S(6)} %select_n.19), kind=kOutput, calls=%fused_computation.33 | convolution fusion | flops 4567859200 | bytes 13238276 | tf_op jit(solution)/shard_map/dot_general | solution.py:249
  259.3 14.2 %fusion.85 = (f32[16,128]{1,0:T(8,128)S(1)}, bf16[16,128,2176]{1,2,0:T(8,128)(2,1)}) fusion(pred[128,2176]{0,1:T(8,128)(4,1)S(1)} %compare_and_fusion, f32[16,2176,128]{2,1,0:T(8,128)} %fusion.62, bf16[4096,576]{0,1:T(8,128)(2,1)} %all-gather.2.cloned.1.call-done, s32[]{:T(128)S(6)} %select_n.19, s32[]{:T(128)S(6)} %add.178, ...), kind=kOutput, calls=%fused_computation.137 | convolution fusion | flops 601622656 | bytes 27844616 | tf_op jit(solution)/shard_map/sub | solution.py:274
  273.4 8.7 %divide_convert_fusion = bf16[128,16,128]{0,2,1:T(8,128)(2,1)S(1)} fusion(bf16[2176,16,128]{0,2,1:T(8,128)(2,1)} %bitcast.204, bf16[16,128,2176]{1,2,0:T(8,128)(2,1)} %get-tuple-element.130, f32[128,16]{0,1:T(8,128)S(1)} %bitcast.205), kind=kOutput, calls=%fused_computation.75 | convolution fusion | flops 1141374976 | bytes 18358272 | tf_op jit(solution)/shard_map/hts,shv->thv/dot_general | solution.py:276
  (147 shorter events, 78.7 us)
Async XLA Ops:
  7.2 221.5 %copy-start = (bf16[512,2048]{1,0:T(8,128)(2,1)S(1)}, bf16[512,2048]{1,0:T(8,128)(2,1)}, u32[]{:S(2)}) copy-start(bf16[512,2048]{1,0:T(8,128)(2,1)} %param.19) | copy-start | bytes 6291460
  7.2 221.5 %all-gather.2.cloned.1.call-start = ((), (), s32[]{:S(2)}) async-start(), calls=%async_computation | async-start | bytes 4866048 | tf_op jit(solution)/shard_map/all_gather | solution.py:238
  9.5 6.8 %copy-start.15 = (f32[128,16]{0,1:T(8,128)S(1)}, f32[128,16]{0,1:T(8,128)}, u32[]{:S(2)}) copy-start(f32[128,16]{0,1:T(8,128)} %param.16) | copy-start | bytes 24580
  70.7 6.6 %copy-start.3 = (f32[2,16,64,128]{3,2,1,0:T(8,128)S(1)}, f32[2,16,64,128]{3,2,1,0:T(8,128)}, u32[]{:S(2)}) copy-start(f32[2,16,64,128]{3,2,1,0:T(8,128)} %get-tuple-element.219) | copy-start | bytes 3145732 | tf_op jit(solution)/shard_map/while
  70.7 6.6 %copy-start.5 = (f32[2,16,64,128]{3,2,1,0:T(8,128)S(1)}, f32[2,16,64,128]{3,2,1,0:T(8,128)}, u32[]{:S(2)}) copy-start(f32[2,16,64,128]{3,2,1,0:T(8,128)} %get-tuple-element.220) | copy-start | bytes 3145732 | tf_op jit(solution)/shard_map/while
  70.7 6.6 %copy-start.11 = (f32[2,16,64,128]{3,2,0,1:T(8,128)S(1)}, f32[2,16,64,128]{3,2,0,1:T(8,128)}, u32[]{:S(2)}) copy-start(f32[2,16,64,128]{3,2,0,1:T(8,128)} %get-tuple-element.205) | copy-start | bytes 3145732 | tf_op jit(solution)/shard_map/while
  70.8 7.6 %copy-start.4 = (f32[2,16,128,128]{3,2,1,0:T(8,128)S(1)}, f32[2,16,128,128]{3,2,1,0:T(8,128)}, u32[]{:S(2)}) copy-start(f32[2,16,128,128]{3,2,1,0:T(8,128)} %get-tuple-element.218) | copy-start | bytes 6291460 | tf_op jit(solution)/shard_map/while
  80.6 6.6 %copy-start.5 = (f32[2,16,64,128]{3,2,1,0:T(8,128)S(1)}, f32[2,16,64,128]{3,2,1,0:T(8,128)}, u32[]{:S(2)}) copy-start(f32[2,16,64,128]{3,2,1,0:T(8,128)} %get-tuple-element.220) | copy-start | bytes 3145732 | tf_op jit(solution)/shard_map/while
  80.6 6.6 %copy-start.11 = (f32[2,16,64,128]{3,2,0,1:T(8,128)S(1)}, f32[2,16,64,128]{3,2,0,1:T(8,128)}, u32[]{:S(2)}) copy-start(f32[2,16,64,128]{3,2,0,1:T(8,128)} %get-tuple-element.205) | copy-start | bytes 3145732 | tf_op jit(solution)/shard_map/while
  80.7 7.5 %copy-start.4 = (f32[2,16,128,128]{3,2,1,0:T(8,128)S(1)}, f32[2,16,128,128]{3,2,1,0:T(8,128)}, u32[]{:S(2)}) copy-start(f32[2,16,128,128]{3,2,1,0:T(8,128)} %get-tuple-element.218) | copy-start | bytes 6291460 | tf_op jit(solution)/shard_map/while
  92.5 19.1 %collective-permute-start.4 = (bf16[16,128,128]{2,1,0:T(8,128)(2,1)}, bf16[16,128,128]{2,1,0:T(8,128)(2,1)}, u32[]{:S(2)}, u32[]{:S(2)}) collective-permute-start(bf16[16,128,128]{2,1,0:T(8,128)(2,1)} %convert_element_type.135), channel_id=1, source_target_pairs={{0,8},{8,16},{16,24},{24,32},{32,40},{40,48},{48,56},{56,64},{64,7... | collective-permute-start | bytes 1572872 | tf_op jit(solution)/shard_map/ppermute | solution.py:42
  96.7 28.6 %collective-permute-start = (bf16[16,128,128]{2,1,0:T(8,128)(2,1)}, bf16[16,128,128]{2,1,0:T(8,128)(2,1)}, u32[]{:S(2)}, u32[]{:S(2)}) collective-permute-start(bf16[16,128,128]{2,1,0:T(8,128)(2,1)} %convert_element_type.131), channel_id=1, source_target_pairs={{0,8},{8,16},{16,24},{24,32},{32,40},{40,48},{48,56},{56,64},{64,7... | collective-permute-start | bytes 1572872 | tf_op jit(solution)/shard_map/ppermute | solution.py:42
  113.7 20.6 %collective-permute-start.5 = (bf16[16,128,128]{2,1,0:T(8,128)(2,1)S(1)}, bf16[16,128,128]{2,1,0:T(8,128)(2,1)S(1)}, u32[]{:S(2)}, u32[]{:S(2)}) collective-permute-start(bf16[16,128,128]{2,1,0:T(8,128)(2,1)S(1)} %get-tuple-element.125), channel_id=1, source_target_pairs={{0,16},{8,24},{16,32},{24,40},{32,48},{40,56},{48,64},{56,72},{64,... | collective-permute-start | bytes 1572872 | tf_op jit(solution)/shard_map/ppermute | solution.py:42
  127.0 19.2 %collective-permute-start.1 = (bf16[16,128,128]{2,1,0:T(8,128)(2,1)S(1)}, bf16[16,128,128]{2,1,0:T(8,128)(2,1)S(1)}, u32[]{:S(2)}, u32[]{:S(2)}) collective-permute-start(bf16[16,128,128]{2,1,0:T(8,128)(2,1)S(1)} %get-tuple-element.121), channel_id=1, source_target_pairs={{0,16},{8,24},{16,32},{24,40},{32,48},{40,56},{48,64},{56,72},{64,... | collective-permute-start | bytes 1572872 | tf_op jit(solution)/shard_map/ppermute | solution.py:42
  135.0 18.3 %collective-permute-start.6 = (bf16[16,128,128]{2,1,0:T(8,128)(2,1)S(1)}, bf16[16,128,128]{2,1,0:T(8,128)(2,1)S(1)}, u32[]{:S(2)}, u32[]{:S(2)}) collective-permute-start(bf16[16,128,128]{2,1,0:T(8,128)(2,1)S(1)} %get-tuple-element.127), channel_id=1, source_target_pairs={{0,32},{8,40},{16,48},{24,56},{32,64},{40,72},{48,80},{56,88},{64,... | collective-permute-start | bytes 1572872 | tf_op jit(solution)/shard_map/ppermute | solution.py:42
  146.9 79.3 %copy-start.13 = (f32[2,16,64,128]{3,2,0,1:T(8,128)S(1)}, f32[2,16,64,128]{3,2,0,1:T(8,128)}, u32[]{:S(2)}) copy-start(f32[2,16,64,128]{3,2,0,1:T(8,128)} %get-tuple-element.52) | copy-start | bytes 3145732
  146.9 79.3 %copy-start.14 = (f32[2,16,64,128]{3,2,0,1:T(8,128)S(1)}, f32[2,16,64,128]{3,2,0,1:T(8,128)}, u32[]{:S(2)}) copy-start(f32[2,16,64,128]{3,2,0,1:T(8,128)} %get-tuple-element.55) | copy-start | bytes 3145732
  146.9 23.5 %collective-permute-start.2 = (bf16[16,128,128]{2,1,0:T(8,128)(2,1)S(1)}, bf16[16,128,128]{2,1,0:T(8,128)(2,1)S(1)}, u32[]{:S(2)}, u32[]{:S(2)}) collective-permute-start(bf16[16,128,128]{2,1,0:T(8,128)(2,1)S(1)} %get-tuple-element.123), channel_id=1, source_target_pairs={{0,32},{8,40},{16,48},{24,56},{32,64},{40,72},{48,80},{56,88},{64,... | collective-permute-start | bytes 1572872 | tf_op jit(solution)/shard_map/ppermute | solution.py:42
  154.0 71.9 %collective-permute-start.8 = (bf16[16,128,128]{2,1,0:T(8,128)(2,1)S(1)}, bf16[16,128,128]{2,1,0:T(8,128)(2,1)S(1)}, u32[]{:S(2)}, u32[]{:S(2)}) collective-permute-start(bf16[16,128,128]{2,1,0:T(8,128)(2,1)S(1)} %fusion.37), channel_id=1, source_target_pairs={{0,8},{8,16},{16,24},{24,32},{32,40},{40,48},{48,56},{56,64},{64,7... | collective-permute-start | bytes 1572872 | tf_op jit(solution)/shard_map/ppermute | solution.py:42
  162.9 63.0 %collective-permute-start.7 = (bf16[16,128,128]{2,1,0:T(8,128)(2,1)S(1)}, bf16[16,128,128]{2,1,0:T(8,128)(2,1)S(1)}, u32[]{:S(2)}, u32[]{:S(2)}) collective-permute-start(bf16[16,128,128]{2,1,0:T(8,128)(2,1)S(1)} %fusion.37), channel_id=1, source_target_pairs={{0,72},{8,80},{16,88},{24,96},{32,104},{40,112},{48,120},{56,128},... | collective-permute-start | bytes 1572872 | tf_op jit(solution)/shard_map/ppermute | solution.py:42
  171.0 54.9 %collective-permute-start.3 = (bf16[16,128,128]{2,1,0:T(8,128)(2,1)S(1)}, bf16[16,128,128]{2,1,0:T(8,128)(2,1)S(1)}, u32[]{:S(2)}, u32[]{:S(2)}) collective-permute-start(bf16[16,128,128]{2,1,0:T(8,128)(2,1)S(1)} %convolution_convert_fusion.2), channel_id=1, source_target_pairs={{0,8},{8,16},{16,24},{24,32},{32,40},{40,48},{48,56},{56,64},{64,7... | collective-permute-start | bytes 1572872 | tf_op jit(solution)/shard_map/ppermute | solution.py:42
  228.7 9.1 %copy-start.8 = (bf16[128,3072]{0,1:T(8,128)(2,1)S(1)}, bf16[128,3072]{0,1:T(8,128)(2,1)}, u32[]{:S(2)}) copy-start(bf16[128,3072]{0,1:T(8,128)(2,1)} %copy.102) | copy-start | bytes 2359300
  237.8 12.4 %copy-start.16 = (bf16[512,2048]{1,0:T(8,128)(2,1)S(1)}, bf16[512,2048]{1,0:T(8,128)(2,1)}, u32[]{:S(2)}) copy-start(bf16[512,2048]{1,0:T(8,128)(2,1)} %param.20) | copy-start | bytes 6291460
  273.4 9.7 %copy-start.1 = (bf16[512,2048]{1,0:T(8,128)(2,1)S(1)}, bf16[512,2048]{1,0:T(8,128)(2,1)}, u32[]{:S(2)}) copy-start(bf16[512,2048]{1,0:T(8,128)(2,1)} %param.19) | copy-start | bytes 6291460
  (10 other events, 42.3 us)
Sparse Core Ops, SparseCore 0:
  10.5 85.9 all-gather.1

commit v2 on v1

--- a/solution.py
+++ b/solution.py
@@ -184,7 +184,10 @@
 
     slab_pair, per_block = lax.scan(advance_block, (identity_map, zero_add), block_outs)
     effective_everything, output_everything = per_block
-    carried_in = incoming_state(slab_pair, slab_rows)
+    attend_group, group_count = latent_attention(
+        mla_query, latents, key_up, value_up, positions, docids, doc_starts, head_count
+    )
+    carried_in, mla_parts = incoming_state(slab_pair, slab_rows, attend_group, group_count)
     delta_attention_complete = output_everything + jnp.einsum(
         "enzx,nxu->enzu", effective_everything, carried_in, precision=PRECISE_PRODUCT
     )
@@ -193,9 +196,7 @@
         .reshape(slab_rows, -1)
         .astype(jnp.bfloat16)
     )
-    mla_out = latent_attention(
-        mla_query, latents, key_up, value_up, positions, docids, doc_starts, head_count
-    )
+    mla_out = jnp.concatenate(mla_parts, axis=1).reshape(slab_rows, -1)
     return (kda_out, mla_out)
 
 
@@ -204,27 +205,45 @@
     return -(-longest // slab_rows)
 
 
-def incoming_state(slab_pair, slab_rows):
+def carry_rounds(slab_rows):
+    window = window_slabs_of(slab_rows)
+    distance, rounds = 1, 1
+    while 2 * distance < window:
+        distance, rounds = 2 * distance, rounds + 1
+    return rounds
+
+
+def incoming_state(slab_pair, slab_rows, attend_group, group_count):
     map_now, add_now = slab_pair
     window = window_slabs_of(slab_rows)
-
-    def received(value, distance):
-        return shifted(value.astype(jnp.bfloat16), "ctx", distance).astype(jnp.float32)
+    rounds = carry_rounds(slab_rows)
+    groups_at = [[] for _ in range(rounds)]
+    for group in range(group_count):
+        groups_at[group * rounds // group_count].append(group)
+    parts = []
+
+    def exchange(values, distances, step):
+        sent = tuple(v.astype(jnp.bfloat16) for v in values)
+        sent = lax.optimization_barrier(sent)
+        got = tuple(shifted(v, "ctx", d) for v, d in zip(sent, distances))
+        done = [attend_group(group, sent[0]) for group in groups_at[step]]
+        got, done = lax.optimization_barrier((got, done))
+        parts.extend(done)
+        return tuple(v.astype(jnp.float32) for v in got)
 
     def product(left, right):
         return jnp.einsum("hkj,hjl->hkl", left, right, precision=PRECISE_PRODUCT)
 
-    distance = 1
+    distance, step = 1, 0
     while 2 * distance < window:
-        map_before = received(map_now, distance)
-        add_before = received(add_now, distance)
+        map_before, add_before = exchange((map_now, add_now), (distance, distance), step)
         add_now = product(map_now, add_before) + add_now
         map_now = product(map_now, map_before)
-        distance *= 2
-    map_last = received(map_now, 1)
-    add_last = received(add_now, 1)
-    add_far = received(add_now, distance + 1)
-    return product(map_last, add_far) + add_last
+        distance, step = 2 * distance, step + 1
+    map_last, add_last, add_far = exchange(
+        (map_now, add_now, add_now), (1, 1, distance + 1), step
+    )
+    return product(map_last, add_far) + add_last, parts
 
 
 def latent_attention(
@@ -239,46 +258,71 @@
     first_slab = jnp.clip(lax.axis_index("ctx") - reach, 0, slabs - window_slabs)
     key_first = first_slab * slab_rows
     key_rows = lax.dynamic_slice_in_dim(everything, key_first, window_rows, 0)
-    latent_part = key_rows[:, :LATENT]
-    keys_nope = (
-        jnp.dot(latent_part, key_up, preferred_element_type=jnp.float32)
-        .astype(jnp.bfloat16)
-        .reshape(window_rows, head_count, NOPE)
-    )
-    values = (
-        jnp.dot(latent_part, value_up, preferred_element_type=jnp.float32)
-        .astype(jnp.bfloat16)
-        .reshape(window_rows, head_count, -1)
-    )
     queries = mla_query.reshape(slab_rows, head_count, NOPE + ROPE)
     score_scale = 1.0 / math.sqrt(NOPE + ROPE)
-    scores = jnp.einsum(
-        "thd,shd->hts", queries[:, :, :NOPE], keys_nope, preferred_element_type=jnp.float32
-    )
-    scores = (
-        scores
-        + jnp.einsum(
-            "thr,sr->hts",
-            queries[:, :, NOPE:],
-            key_rows[:, LATENT:],
-            preferred_element_type=jnp.float32,
-        )
-    ) * score_scale
     key_places = key_first + jnp.arange(window_rows, dtype=jnp.int32)
     key_docs = doc_of(key_places, doc_starts)
     allowed = (key_places[None, :] <= positions[:, None]) & (
         key_docs[None, :] == docids[:, None]
     )
-    masked = jnp.where(allowed[None], scores, -1e30)
-    row_max = jnp.max(masked, axis=2, keepdims=True)
-    weights = jnp.where(allowed[None], jnp.exp(masked - row_max), 0.0)
-    row_total = jnp.sum(weights, axis=2)
-    summed = jnp.einsum(
-        "hts,shv->thv", weights.astype(jnp.bfloat16), values, preferred_element_type=jnp.float32
-    )
-    return (
-        (summed / jnp.transpose(row_total)[:, :, None]).astype(jnp.bfloat16).reshape(slab_rows, -1)
-    )
+    value_width = value_up.shape[1] // head_count
+    group_count = carry_rounds(slab_rows)
+    while head_count % group_count:
+        group_count -= 1
+    per_group = head_count // group_count
+
+    def attend_group(group, tie):
+        rows, _ = lax.optimization_barrier((key_rows, tie))
+        heads = slice(group * per_group, (group + 1) * per_group)
+        latent_part = rows[:, :LATENT]
+        keys_nope = (
+            jnp.dot(
+                latent_part,
+                key_up[:, group * per_group * NOPE : (group + 1) * per_group * NOPE],
+                preferred_element_type=jnp.float32,
+            )
+            .astype(jnp.bfloat16)
+            .reshape(window_rows, per_group, NOPE)
+        )
+        values = (
+            jnp.dot(
+                latent_part,
+                value_up[
+                    :, group * per_group * value_width : (group + 1) * per_group * value_width
+                ],
+                preferred_element_type=jnp.float32,
+            )
+            .astype(jnp.bfloat16)
+            .reshape(window_rows, per_group, value_width)
+        )
+        scores = jnp.einsum(
+            "thd,shd->hts",
+            queries[:, heads, :NOPE],
+            keys_nope,
+            preferred_element_type=jnp.float32,
+        )
+        scores = (
+            scores
+            + jnp.einsum(
+                "thr,sr->hts",
+                queries[:, heads, NOPE:],
+                rows[:, LATENT:],
+                preferred_element_type=jnp.float32,
+            )
+        ) * score_scale
+        masked = jnp.where(allowed[None], scores, -1e30)
+        row_max = jnp.max(masked, axis=2, keepdims=True)
+        weights = jnp.where(allowed[None], jnp.exp(masked - row_max), 0.0)
+        row_total = jnp.sum(weights, axis=2)
+        summed = jnp.einsum(
+            "hts,shv->thv",
+            weights.astype(jnp.bfloat16),
+            values,
+            preferred_element_type=jnp.float32,
+        )
+        return (summed / jnp.transpose(row_total)[:, :, None]).astype(jnp.bfloat16)
+
+    return attend_group, group_count
 
 
 def solution(mesh):

time: 295 us -> 273 us (0.925)
  the two profiles are of different devices: /device:TPU:120 before, /device:TPU:192 now
where the time goes in v2:
time: 273 us; the launch traced here: 267 us
  matrix products  130 us (48%)
  waiting for transfers between devices  56.7 us (21%)
  starting transfers between devices  23.1 us (8%)
  other arithmetic  21.8 us (8%)
  local copies, waits for them, and re-layouts  21.1 us (8%)
  between operations  15 us (5%)
    ppermute x9, waiting for transfers between devices, shifted(): return lax.ppermute(block, axis, route)  56 us
    dot_general x4, matrix products, attend_group(): jnp.einsum('hts,shv->thv', weights.astype(jnp.bfloat16), values, preferre...  25.8 us
    ppermute x9, starting transfers between devices, shifted(): return lax.ppermute(block, axis, route)  23 us
    dot_general x7, matrix products, product(): return jnp.einsum('hkj,hjl->hkl', left, right, precision=PRECISE_PRODUCT)  16 us
    dot_general x4, matrix products, attend_group(): jnp.dot(latent_part, value_up[:, group * per_group * value_width:(group +...  15.7 us
    unnamed x63, local copies, waits for them, and re-layouts  10.7 us
    dot_general x4, matrix products, attend_group(): jnp.dot(latent_part, key_up[:, group * per_group * NOPE:(group + 1) * per...  10.4 us
    unnamed x7, other arithmetic  6.22 us
  transfers between devices with their start and end apart: 10, of which 5 were waited for; matrix products, arithmetic and copies ran while one was open for 55% of the time, Pallas kernels for 0%

profile of v2, /device:TPU:192, one launch (start us, length us, event | category | flops | bytes accessed | tf_op | source)
XLA Modules:
  0.0 267.5 jit_solution(13347468278253966466)
XLA Ops:
  25.9 3.4 %fusion.70 = f32[2,16,64,64]{3,2,1,0:T(8,128)S(1)} fusion(f32[2,16,64]{2,1,0:T(8,128)S(1)} %get-tuple-element.167, pred[2,64,64]{2,1,0:T(8,128)(4,1)S(1)} %get-tuple-element.170, f32[2,64,16,128]{3,2,1,0:T(8,128)S(1)} %bitcast.260, f32[2,64,16]{1,2,0:T(8,128)S(1)} %copy.124, f32[2,64,16,128]{3,2,1,0:T(8,128)S(1)} %fusion.112), kind=kOutput, calls=%fused_computation.99 | convolution fusion | flops 202899456 | bytes 2646016 | tf_op jit(solution)/shard_map/vmap(thk,shk->hts)/dot_general | solution.py:79
  42.9 2.9 %convolution_select_fusion = f32[2,16,64,64]{3,2,1,0:T(8,128)S(1)} fusion(pred[2,64,64]{2,1,0:T(8,128)(4,1)S(1)} %get-tuple-element.169, f32[2,64,16,128]{3,2,1,0:T(8,128)S(1)} %bitcast.265, f32[2,64,16]{1,2,0:T(8,128)S(1)} %copy.133, f32[2,64,16,128]{3,2,1,0:T(8,128)S(1)} %fusion.112, f32[2,64,16,128]{3,2,1,0:T(8,128)S(1)} %bitcast.261, ...), kind=kOutput, calls=%fused_computation.97 | convolution fusion | flops 202768384 | bytes 3694592 | tf_op jit(solution)/shard_map/vmap(thk,shk->hts)/dot_general | solution.py:90
  50.0 3.0 %convolution_subtract_fusion = f32[2,16,64,128]{3,2,1,0:T(8,128)} fusion(f32[2,16,64,64]{3,2,1,0:T(8,128)S(1)} %convolution_select_fusion, f32[2,16,64,128]{3,2,1,0:T(8,128)S(1)} %fusion.116, f32[2,64]{1,0:T(2,128)S(1)} %get-tuple-element.172, f32[2,64,16]{1,2,0:T(8,128)S(1)} %copy.133, f32[2,64,16,128]{3,2,1,0:T(8,128)S(1)} %bitcast.266, ...), kind=kOutput, calls=%fused_computation.95 | convolution fusion | flops 202375168 | bytes 4727296 | tf_op jit(solution)/shard_map/vmap(hts,hsk->htk)/dot_general | solution.py:94
  53.0 5.6 %fusion.159 = f32[2,16,128,128]{3,2,1,0:T(8,128)} fusion(f32[2,16,64,128]{3,2,1,0:T(8,128)S(1)} %fusion.114, f32[2,64,16,128]{3,2,1,0:T(8,128)S(1)} %fusion.112, f32[2,64,16,128]{3,2,1,0:T(8,128)S(1)} %bitcast.263, f32[2,64]{1,0:T(2,128)S(1)} %get-tuple-element.171, f32[2,16,128]{2,1,0:T(8,128)S(1)} %slice_bitcast_fusion, f32[2,64,16]{1,2,0:T(8,128)S(1)} %copy.124), kind=kOutput, calls=%fused_computation.179 | convolution fusion | flops 403701760 | bytes 5267968 | tf_op jit(solution)/shard_map/vmap(omt,mor->mtr)/dot_general | solution.py:106
  58.6 6.1 %multiply_subtract_fusion = f32[2,16,128,128]{3,2,1,0:T(8,128)S(1)} fusion(f32[2,16,64,128]{3,2,1,0:T(8,128)S(1)} %fusion.116, f32[128,128]{1,0:T(8,128)S(1)} %fusion.164, f32[2,16,128]{2,1,0:T(8,128)S(1)} %bitcast.286, f32[2]{0:T(128)S(1)} %slice_reduce_fusion.1, f32[2,64,16,128]{3,2,1,0:T(8,128)S(1)} %fusion.112, f32[2,64,16,128]{3,2,1,0:T(8,128)} %bitcast.264, ...), kind=kOutput, calls=%fused_computation.79 | convolution fusion | flops 405274624 | bytes 5349896 | tf_op jit(solution)/shard_map/vmap(shk,hsj->hkj)/dot_general | solution.py:103
  64.8 20.0 %while.17 = (s32[]{:T(128)}, f32[16,128,128]{2,1,0:T(8,128)S(1)}, f32[16,128,128]{2,1,0:T(8,128)}, f32[2,16,64,128]{3,2,0,1:T(8,128)}, f32[2,16,64,128]{3,2,0,1:...) while((s32[]{:T(128)}, f32[16,128,128]{2,1,0:T(8,128)S(1)}, ...), condition=%wide.region_7.8_spmd.clone, body=%wide.region_6.7_spmd.clone.sunk | while | flops 1208877056 | bytes 37227752 | solution.py:185
  66.2 3.1 %fusion.268 = f32[2,16,64,128]{3,2,0,1:T(8,128)} fusion(f32[2,16,64,128]{3,2,0,1:T(8,128)} %get-tuple-element.253, s32[]{:T(128)} %get-tuple-element.249, f32[16,128,128]{2,1,0:T(8,128)S(1)} %copy.251, f32[2,16,64,128]{3,2,1,0:T(8,128)} %get-tuple-element.268, pred[]{:T(512)S(6)} %compare.3, f32[2,16,64,128]{3,2,1,0:T(8,128)} %get-tuple-element.267), kind=kOutput, calls=%fused_computation.3.clone.1 | convolution fusion | flops 201719808 | bytes 2622465 | tf_op jit(solution)/shard_map/while/body/eval_jaxpr/cor,crm->com/dot_general | solution.py:171
  76.1 3.1 %fusion.268 = f32[2,16,64,128]{3,2,0,1:T(8,128)} fusion(f32[2,16,64,128]{3,2,0,1:T(8,128)} %get-tuple-element.253, s32[]{:T(128)} %get-tuple-element.249, f32[16,128,128]{2,1,0:T(8,128)S(1)} %copy.251, f32[2,16,64,128]{3,2,1,0:T(8,128)} %get-tuple-element.268, pred[]{:T(512)S(6)} %compare.3, f32[2,16,64,128]{3,2,1,0:T(8,128)} %get-tuple-element.267), kind=kOutput, calls=%fused_computation.3.clone.1 | convolution fusion | flops 201719808 | bytes 2622465 | tf_op jit(solution)/shard_map/while/body/eval_jaxpr/cor,crm->com/dot_general | solution.py:171
  87.7 3.4 %collective-permute-start = (bf16[16,128,128]{2,1,0:T(8,128)(2,1)}, bf16[16,128,128]{2,1,0:T(8,128)(2,1)}, u32[]{:S(2)}, u32[]{:S(2)}) collective-permute-start(bf16[16,128,128]{2,1,0:T(8,128)(2,1)} %convert_element_type.167), channel_id=1, source_target_pairs={{0,8},{8,16},{16,24},{24,32},{32,40},{40,48},{48,56},{56,64},{64,7... | collective-permute-start | bytes 1572872 | tf_op jit(solution)/shard_map/ppermute | solution.py:42
  91.1 3.4 %collective-permute-start.1 = (bf16[16,128,128]{2,1,0:T(8,128)(2,1)}, bf16[16,128,128]{2,1,0:T(8,128)(2,1)}, u32[]{:S(2)}, u32[]{:S(2)}) collective-permute-start(bf16[16,128,128]{2,1,0:T(8,128)(2,1)} %convert_element_type.168), channel_id=1, source_target_pairs={{0,8},{8,16},{16,24},{24,32},{32,40},{40,48},{48,56},{56,64},{64,7... | collective-permute-start | bytes 1572872 | tf_op jit(solution)/shard_map/ppermute | solution.py:42
  98.8 2.9 %convolution_convert_fusion.6 = bf16[2176,512]{0,1:T(8,128)(2,1)S(1)} fusion(bf16[2176,576]{0,1:T(8,128)(2,1)S(1)} %constant_dynamic-slice_fusion, bf16[512,2048]{1,0:T(8,128)(2,1)} %param.19), kind=kOutput, calls=%fused_computation.69 | convolution fusion | flops 1141964800 | bytes 4980736 | tf_op jit(solution)/shard_map/dot_general | solution.py:279
  105.5 3.9 %convolution_convert_fusion.7 = bf16[2176,512]{0,1:T(8,128)(2,1)} fusion(bf16[2176,576]{0,1:T(8,128)(2,1)S(1)} %constant_dynamic-slice_fusion, bf16[512,2048]{1,0:T(8,128)(2,1)} %param.20), kind=kOutput, calls=%fused_computation.70 | convolution fusion | flops 1141964800 | bytes 4980736 | tf_op jit(solution)/shard_map/dot_general | solution.py:288
  109.5 6.0 %fusion.107 = bf16[128,4,128]{0,2,1:T(8,128)(2,1)S(1)} fusion(bf16[2176,4,128]{0,2,1:T(8,128)(2,1)} %bitcast.289, f32[128,4]{0,1:T(4,128)S(1)} %bitcast.295, f32[4,128,2176]{1,2,0:T(8,128)} %copy-done.11, pred[128,2176]{0,1:T(8,128)(4,1)S(1)} %compare_and_fusion), kind=kOutput, calls=%fused_computation.119 | convolution fusion | flops 288688768 | bytes 7096320 | tf_op jit(solution)/shard_map/hts,shv->thv/dot_general | solution.py:317
  132.0 4.6 %collective-permute-start.3 = (bf16[16,128,128]{2,1,0:T(8,128)(2,1)}, bf16[16,128,128]{2,1,0:T(8,128)(2,1)S(1)}, u32[]{:S(2)}, u32[]{:S(2)}) collective-permute-start(bf16[16,128,128]{2,1,0:T(8,128)(2,1)} %get-tuple-element.87), channel_id=1, source_target_pairs={{0,16},{8,24},{16,32},{24,40},{32,48},{40,56},{48,64},{56,72},{64,... | collective-permute-start | bytes 1572872 | tf_op jit(solution)/shard_map/ppermute | solution.py:42
  136.7 3.9 %convolution_convert_fusion.5 = bf16[2176,512]{0,1:T(8,128)(2,1)} fusion(bf16[2176,576]{0,1:T(8,128)(2,1)S(1)} %copy-done.5, bf16[512,2048]{1,0:T(8,128)(2,1)} %param.20), kind=kOutput, calls=%fused_computation.68 | convolution fusion | flops 1141964800 | bytes 4980736 | tf_op jit(solution)/shard_map/dot_general | solution.py:288
  140.6 6.6 %fusion.104 = bf16[128,4,128]{0,2,1:T(8,128)(2,1)} fusion(bf16[2176,4,128]{0,2,1:T(8,128)(2,1)} %bitcast.290, f32[128,4]{0,1:T(4,128)S(1)} %bitcast.293, f32[4,128,2176]{1,2,0:T(8,128)} %copy-done.9, pred[128,2176]{0,1:T(8,128)(4,1)S(1)} %compare_and_fusion), kind=kOutput, calls=%fused_computation.118 | convolution fusion | flops 288688768 | bytes 7096320 | tf_op jit(solution)/shard_map/hts,shv->thv/dot_general | solution.py:317
  147.2 5.5 %collective-permute-done.3 = bf16[16,128,128]{2,1,0:T(8,128)(2,1)S(1)} collective-permute-done((bf16[16,128,128]{2,1,0:T(8,128)(2,1)}, bf16[16,128,128]{2,1,0:T(8,128)(2,1)S(1)}, u32[]{:S(2)}, u32[]{:S(2)}) %collective-permute-start.3) | collective-permute-done | bytes 524320 | tf_op jit(solution)/shard_map/ppermute | solution.py:42
  168.0 3.9 %convolution_convert_fusion.3 = bf16[2176,512]{0,1:T(8,128)(2,1)} fusion(bf16[2176,576]{0,1:T(8,128)(2,1)S(1)} %copy-done.6, bf16[512,2048]{1,0:T(8,128)(2,1)} %param.20), kind=kOutput, calls=%fused_computation.66 | convolution fusion | flops 1141964800 | bytes 4980736 | tf_op jit(solution)/shard_map/dot_general | solution.py:288
  171.9 6.6 %fusion.101 = bf16[128,4,128]{0,2,1:T(8,128)(2,1)} fusion(bf16[2176,4,128]{0,2,1:T(8,128)(2,1)} %bitcast.291, f32[128,4]{0,1:T(4,128)S(1)} %bitcast.294, f32[4,128,2176]{1,2,0:T(8,128)} %copy-done.10, pred[128,2176]{0,1:T(8,128)(4,1)S(1)} %compare_and_fusion), kind=kOutput, calls=%fused_computation.117 | convolution fusion | flops 288688768 | bytes 7096320 | tf_op jit(solution)/shard_map/hts,shv->thv/dot_general | solution.py:317
  178.5 4.9 %collective-permute-done.5 = bf16[16,128,128]{2,1,0:T(8,128)(2,1)} collective-permute-done((bf16[16,128,128]{2,1,0:T(8,128)(2,1)}, bf16[16,128,128]{2,1,0:T(8,128)(2,1)}, u32[]{:S(2)}, u32[]{:S(2)}) %collective-permute-start.5) | collective-permute-done | bytes 524320 | tf_op jit(solution)/shard_map/ppermute | solution.py:42
  200.2 3.9 %convolution_convert_fusion.1 = bf16[2176,512]{0,1:T(8,128)(2,1)} fusion(bf16[2176,576]{0,1:T(8,128)(2,1)S(1)} %copy-done.7, bf16[512,2048]{1,0:T(8,128)(2,1)} %param.20), kind=kOutput, calls=%fused_computation.64 | convolution fusion | flops 1141964800 | bytes 4980736 | tf_op jit(solution)/shard_map/dot_general | solution.py:288
  204.1 6.6 %fusion.98 = bf16[128,4,128]{0,2,1:T(8,128)(2,1)} fusion(bf16[2176,4,128]{0,2,1:T(8,128)(2,1)} %bitcast.288, f32[128,4]{0,1:T(4,128)S(1)} %bitcast.292, f32[4,128,2176]{1,2,0:T(8,128)} %copy-done.8, pred[128,2176]{0,1:T(8,128)(4,1)S(1)} %compare_and_fusion), kind=kOutput, calls=%fused_computation.116 | convolution fusion | flops 288688768 | bytes 7096320 | tf_op jit(solution)/shard_map/hts,shv->thv/dot_general | solution.py:317
  210.7 9.8 %collective-permute-done.7 = bf16[16,128,128]{2,1,0:T(8,128)(2,1)S(1)} collective-permute-done((bf16[16,128,128]{2,1,0:T(8,128)(2,1)}, bf16[16,128,128]{2,1,0:T(8,128)(2,1)S(1)}, u32[]{:S(2)}, u32[]{:S(2)}) %collective-permute-start.7) | collective-permute-done | bytes 524320 | tf_op jit(solution)/shard_map/ppermute | solution.py:42
  221.4 33.1 %collective-permute-done.8 = bf16[16,128,128]{2,1,0:T(8,128)(2,1)} collective-permute-done((bf16[16,128,128]{2,1,0:T(8,128)(2,1)}, bf16[16,128,128]{2,1,0:T(8,128)(2,1)}, u32[]{:S(2)}, u32[]{:S(2)}) %collective-permute-start.8) | collective-permute-done | bytes 524320 | tf_op jit(solution)/shard_map/ppermute | solution.py:42
  (190 shorter events, 116.0 us)
Async XLA Ops:
  7.2 89.7 %all-gather.2.cloned.1.call-start = ((), (), s32[]{:S(2)}) async-start(), calls=%async_computation | async-start | bytes 4866048 | tf_op jit(solution)/shard_map/all_gather | solution.py:257
  18.4 34.5 %copy-start.1 = (f32[16,8,16,128]{3,2,1,0:T(8,128)}, f32[16,8,16,128]{3,2,1,0:T(8,128)S(1)}, u32[]{:S(2)}) copy-start(f32[16,8,16,128]{3,2,1,0:T(8,128)S(1)} %copy.177) | copy-start | bytes 3145732
  84.7 9.9 %copy-start.21 = (bf16[128,3072]{1,0:T(8,128)(2,1)S(1)}, bf16[128,3072]{1,0:T(8,128)(2,1)}, u32[]{:S(2)}) copy-start(bf16[128,3072]{1,0:T(8,128)(2,1)} %param.17) | copy-start | bytes 2359300
  87.7 27.7 %collective-permute-start = (bf16[16,128,128]{2,1,0:T(8,128)(2,1)}, bf16[16,128,128]{2,1,0:T(8,128)(2,1)}, u32[]{:S(2)}, u32[]{:S(2)}) collective-permute-start(bf16[16,128,128]{2,1,0:T(8,128)(2,1)} %convert_element_type.167), channel_id=1, source_target_pairs={{0,8},{8,16},{16,24},{24,32},{32,40},{40,48},{48,56},{56,64},{64,7... | collective-permute-start | bytes 1572872 | tf_op jit(solution)/shard_map/ppermute | solution.py:42
  91.1 27.0 %collective-permute-start.1 = (bf16[16,128,128]{2,1,0:T(8,128)(2,1)}, bf16[16,128,128]{2,1,0:T(8,128)(2,1)}, u32[]{:S(2)}, u32[]{:S(2)}) collective-permute-start(bf16[16,128,128]{2,1,0:T(8,128)(2,1)} %convert_element_type.168), channel_id=1, source_target_pairs={{0,8},{8,16},{16,24},{24,32},{32,40},{40,48},{48,56},{56,64},{64,7... | collective-permute-start | bytes 1572872 | tf_op jit(solution)/shard_map/ppermute | solution.py:42
  95.0 34.2 %copy-start.14 = (bf16[128,3072]{0,1:T(8,128)(2,1)}, bf16[128,3072]{0,1:T(8,128)(2,1)S(1)}, u32[]{:S(2)}) copy-start(bf16[128,3072]{0,1:T(8,128)(2,1)S(1)} %copy.135) | copy-start | bytes 2359300
  98.8 6.1 %copy-start.4 = (bf16[2176,576]{0,1:T(8,128)(2,1)}, bf16[2176,576]{0,1:T(8,128)(2,1)S(1)}, u32[]{:S(2)}) copy-start(bf16[2176,576]{0,1:T(8,128)(2,1)S(1)} %constant_dynamic-slice_fusion) | copy-start | bytes 7520260
  109.5 8.7 %copy-start = (f32[16,128,128]{2,1,0:T(8,128)S(1)}, f32[16,128,128]{2,1,0:T(8,128)}, u32[]{:S(2)}) copy-start(f32[16,128,128]{2,1,0:T(8,128)} %get-tuple-element.80) | copy-start | bytes 3145732
  121.0 4.7 %copy-start.5 = (bf16[2176,576]{0,1:T(8,128)(2,1)S(1)}, bf16[2176,576]{0,1:T(8,128)(2,1)}, u32[]{:S(2)}) copy-start(bf16[2176,576]{0,1:T(8,128)(2,1)} %copy-done.4) | copy-start | bytes 7520260
  123.6 23.6 %collective-permute-start.2 = (bf16[16,128,128]{2,1,0:T(8,128)(2,1)}, bf16[16,128,128]{2,1,0:T(8,128)(2,1)S(1)}, u32[]{:S(2)}, u32[]{:S(2)}) collective-permute-start(bf16[16,128,128]{2,1,0:T(8,128)(2,1)} %get-tuple-element.86), channel_id=1, source_target_pairs={{0,16},{8,24},{16,32},{24,40},{32,48},{40,56},{48,64},{56,72},{64,... | collective-permute-start | bytes 1572872 | tf_op jit(solution)/shard_map/ppermute | solution.py:42
  132.0 20.6 %collective-permute-start.3 = (bf16[16,128,128]{2,1,0:T(8,128)(2,1)}, bf16[16,128,128]{2,1,0:T(8,128)(2,1)S(1)}, u32[]{:S(2)}, u32[]{:S(2)}) collective-permute-start(bf16[16,128,128]{2,1,0:T(8,128)(2,1)} %get-tuple-element.87), channel_id=1, source_target_pairs={{0,16},{8,24},{16,32},{24,40},{32,48},{40,56},{48,64},{56,72},{64,... | collective-permute-start | bytes 1572872 | tf_op jit(solution)/shard_map/ppermute | solution.py:42
  147.2 8.8 %copy-start.13 = (f32[16,128,128]{2,1,0:T(8,128)S(1)}, f32[16,128,128]{2,1,0:T(8,128)}, u32[]{:S(2)}) copy-start(f32[16,128,128]{2,1,0:T(8,128)} %get-tuple-element.176) | copy-start | bytes 3145732
  147.2 5.5 %copy-start.24 = (bf16[16,128,128]{2,1,0:T(8,128)(2,1)}, bf16[16,128,128]{2,1,0:T(8,128)(2,1)S(1)}, u32[]{:S(2)}) copy-start(bf16[16,128,128]{2,1,0:T(8,128)(2,1)S(1)} %collective-permute-done.2) | copy-start | bytes 1572868
  157.5 4.8 %copy-start.15 = (bf16[128,3072]{0,1:T(8,128)(2,1)S(1)}, bf16[128,3072]{0,1:T(8,128)(2,1)}, u32[]{:S(2)}) copy-start(bf16[128,3072]{0,1:T(8,128)(2,1)} %copy-done.14) | copy-start | bytes 2359300
  157.5 21.0 %collective-permute-start.4 = (bf16[16,128,128]{2,1,0:T(8,128)(2,1)}, bf16[16,128,128]{2,1,0:T(8,128)(2,1)}, u32[]{:S(2)}, u32[]{:S(2)}) collective-permute-start(bf16[16,128,128]{2,1,0:T(8,128)(2,1)} %get-tuple-element.91), channel_id=1, source_target_pairs={{0,32},{8,40},{16,48},{24,56},{32,64},{40,72},{48,80},{56,88},{64,... | collective-permute-start | bytes 1572872 | tf_op jit(solution)/shard_map/ppermute | solution.py:42
  166.1 17.4 %collective-permute-start.5 = (bf16[16,128,128]{2,1,0:T(8,128)(2,1)}, bf16[16,128,128]{2,1,0:T(8,128)(2,1)}, u32[]{:S(2)}, u32[]{:S(2)}) collective-permute-start(bf16[16,128,128]{2,1,0:T(8,128)(2,1)} %get-tuple-element.92), channel_id=1, source_target_pairs={{0,32},{8,40},{16,48},{24,56},{32,64},{40,72},{48,80},{56,88},{64,... | collective-permute-start | bytes 1572872 | tf_op jit(solution)/shard_map/ppermute | solution.py:42
  183.4 7.2 %copy-start.7 = (bf16[2176,576]{0,1:T(8,128)(2,1)S(1)}, bf16[2176,576]{0,1:T(8,128)(2,1)}, u32[]{:S(2)}) copy-start(bf16[2176,576]{0,1:T(8,128)(2,1)} %copy-done.4) | copy-start | bytes 7520260
  188.5 22.2 %collective-permute-start.6 = (bf16[16,128,128]{2,1,0:T(8,128)(2,1)}, bf16[16,128,128]{2,1,0:T(8,128)(2,1)S(1)}, u32[]{:S(2)}, u32[]{:S(2)}) collective-permute-start(bf16[16,128,128]{2,1,0:T(8,128)(2,1)} %convolution_convert_fusion.8), channel_id=1, source_target_pairs={{0,8},{8,16},{16,24},{24,32},{32,40},{40,48},{48,56},{56,64},{64,7... | collective-permute-start | bytes 1572872 | tf_op jit(solution)/shard_map/ppermute | solution.py:42
  197.0 23.6 %collective-permute-start.7 = (bf16[16,128,128]{2,1,0:T(8,128)(2,1)}, bf16[16,128,128]{2,1,0:T(8,128)(2,1)S(1)}, u32[]{:S(2)}, u32[]{:S(2)}) collective-permute-start(bf16[16,128,128]{2,1,0:T(8,128)(2,1)} %fusion.71), channel_id=1, source_target_pairs={{0,8},{8,16},{16,24},{24,32},{32,40},{40,48},{48,56},{56,64},{64,7... | collective-permute-start | bytes 1572872 | tf_op jit(solution)/shard_map/ppermute | solution.py:42
  198.9 55.5 %collective-permute-start.8 = (bf16[16,128,128]{2,1,0:T(8,128)(2,1)}, bf16[16,128,128]{2,1,0:T(8,128)(2,1)}, u32[]{:S(2)}, u32[]{:S(2)}) collective-permute-start(bf16[16,128,128]{2,1,0:T(8,128)(2,1)} %fusion.71), channel_id=1, source_target_pairs={{0,72},{8,80},{16,88},{24,96},{32,104},{40,112},{48,120},{56,128},... | collective-permute-start | bytes 1572872 | tf_op jit(solution)/shard_map/ppermute | solution.py:42
  204.1 50.3 %copy-start.27 = (bf16[128,4,128]{0,2,1:T(8,128)(2,1)S(1)}, bf16[128,4,128]{0,2,1:T(8,128)(2,1)}, u32[]{:S(2)}) copy-start(bf16[128,4,128]{0,2,1:T(8,128)(2,1)} %fusion.104) | copy-start | bytes 393220
  204.1 50.3 %copy-start.28 = (bf16[128,4,128]{0,2,1:T(8,128)(2,1)S(1)}, bf16[128,4,128]{0,2,1:T(8,128)(2,1)}, u32[]{:S(2)}) copy-start(bf16[128,4,128]{0,2,1:T(8,128)(2,1)} %fusion.101) | copy-start | bytes 393220
  210.7 47.2 %copy-start.19 = (f32[2,16,64,128]{3,2,0,1:T(8,128)S(1)}, f32[2,16,64,128]{3,2,0,1:T(8,128)}, u32[]{:S(2)}) copy-start(f32[2,16,64,128]{3,2,0,1:T(8,128)} %get-tuple-element.103) | copy-start | bytes 3145732
  210.7 47.2 %copy-start.20 = (f32[2,16,64,128]{3,2,0,1:T(8,128)S(1)}, f32[2,16,64,128]{3,2,0,1:T(8,128)}, u32[]{:S(2)}) copy-start(f32[2,16,64,128]{3,2,0,1:T(8,128)} %get-tuple-element.78) | copy-start | bytes 3145732
  (21 other events, 48.5 us)
Sparse Core Ops, SparseCore 0:
  10.5 84.0 all-gather.1

commit v3 on v2

--- a/solution.py
+++ b/solution.py
@@ -182,8 +182,18 @@
         )
         return ((map_after, increment_later), (eff_now, output_current))
 
-    slab_pair, per_block = lax.scan(advance_block, (identity_map, zero_add), block_outs)
-    effective_everything, output_everything = per_block
+    local_output, query_effective, handed_operator, handed_update = block_outs
+    slab_pair = (handed_operator[0], handed_update[0])
+    effective_blocks, output_blocks = [query_effective[0]], [local_output[0]]
+    for block in range(1, block_count):
+        slab_pair, (eff_now, output_current) = advance_block(
+            slab_pair,
+            (local_output[block], query_effective[block], handed_operator[block], handed_update[block]),
+        )
+        effective_blocks.append(eff_now)
+        output_blocks.append(output_current)
+    effective_everything = jnp.stack(effective_blocks)
+    output_everything = jnp.stack(output_blocks)
     attend_group, group_count = latent_attention(
         mla_query, latents, key_up, value_up, positions, docids, doc_starts, head_count
     )
@@ -234,16 +244,18 @@
     def product(left, right):
         return jnp.einsum("hkj,hjl->hkl", left, right, precision=PRECISE_PRODUCT)
 
+    value_dim = add_now.shape[2]
     distance, step = 1, 0
     while 2 * distance < window:
-        map_before, add_before = exchange((map_now, add_now), (distance, distance), step)
-        add_now = product(map_now, add_before) + add_now
-        map_now = product(map_now, map_before)
+        (before,) = exchange((jnp.concatenate([add_now, map_now], axis=2),), (distance,), step)
+        joined = product(map_now, before)
+        add_now = joined[:, :, :value_dim] + add_now
+        map_now = joined[:, :, value_dim:]
         distance, step = 2 * distance, step + 1
-    map_last, add_last, add_far = exchange(
-        (map_now, add_now, add_now), (1, 1, distance + 1), step
-    )
-    return product(map_last, add_far) + add_last, parts
+    last, add_far = exchange(
+        (jnp.concatenate([add_now, map_now], axis=2), add_now), (1, distance + 1), step
+    )
+    return product(last[:, :, value_dim:], add_far) + last[:, :, :value_dim], parts
 
 
 def latent_attention(

time: 273 us -> 280 us (1.026)
  the two profiles are of different devices: /device:TPU:192 before, /device:TPU:200 now
where the time goes in v3:
time: 280 us; the launch traced here: 275 us
  matrix products  132 us (47%)
  waiting for transfers between devices  75 us (27%)
  other arithmetic  24.5 us (9%)
  local copies, waits for them, and re-layouts  17.6 us (6%)
  between operations  15.1 us (5%)
  starting transfers between devices  11.1 us (4%)
    ppermute x5, waiting for transfers between devices, shifted(): return lax.ppermute(block, axis, route)  56.2 us
    dot_general x4, matrix products, attend_group(): jnp.einsum('hts,shv->thv', weights.astype(jnp.bfloat16), values, preferre...  24.4 us
    all_gather x1, waiting for transfers between devices, latent_attention(): everything = lax.all_gather(latents, 'ctx', tiled=True)  18.1 us
    dot_general x5, matrix products, unit_lower_inverse(): jnp.einsum('hij,hjk->hik', result, identity + power_term, precision=PRECI...  16.6 us
    dot_general x4, matrix products, attend_group(): jnp.dot(latent_part, value_up[:, group * per_group * value_width:(group +...  15.5 us
    unnamed x67, local copies, waits for them, and re-layouts  12 us
    ppermute x5, starting transfers between devices, shifted(): return lax.ppermute(block, axis, route)  11.1 us
    dot_general x4, matrix products, attend_group(): jnp.dot(latent_part, key_up[:, group * per_group * NOPE:(group + 1) * per...  10.4 us
  transfers between devices with their start and end apart: 6, of which 4 were waited for; matrix products, arithmetic and copies ran while one was open for 56% of the time, Pallas kernels for 0%

profile of v3, /device:TPU:200, one launch (start us, length us, event | category | flops | bytes accessed | tf_op | source)
XLA Modules:
  0.0 275.4 jit_solution(11830048499989576270)
XLA Ops:
  19.7 3.3 %fusion.46 = f32[2,16,64,64]{3,2,1,0:T(8,128)S(1)} fusion(f32[2,16,64]{2,1,0:T(8,128)S(1)} %get-tuple-element.43, pred[2,64,64]{2,1,0:T(8,128)(4,1)S(1)} %get-tuple-element.46, f32[2,64,16,128]{3,2,1,0:T(8,128)S(1)} %bitcast.236, f32[2,64,16]{1,2,0:T(8,128)S(1)} %copy.189, f32[2,64,16,128]{3,2,1,0:T(8,128)S(1)} %fusion.88), kind=kOutput, calls=%fused_computation.69 | convolution fusion | flops 202899456 | bytes 2646016 | tf_op jit(solution)/shard_map/vmap(thk,shk->hts)/dot_general | solution.py:79
  33.9 11.8 %fusion.175 = f32[2,16,64,64]{3,2,1,0:T(8,128)S(1)} fusion(f32[2,16,64,64]{3,2,1,0:T(8,128)S(1)} %fusion.100, f32[2,16,64,64]{3,2,1,0:T(8,128)S(1)} %convolution_add_fusion.2), kind=kOutput, calls=%fused_computation.231 | convolution fusion | flops 100663296 | bytes 1572864 | tf_op jit(solution)/shard_map/vmap(hij,hjk->hik)/dot_general | solution.py:61
  49.0 4.7 %multiply_subtract_fusion = f32[2,16,128,128]{3,2,1,0:T(8,128)S(1)} fusion(f32[2,16,64,128]{3,2,1,0:T(8,128)S(1)} %fusion.94, f32[128,128]{1,0:T(8,128)S(1)} %fusion.151, f32[2,16,128]{2,1,0:T(8,128)S(1)} %bitcast.262, f32[2]{0:T(128)S(1)} %slice_reduce_fusion, f32[2,64,16,128]{3,2,1,0:T(8,128)S(1)} %fusion.88, f32[2,64,16,128]{3,2,1,0:T(8,128)S(1)} %bitcast.238, ...), kind=kOutput, calls=%fused_computation.52 | convolution fusion | flops 405274624 | bytes 5349896 | tf_op jit(solution)/shard_map/vmap(shk,hsj->hkj)/dot_general | solution.py:103
  53.7 2.9 %fusion.165 = (bf16[16,128,128]{1,2,0:T(8,128)(2,1)S(1)}, f32[16,128,128]{1,2,0:T(8,128)}) fusion(f32[2,16,128,128]{3,2,1,0:T(8,128)S(1)} %multiply_subtract_fusion), kind=kOutput, calls=%fused_computation.221 | convolution fusion | flops 402915328 | bytes 3670016 | tf_op jit(solution)/shard_map/hkj,hjl->hkl/dot_general | solution.py:174
  56.6 4.2 %fusion.146 = f32[2,16,128,128]{2,3,1,0:T(8,128)S(1)} fusion(f32[2,16,64,128]{3,2,1,0:T(8,128)S(1)} %fusion.96, f32[2,64,16,128]{3,2,1,0:T(8,128)S(1)} %fusion.88, f32[2,64,16,128]{3,2,1,0:T(8,128)S(1)} %bitcast.239, f32[2,64]{1,0:T(2,128)S(1)} %get-tuple-element.47, f32[2,16,128]{2,1,0:T(8,128)S(1)} %slice_bitcast_fusion.14, f32[2,64,16]{1,2,0:T(8,128)S(1)} %copy.189), kind=kOutput, calls=%fused_computation.178 | convolution fusion | flops 403701760 | bytes 5267968 | tf_op jit(solution)/shard_map/vmap(omt,mor->mtr)/dot_general | solution.py:106
  60.8 3.5 %fusion.166 = (bf16[16,128,128]{1,2,0:T(8,128)(2,1)S(1)}, f32[16,128,128]{1,2,0:T(8,128)}) fusion(f32[2,16,128,128]{2,3,1,0:T(8,128)S(1)} %fusion.146, f32[2,16,128,128]{3,2,1,0:T(8,128)S(1)} %multiply_subtract_fusion), kind=kOutput, calls=%fused_computation.222 | convolution fusion | flops 403177472 | bytes 4718592 | tf_op jit(solution)/shard_map/ytn,yne->yte/dot_general | solution.py:178
  65.4 3.4 %collective-permute-start = (bf16[16,128,256]{1,2,0:T(8,128)(2,1)}, bf16[16,128,256]{1,2,0:T(8,128)(2,1)}, u32[]{:S(2)}, u32[]{:S(2)}) collective-permute-start(bf16[16,128,256]{1,2,0:T(8,128)(2,1)} %pad_maximum_fusion), channel_id=1, source_target_pairs={{0,8},{8,16},{16,24},{24,32},{32,40},{40,48},{48,56},{56,64},{64,7... | collective-permute-start | bytes 3145736 | tf_op jit(solution)/shard_map/ppermute | solution.py:42
  76.5 2.9 %convolution_select_fusion.1 = f32[2,16,64,64]{3,2,1,0:T(8,128)S(1)} fusion(pred[2,64,64]{2,1,0:T(8,128)(4,1)S(1)} %get-tuple-element.45, f32[2,64,16,128]{3,2,1,0:T(8,128)S(1)} %bitcast.241, f32[2,64,16]{1,2,0:T(8,128)S(1)} %copy.185, f32[2,64,16,128]{3,2,1,0:T(8,128)S(1)} %fusion.88, f32[2,64,16,128]{3,2,1,0:T(8,128)S(1)} %bitcast.240, ...), kind=kOutput, calls=%fused_computation.70 | convolution fusion | flops 202768384 | bytes 3694592 | tf_op jit(solution)/shard_map/vmap(thk,shk->hts)/dot_general | solution.py:90
  84.9 3.1 %convolution_bitcast_fusion.9 = f32[1,16,64,128]{3,2,1,0:T(8,128)} fusion(f32[2,16,128,128]{3,2,1,0:T(8,128)S(1)} %copy-done.1, f32[2,16,64,128]{3,2,1,0:T(8,128)} %copy-done.9), kind=kOutput, calls=%fused_computation.79 | convolution fusion | flops 201326592 | bytes 2097152 | tf_op jit(solution)/shard_map/htk,hkj->htj/dot_general | solution.py:170
  87.9 4.0 %fusion.48 = f32[1,16,64,128]{3,2,1,0:T(8,128)} fusion(f32[2,16,128,128]{2,3,1,0:T(8,128)S(1)} %copy-done.8, f32[2,16,64,128]{3,2,1,0:T(8,128)S(1)} %copy-done.19, f32[2,16,64,128]{3,2,1,0:T(8,128)} %copy-done.9), kind=kOutput, calls=%fused_computation.77 | convolution fusion | flops 201457664 | bytes 2621440 | tf_op jit(solution)/shard_map/cor,crm->com/dot_general | solution.py:171
  93.7 18.1 %all-gather.2.cloned.1.call-done = bf16[4096,576]{0,1:T(8,128)(2,1)} async-done(((bf16[128,576]{0,1:T(8,128)(2,1)}), bf16[4096,576]{0,1:T(8,128)(2,1)}) %all-gather.2.cloned.1.call-update) | async-done | bytes 4718608 | tf_op jit(solution)/shard_map/all_gather | solution.py:269
  113.7 2.9 %convolution_convert_fusion.6 = bf16[2176,512]{0,1:T(8,128)(2,1)S(1)} fusion(bf16[2176,576]{0,1:T(8,128)(2,1)S(1)} %constant_dynamic-slice_fusion, bf16[512,2048]{1,0:T(8,128)(2,1)} %param.17), kind=kOutput, calls=%fused_computation.42 | convolution fusion | flops 1141964800 | bytes 4980736 | tf_op jit(solution)/shard_map/dot_general | solution.py:291
  120.2 2.9 %convolution_convert_fusion.7 = bf16[2176,512]{0,1:T(8,128)(2,1)S(1)} fusion(bf16[2176,576]{0,1:T(8,128)(2,1)S(1)} %constant_dynamic-slice_fusion, bf16[512,2048]{1,0:T(8,128)(2,1)} %param.18), kind=kOutput, calls=%fused_computation.43 | convolution fusion | flops 1141964800 | bytes 4980736 | tf_op jit(solution)/shard_map/dot_general | solution.py:300
  124.5 5.3 %fusion.83 = bf16[128,4,128]{0,2,1:T(8,128)(2,1)S(1)} fusion(bf16[2176,4,128]{0,2,1:T(8,128)(2,1)S(1)} %bitcast.265, f32[128,4]{0,1:T(4,128)S(1)} %bitcast.269, f32[4,128,2176]{1,2,0:T(8,128)} %copy-done.15, pred[128,2176]{0,1:T(8,128)(4,1)S(1)} %compare_and_fusion), kind=kOutput, calls=%fused_computation.91 | convolution fusion | flops 288688768 | bytes 7096320 | tf_op jit(solution)/shard_map/hts,shv->thv/dot_general | solution.py:329
  129.8 2.6 fusion.177
  141.9 4.3 %convolution_convert_fusion.5 = bf16[2176,512]{0,1:T(8,128)(2,1)} fusion(bf16[2176,576]{0,1:T(8,128)(2,1)S(1)} %copy-done.11, bf16[512,2048]{1,0:T(8,128)(2,1)} %param.18), kind=kOutput, calls=%fused_computation.41 | convolution fusion | flops 1141964800 | bytes 4980736 | tf_op jit(solution)/shard_map/dot_general | solution.py:300
  148.3 6.6 %fusion.80 = bf16[128,4,128]{0,2,1:T(8,128)(2,1)} fusion(bf16[2176,4,128]{0,2,1:T(8,128)(2,1)} %bitcast.266, f32[128,4]{0,1:T(4,128)} %bitcast.270, f32[4,128,2176]{1,2,0:T(8,128)} %copy-done.16, pred[128,2176]{0,1:T(8,128)(4,1)S(1)} %compare_and_fusion), kind=kOutput, calls=%fused_computation.90 | convolution fusion | flops 288688768 | bytes 7096320 | tf_op jit(solution)/shard_map/hts,shv->thv/dot_general | solution.py:329
  154.8 7.6 %collective-permute-done.1 = bf16[16,128,256]{1,2,0:T(8,128)(2,1)} collective-permute-done((bf16[16,128,256]{1,2,0:T(8,128)(2,1)}, bf16[16,128,256]{1,2,0:T(8,128)(2,1)}, u32[]{:S(2)}, u32[]{:S(2)}) %collective-permute-start.1) | collective-permute-done | bytes 1048608 | tf_op jit(solution)/shard_map/ppermute | solution.py:42
  175.2 4.3 %convolution_convert_fusion.3 = bf16[2176,512]{0,1:T(8,128)(2,1)} fusion(bf16[2176,576]{0,1:T(8,128)(2,1)S(1)} %copy-done.12, bf16[512,2048]{1,0:T(8,128)(2,1)} %param.18), kind=kOutput, calls=%fused_computation.39 | convolution fusion | flops 1141964800 | bytes 4980736 | tf_op jit(solution)/shard_map/dot_general | solution.py:300
  181.6 6.6 %fusion.77 = bf16[128,4,128]{0,2,1:T(8,128)(2,1)} fusion(bf16[2176,4,128]{0,2,1:T(8,128)(2,1)} %bitcast.267, f32[128,4]{0,1:T(4,128)} %bitcast.271, f32[4,128,2176]{1,2,0:T(8,128)} %copy-done.17, pred[128,2176]{0,1:T(8,128)(4,1)S(1)} %compare_and_fusion), kind=kOutput, calls=%fused_computation.89 | convolution fusion | flops 288688768 | bytes 7096320 | tf_op jit(solution)/shard_map/hts,shv->thv/dot_general | solution.py:329
  188.2 4.2 %collective-permute-done.2 = bf16[16,128,256]{1,2,0:T(8,128)(2,1)} collective-permute-done((bf16[16,128,256]{1,2,0:T(8,128)(2,1)}, bf16[16,128,256]{1,2,0:T(8,128)(2,1)}, u32[]{:S(2)}, u32[]{:S(2)}) %collective-permute-start.2) | collective-permute-done | bytes 1048608 | tf_op jit(solution)/shard_map/ppermute | solution.py:42
  209.0 3.9 %convolution_convert_fusion.1 = bf16[2176,512]{0,1:T(8,128)(2,1)} fusion(bf16[2176,576]{0,1:T(8,128)(2,1)S(1)} %copy-done.13, bf16[512,2048]{1,0:T(8,128)(2,1)} %param.18), kind=kOutput, calls=%fused_computation.37 | convolution fusion | flops 1141964800 | bytes 4980736 | tf_op jit(solution)/shard_map/dot_general | solution.py:300
  212.9 5.9 %fusion.74 = bf16[128,4,128]{0,2,1:T(8,128)(2,1)S(1)} fusion(bf16[2176,4,128]{0,2,1:T(8,128)(2,1)} %bitcast.264, f32[128,4]{0,1:T(4,128)S(1)} %bitcast.268, f32[4,128,2176]{1,2,0:T(8,128)} %copy-done.14, pred[128,2176]{0,1:T(8,128)(4,1)S(1)} %compare_and_fusion), kind=kOutput, calls=%fused_computation.88 | convolution fusion | flops 288688768 | bytes 7096320 | tf_op jit(solution)/shard_map/hts,shv->thv/dot_general | solution.py:329
  218.8 44.4 %collective-permute-done.4 = bf16[16,128,128]{1,2,0:T(8,128)(2,1)S(1)} collective-permute-done((bf16[16,128,128]{1,2,0:T(8,128)(2,1)}, bf16[16,128,128]{1,2,0:T(8,128)(2,1)S(1)}, u32[]{:S(2)}, u32[]{:S(2)}) %collective-permute-start.4) | collective-permute-done | bytes 524320 | tf_op jit(solution)/shard_map/ppermute | solution.py:42
  (166 shorter events, 96.8 us)
Async XLA Ops:
  7.2 104.6 %all-gather.2.cloned.1.call-start = ((), (), s32[]{:S(2)}) async-start(), calls=%async_computation | async-start | bytes 4866048 | tf_op jit(solution)/shard_map/all_gather | solution.py:269
  12.8 4.4 %copy-start.27 = (f32[128,16]{0,1:T(8,128)S(1)}, f32[128,16]{0,1:T(8,128)}, u32[]{:S(2)}) copy-start(f32[128,16]{0,1:T(8,128)} %param.14) | copy-start | bytes 24580
  33.8 11.8 %copy-start.20 = (f32[16,8,16,128]{3,2,1,0:T(8,128)S(1)}, f32[16,8,16,128]{3,2,1,0:T(8,128)}, u32[]{:S(2)}) copy-start(f32[16,8,16,128]{3,2,1,0:T(8,128)} %copy.263) | copy-start | bytes 3145732
  49.0 4.7 %copy-start.5 = (f32[2,16,64,128]{3,2,1,0:T(8,128)}, f32[2,16,64,128]{3,2,1,0:T(8,128)S(1)}, u32[]{:S(2)}) copy-start(f32[2,16,64,128]{3,2,1,0:T(8,128)S(1)} %fusion.94) | copy-start | bytes 3145732
  53.7 7.1 %copy-start = (f32[2,16,128,128]{3,2,1,0:T(8,128)}, f32[2,16,128,128]{3,2,1,0:T(8,128)S(1)}, u32[]{:S(2)}) copy-start(f32[2,16,128,128]{3,2,1,0:T(8,128)S(1)} %multiply_subtract_fusion) | copy-start | bytes 6291460
  60.8 4.6 %copy-start.7 = (f32[2,16,128,128]{2,3,1,0:T(8,128)}, f32[2,16,128,128]{2,3,1,0:T(8,128)S(1)}, u32[]{:S(2)}) copy-start(f32[2,16,128,128]{2,3,1,0:T(8,128)S(1)} %fusion.146) | copy-start | bytes 6291460
  65.4 64.4 %collective-permute-start = (bf16[16,128,256]{1,2,0:T(8,128)(2,1)}, bf16[16,128,256]{1,2,0:T(8,128)(2,1)}, u32[]{:S(2)}, u32[]{:S(2)}) collective-permute-start(bf16[16,128,256]{1,2,0:T(8,128)(2,1)} %pad_maximum_fusion), channel_id=1, source_target_pairs={{0,8},{8,16},{16,24},{24,32},{32,40},{40,48},{48,56},{56,64},{64,7... | collective-permute-start | bytes 3145736 | tf_op jit(solution)/shard_map/ppermute | solution.py:42
  113.7 6.4 %copy-start.10 = (bf16[2176,576]{0,1:T(8,128)(2,1)}, bf16[2176,576]{0,1:T(8,128)(2,1)S(1)}, u32[]{:S(2)}) copy-start(bf16[2176,576]{0,1:T(8,128)(2,1)S(1)} %constant_dynamic-slice_fusion) | copy-start | bytes 7520260
  132.6 3.3 %copy-start.11 = (bf16[2176,576]{0,1:T(8,128)(2,1)S(1)}, bf16[2176,576]{0,1:T(8,128)(2,1)}, u32[]{:S(2)}) copy-start(bf16[2176,576]{0,1:T(8,128)(2,1)} %copy-done.10) | copy-start | bytes 7520260
  133.8 28.7 %collective-permute-start.1 = (bf16[16,128,256]{1,2,0:T(8,128)(2,1)}, bf16[16,128,256]{1,2,0:T(8,128)(2,1)}, u32[]{:S(2)}, u32[]{:S(2)}) collective-permute-start(bf16[16,128,256]{1,2,0:T(8,128)(2,1)} %pad_maximum_fusion.1), channel_id=1, source_target_pairs={{0,16},{8,24},{16,32},{24,40},{32,48},{40,56},{48,64},{56,72},{64,... | collective-permute-start | bytes 3145736 | tf_op jit(solution)/shard_map/ppermute | solution.py:42
  141.9 4.4 %copy-start.16 = (f32[4,128,2176]{1,2,0:T(8,128)}, f32[4,128,2176]{1,2,0:T(8,128)S(1)}, u32[]{:S(2)}) copy-start(f32[4,128,2176]{1,2,0:T(8,128)S(1)} %fusion.24) | copy-start | bytes 13369348
  164.8 4.4 %copy-start.12 = (bf16[2176,576]{0,1:T(8,128)(2,1)S(1)}, bf16[2176,576]{0,1:T(8,128)(2,1)}, u32[]{:S(2)}) copy-start(bf16[2176,576]{0,1:T(8,128)(2,1)} %copy-done.10) | copy-start | bytes 7520260
  167.0 25.3 %collective-permute-start.2 = (bf16[16,128,256]{1,2,0:T(8,128)(2,1)}, bf16[16,128,256]{1,2,0:T(8,128)(2,1)}, u32[]{:S(2)}, u32[]{:S(2)}) collective-permute-start(bf16[16,128,256]{1,2,0:T(8,128)(2,1)} %pad_maximum_fusion.2), channel_id=1, source_target_pairs={{0,32},{8,40},{16,48},{24,56},{32,64},{40,72},{48,80},{56,88},{64,... | collective-permute-start | bytes 3145736 | tf_op jit(solution)/shard_map/ppermute | solution.py:42
  175.2 4.4 %copy-start.17 = (f32[4,128,2176]{1,2,0:T(8,128)}, f32[4,128,2176]{1,2,0:T(8,128)S(1)}, u32[]{:S(2)}) copy-start(f32[4,128,2176]{1,2,0:T(8,128)S(1)} %fusion.21) | copy-start | bytes 13369348
  188.2 6.8 %copy-start.4 = (f32[16,128,256]{1,2,0:T(8,128)S(1)}, f32[16,128,256]{1,2,0:T(8,128)}, u32[]{:S(2)}) copy-start(f32[16,128,256]{1,2,0:T(8,128)} %copy-done.3) | copy-start | bytes 6291460
  196.0 4.9 %copy-start.13 = (bf16[2176,576]{0,1:T(8,128)(2,1)S(1)}, bf16[2176,576]{0,1:T(8,128)(2,1)}, u32[]{:S(2)}) copy-start(bf16[2176,576]{0,1:T(8,128)(2,1)} %copy-done.10) | copy-start | bytes 7520260
  197.4 65.8 %collective-permute-start.3 = (bf16[16,128,256]{1,2,0:T(8,128)(2,1)S(1)}, bf16[16,128,256]{1,2,0:T(8,128)(2,1)S(1)}, u32[]{:S(2)}, u32[]{:S(2)}) collective-permute-start(bf16[16,128,256]{1,2,0:T(8,128)(2,1)S(1)} %pad_maximum_fusion.3), channel_id=1, source_target_pairs={{0,8},{8,16},{16,24},{24,32},{32,40},{40,48},{48,56},{56,64},{64,7... | collective-permute-start | bytes 3145736 | tf_op jit(solution)/shard_map/ppermute | solution.py:42
  199.4 63.9 %collective-permute-start.4 = (bf16[16,128,128]{1,2,0:T(8,128)(2,1)}, bf16[16,128,128]{1,2,0:T(8,128)(2,1)S(1)}, u32[]{:S(2)}, u32[]{:S(2)}) collective-permute-start(bf16[16,128,128]{1,2,0:T(8,128)(2,1)} %fusion.90), channel_id=1, source_target_pairs={{0,72},{8,80},{16,88},{24,96},{32,104},{40,112},{48,120},{56,128},... | collective-permute-start | bytes 1572872 | tf_op jit(solution)/shard_map/ppermute | solution.py:42
  218.8 44.8 %slice-start = ((f32[2,16,64,128]{3,2,1,0:T(8,128)}), f32[1,16,64,128]{3,2,1,0:T(8,128)S(1)}, s32[]{:S(2)}) async-start(f32[2,16,64,128]{3,2,1,0:T(8,128)} %copy-done.9), calls=%async_computation.1 | async-start | bytes 1048576 | tf_op jit(solution)/shard_map/slice | solution.py:187
  218.8 44.8 %slice-start.1 = ((f32[2,16,64,128]{3,2,1,0:T(8,128)}), f32[1,16,64,128]{3,2,1,0:T(8,128)S(1)}, s32[]{:S(2)}) async-start(f32[2,16,64,128]{3,2,1,0:T(8,128)} %copy-done.18), calls=%async_computation.2 | async-start | bytes 1048576 | tf_op jit(solution)/shard_map/slice | solution.py:187
  218.8 44.8 %copy-start.23 = (f32[1,16,64,128]{3,2,1,0:T(8,128)S(1)}, f32[1,16,64,128]{3,2,1,0:T(8,128)}, u32[]{:S(2)}) copy-start(f32[1,16,64,128]{3,2,1,0:T(8,128)} %fusion.48) | copy-start | bytes 1572868
  218.8 44.8 %copy-start.24 = (f32[1,16,64,128]{3,2,1,0:T(8,128)S(1)}, f32[1,16,64,128]{3,2,1,0:T(8,128)}, u32[]{:S(2)}) copy-start(f32[1,16,64,128]{3,2,1,0:T(8,128)} %convolution_bitcast_fusion.9) | copy-start | bytes 1572868
  263.6 3.6 %copy-start.25 = (bf16[128,4,128]{0,2,1:T(8,128)(2,1)S(1)}, bf16[128,4,128]{0,2,1:T(8,128)(2,1)}, u32[]{:S(2)}) copy-start(bf16[128,4,128]{0,2,1:T(8,128)(2,1)} %fusion.80) | copy-start | bytes 393220
  263.6 3.6 %copy-start.26 = (bf16[128,4,128]{0,2,1:T(8,128)(2,1)S(1)}, bf16[128,4,128]{0,2,1:T(8,128)(2,1)}, u32[]{:S(2)}) copy-start(bf16[128,4,128]{0,2,1:T(8,128)(2,1)} %fusion.77) | copy-start | bytes 393220
  (13 other events, 28.3 us)
Sparse Core Ops, SparseCore 0:
  10.5 101.2 all-gather.1

commit v4 on v3

--- a/solution.py
+++ b/solution.py
@@ -217,7 +217,7 @@
 
 def carry_rounds(slab_rows):
     window = window_slabs_of(slab_rows)
-    distance, rounds = 1, 1
+    distance, rounds = 1, 2
     while 2 * distance < window:
         distance, rounds = 2 * distance, rounds + 1
     return rounds
@@ -229,17 +229,16 @@
     rounds = carry_rounds(slab_rows)
     groups_at = [[] for _ in range(rounds)]
     for group in range(group_count):
-        groups_at[group * rounds // group_count].append(group)
+        groups_at[rounds - group_count + group if rounds > group_count else group * rounds // group_count].append(group)
     parts = []
 
-    def exchange(values, distances, step):
-        sent = tuple(v.astype(jnp.bfloat16) for v in values)
-        sent = lax.optimization_barrier(sent)
-        got = tuple(shifted(v, "ctx", d) for v, d in zip(sent, distances))
-        done = [attend_group(group, sent[0]) for group in groups_at[step]]
+    def exchange(value, distance, step):
+        sent = lax.optimization_barrier(value.astype(jnp.bfloat16))
+        got = shifted(sent, "ctx", distance)
+        done = [attend_group(group, sent) for group in groups_at[step]]
         got, done = lax.optimization_barrier((got, done))
         parts.extend(done)
-        return tuple(v.astype(jnp.float32) for v in got)
+        return got.astype(jnp.float32)
 
     def product(left, right):
         return jnp.einsum("hkj,hjl->hkl", left, right, precision=PRECISE_PRODUCT)
@@ -247,15 +246,13 @@
     value_dim = add_now.shape[2]
     distance, step = 1, 0
     while 2 * distance < window:
-        (before,) = exchange((jnp.concatenate([add_now, map_now], axis=2),), (distance,), step)
+        before = exchange(jnp.concatenate([add_now, map_now], axis=2), distance, step)
         joined = product(map_now, before)
         add_now = joined[:, :, :value_dim] + add_now
         map_now = joined[:, :, value_dim:]
         distance, step = 2 * distance, step + 1
-    last, add_far = exchange(
-        (jnp.concatenate([add_now, map_now], axis=2), add_now), (1, distance + 1), step
-    )
-    return product(last[:, :, value_dim:], add_far) + last[:, :, :value_dim], parts
+    add_now = product(map_now, exchange(add_now, distance, step)) + add_now
+    return exchange(add_now, 1, step + 1), parts
 
 
 def latent_attention(

time: 280 us -> 247 us (0.88)
  the two profiles are of different devices: /device:TPU:200 before, /device:TPU:4 now
where the time goes in v4:
time: 247 us; the launch traced here: 242 us
  matrix products  122 us (49%)
  waiting for transfers between devices  29.4 us (12%)
  starting transfers between devices  28.1 us (11%)
  other arithmetic  26.4 us (11%)
  local copies, waits for them, and re-layouts  20.8 us (8%)
  between operations  15.1 us (6%)
    ppermute x5, starting transfers between devices, shifted(): return lax.ppermute(block, axis, route)  28.1 us
    dot_general x4, matrix products, attend_group(): jnp.einsum('hts,shv->thv', weights.astype(jnp.bfloat16), values, preferre...  25.3 us
    ppermute x5, waiting for transfers between devices, shifted(): return lax.ppermute(block, axis, route)  24.1 us
    dot_general x4, matrix products, attend_group(): jnp.dot(latent_part, value_up[:, group * per_group * value_width:(group +...  16.5 us
    unnamed x68, local copies, waits for them, and re-layouts  14.2 us
    dot_general x4, matrix products, product(): return jnp.einsum('hkj,hjl->hkl', left, right, precision=PRECISE_PRODUCT)  10.6 us
    dot_general x4, matrix products, attend_group(): jnp.dot(latent_part, key_up[:, group * per_group * NOPE:(group + 1) * per...  10.4 us
    sub x4, other arithmetic, attend_group(): weights = jnp.where(allowed[None], jnp.exp(masked - row_max), 0.0)  7.39 us
  transfers between devices with their start and end apart: 6, of which 3 were waited for; matrix products, arithmetic and copies ran while one was open for 61% of the time, Pallas kernels for 0%

profile of v4, /device:TPU:4, one launch (start us, length us, event | category | flops | bytes accessed | tf_op | source)
XLA Modules:
  0.0 242.1 jit_solution(10032510007553559726)
XLA Ops:
  19.6 3.4 %fusion.45 = f32[2,16,64,64]{3,2,1,0:T(8,128)S(1)} fusion(f32[2,16,64]{2,1,0:T(8,128)S(1)} %get-tuple-element.39, pred[2,64,64]{2,1,0:T(8,128)(4,1)S(1)} %get-tuple-element.44, f32[2,64,16,128]{3,2,1,0:T(8,128)S(1)} %bitcast.236, f32[2,64,16]{1,2,0:T(8,128)S(1)} %copy.187, f32[2,64,16,128]{3,2,1,0:T(8,128)S(1)} %fusion.88), kind=kOutput, calls=%fused_computation.68 | convolution fusion | flops 202899456 | bytes 2646016 | tf_op jit(solution)/shard_map/vmap(thk,shk->hts)/dot_general | solution.py:79
  39.9 4.7 %multiply_subtract_fusion = f32[2,16,128,128]{3,2,1,0:T(8,128)S(1)} fusion(f32[2,16,64,128]{3,2,1,0:T(8,128)S(1)} %fusion.94, f32[128,128]{1,0:T(8,128)S(1)} %fusion.151, f32[2,16,128]{2,1,0:T(8,128)S(1)} %bitcast.262, f32[2]{0:T(128)S(1)} %slice_reduce_fusion, f32[2,64,16,128]{3,2,1,0:T(8,128)S(1)} %fusion.88, f32[2,64,16,128]{3,2,1,0:T(8,128)S(1)} %bitcast.238, ...), kind=kOutput, calls=%fused_computation.52 | convolution fusion | flops 405274624 | bytes 5349896 | tf_op jit(solution)/shard_map/vmap(shk,hsj->hkj)/dot_general | solution.py:103
  44.6 2.9 %fusion.167 = (bf16[16,128,128]{1,2,0:T(8,128)(2,1)S(1)}, f32[16,128,128]{1,2,0:T(8,128)}) fusion(f32[2,16,128,128]{3,2,1,0:T(8,128)S(1)} %multiply_subtract_fusion), kind=kOutput, calls=%fused_computation.219 | convolution fusion | flops 402915328 | bytes 3670016 | tf_op jit(solution)/shard_map/hkj,hjl->hkl/dot_general | solution.py:174
  47.5 4.2 %fusion.146 = f32[2,16,128,128]{2,3,1,0:T(8,128)S(1)} fusion(f32[2,16,64,128]{3,2,1,0:T(8,128)S(1)} %fusion.96, f32[2,64,16,128]{3,2,1,0:T(8,128)S(1)} %fusion.88, f32[2,64,16,128]{3,2,1,0:T(8,128)S(1)} %bitcast.239, f32[2,64]{1,0:T(2,128)S(1)} %get-tuple-element.42, f32[2,16,128]{2,1,0:T(8,128)S(1)} %slice_bitcast_fusion.14, f32[2,64,16]{1,2,0:T(8,128)S(1)} %copy.187), kind=kOutput, calls=%fused_computation.175 | convolution fusion | flops 403701760 | bytes 5267968 | tf_op jit(solution)/shard_map/vmap(omt,mor->mtr)/dot_general | solution.py:106
  55.3 3.1 %collective-permute-start = (bf16[16,128,256]{1,2,0:T(8,128)(2,1)}, bf16[16,128,256]{1,2,0:T(8,128)(2,1)}, u32[]{:S(2)}, u32[]{:S(2)}) collective-permute-start(bf16[16,128,256]{1,2,0:T(8,128)(2,1)} %pad_maximum_fusion), channel_id=1, source_target_pairs={{0,8},{8,16},{16,24},{24,32},{32,40},{40,48},{48,56},{56,64},{64,7... | collective-permute-start | bytes 3145736 | tf_op jit(solution)/shard_map/ppermute | solution.py:42
  63.9 2.9 %convolution_select_fusion.1 = f32[2,16,64,64]{3,2,1,0:T(8,128)S(1)} fusion(pred[2,64,64]{2,1,0:T(8,128)(4,1)S(1)} %get-tuple-element.43, f32[2,64,16,128]{3,2,1,0:T(8,128)S(1)} %bitcast.241, f32[2,64,16]{1,2,0:T(8,128)S(1)} %copy.183, f32[2,64,16,128]{3,2,1,0:T(8,128)S(1)} %fusion.88, f32[2,64,16,128]{3,2,1,0:T(8,128)S(1)} %bitcast.240, ...), kind=kOutput, calls=%fused_computation.69 | convolution fusion | flops 202768384 | bytes 3694592 | tf_op jit(solution)/shard_map/vmap(thk,shk->hts)/dot_general | solution.py:90
  72.0 2.9 %fusion.48 = f32[1,16,64,128]{3,2,1,0:T(8,128)} fusion(f32[2,16,128,128]{2,3,1,0:T(8,128)S(1)} %copy-done.8, f32[2,16,64,128]{3,2,1,0:T(8,128)S(1)} %fusion.178, f32[2,16,64,128]{3,2,1,0:T(8,128)S(1)} %convolution_subtract_fusion), kind=kOutput, calls=%fused_computation.77 | convolution fusion | flops 201457664 | bytes 2621440 | tf_op jit(solution)/shard_map/cor,crm->com/dot_general | solution.py:171
  78.8 22.3 %collective-permute-done = bf16[16,128,256]{1,2,0:T(8,128)(2,1)} collective-permute-done((bf16[16,128,256]{1,2,0:T(8,128)(2,1)}, bf16[16,128,256]{1,2,0:T(8,128)(2,1)}, u32[]{:S(2)}, u32[]{:S(2)}) %collective-permute-start) | collective-permute-done | bytes 1048608 | tf_op jit(solution)/shard_map/ppermute | solution.py:42
  107.2 4.6 %all-gather.2.cloned.1.call-done = bf16[4096,576]{0,1:T(8,128)(2,1)} async-done(((bf16[128,576]{0,1:T(8,128)(2,1)}), bf16[4096,576]{0,1:T(8,128)(2,1)}) %all-gather.2.cloned.1.call-update) | async-done | bytes 4718608 | tf_op jit(solution)/shard_map/all_gather | solution.py:266
  113.8 2.9 %convolution_convert_fusion.6 = bf16[2176,512]{0,1:T(8,128)(2,1)S(1)} fusion(bf16[2176,576]{0,1:T(8,128)(2,1)S(1)} %constant_dynamic-slice_fusion, bf16[512,2048]{1,0:T(8,128)(2,1)} %param.17), kind=kOutput, calls=%fused_computation.42 | convolution fusion | flops 1141964800 | bytes 4980736 | tf_op jit(solution)/shard_map/dot_general | solution.py:288
  120.2 4.3 %convolution_convert_fusion.7 = bf16[2176,512]{0,1:T(8,128)(2,1)} fusion(bf16[2176,576]{0,1:T(8,128)(2,1)S(1)} %constant_dynamic-slice_fusion, bf16[512,2048]{1,0:T(8,128)(2,1)} %param.18), kind=kOutput, calls=%fused_computation.43 | convolution fusion | flops 1141964800 | bytes 4980736 | tf_op jit(solution)/shard_map/dot_general | solution.py:297
  126.5 5.9 %fusion.83 = bf16[128,4,128]{0,2,1:T(8,128)(2,1)S(1)} fusion(bf16[2176,4,128]{0,2,1:T(8,128)(2,1)} %bitcast.265, f32[128,4]{0,1:T(4,128)} %bitcast.269, f32[4,128,2176]{1,2,0:T(8,128)} %copy-done.17, pred[128,2176]{0,1:T(8,128)(4,1)S(1)} %compare_and_fusion), kind=kOutput, calls=%fused_computation.91 | convolution fusion | flops 288688768 | bytes 7096320 | tf_op jit(solution)/shard_map/hts,shv->thv/dot_general | solution.py:326
  137.1 2.9 %collective-permute-start.2 = (bf16[16,128,256]{1,2,0:T(8,128)(2,1)}, bf16[16,128,256]{1,2,0:T(8,128)(2,1)}, u32[]{:S(2)}, u32[]{:S(2)}) collective-permute-start(bf16[16,128,256]{1,2,0:T(8,128)(2,1)} %pad_maximum_fusion.2), channel_id=1, source_target_pairs={{0,32},{8,40},{16,48},{24,56},{32,64},{40,72},{48,80},{56,88},{64,... | collective-permute-start | bytes 3145736 | tf_op jit(solution)/shard_map/ppermute | solution.py:42
  146.0 4.3 %convolution_convert_fusion.5 = bf16[2176,512]{0,1:T(8,128)(2,1)} fusion(bf16[2176,576]{0,1:T(8,128)(2,1)S(1)} %copy-done.13, bf16[512,2048]{1,0:T(8,128)(2,1)} %param.18), kind=kOutput, calls=%fused_computation.41 | convolution fusion | flops 1141964800 | bytes 4980736 | tf_op jit(solution)/shard_map/dot_general | solution.py:297
  152.4 6.6 %fusion.80 = bf16[128,4,128]{0,2,1:T(8,128)(2,1)} fusion(bf16[2176,4,128]{0,2,1:T(8,128)(2,1)} %bitcast.266, f32[128,4]{0,1:T(4,128)} %bitcast.270, f32[4,128,2176]{1,2,0:T(8,128)} %copy-done.18, pred[128,2176]{0,1:T(8,128)(4,1)S(1)} %compare_and_fusion), kind=kOutput, calls=%fused_computation.90 | convolution fusion | flops 288688768 | bytes 7096320 | tf_op jit(solution)/shard_map/hts,shv->thv/dot_general | solution.py:326
  160.8 2.6 %fusion.110 = f32[16,128,256]{2,1,0:T(8,128)S(1)} fusion(bf16[16,128,256]{1,2,0:T(8,128)(2,1)} %collective-permute-done.2, f32[16,128,256]{1,2,0:T(8,128)} %copy-done.2), kind=kOutput, calls=%fused_computation.133 | convolution fusion | flops 805306368 | bytes 4194304 | tf_op jit(solution)/shard_map/hkj,hjl->hkl/dot_general | solution.py:244
  168.4 3.1 %fusion.165 = (bf16[16,128,128]{1,2,0:T(8,128)(2,1)}, f32[16,128,128]{1,2,0:T(8,128)}) fusion(f32[16,128,128]{1,2,0:T(8,128)} %copy.250, f32[16,128,128]{1,2,0:T(8,128)S(1)} %get-tuple-element.48, f32[16,128,256]{1,2,0:T(8,128)S(1)} %fusion.179, f32[16,128,256]{1,2,0:T(8,128)} %copy-done.2), kind=kLoop, calls=%fused_computation.218 | loop fusion | flops 1048576 | bytes 5767168 | tf_op jit(solution)/shard_map/convert_element_type | solution.py:236
  171.5 6.7 %collective-permute-start.3 = (bf16[16,128,128]{1,2,0:T(8,128)(2,1)}, bf16[16,128,128]{1,2,0:T(8,128)(2,1)}, u32[]{:S(2)}, u32[]{:S(2)}) collective-permute-start(bf16[16,128,128]{1,2,0:T(8,128)(2,1)} %get-tuple-element.36), channel_id=1, source_target_pairs={{0,64},{8,72},{16,80},{24,88},{32,96},{40,104},{48,112},{56,120},{... | collective-permute-start | bytes 1572872 | tf_op jit(solution)/shard_map/ppermute | solution.py:42
  186.3 3.9 %convolution_convert_fusion.3 = bf16[2176,512]{0,1:T(8,128)(2,1)} fusion(bf16[2176,576]{0,1:T(8,128)(2,1)S(1)} %copy-done.14, bf16[512,2048]{1,0:T(8,128)(2,1)} %param.18), kind=kOutput, calls=%fused_computation.39 | convolution fusion | flops 1141964800 | bytes 4980736 | tf_op jit(solution)/shard_map/dot_general | solution.py:297
  190.3 6.7 %fusion.77 = bf16[128,4,128]{0,2,1:T(8,128)(2,1)} fusion(bf16[2176,4,128]{0,2,1:T(8,128)(2,1)} %bitcast.267, f32[128,4]{0,1:T(4,128)} %bitcast.271, f32[4,128,2176]{1,2,0:T(8,128)} %copy-done.19, pred[128,2176]{0,1:T(8,128)(4,1)S(1)} %compare_and_fusion), kind=kOutput, calls=%fused_computation.89 | convolution fusion | flops 288688768 | bytes 7096320 | tf_op jit(solution)/shard_map/hts,shv->thv/dot_general | solution.py:326
  197.0 3.2 %fusion.47 = bf16[16,128,128]{1,2,0:T(8,128)(2,1)} fusion(f32[16,128,128]{1,2,0:T(8,128)S(1)} %copy-done.21, bf16[16,128,128]{1,2,0:T(8,128)(2,1)} %collective-permute-done.3, f32[16,128,256]{2,1,0:T(8,128)S(1)} %copy-done.10), kind=kOutput, calls=%fused_computation.75 | convolution fusion | flops 403177472 | bytes 3145728 | tf_op jit(solution)/shard_map/hkj,hjl->hkl/dot_general | solution.py:244
  200.2 13.1 %collective-permute-start.4 = (bf16[16,128,128]{1,2,0:T(8,128)(2,1)}, bf16[16,128,128]{1,2,0:T(8,128)(2,1)S(1)}, u32[]{:S(2)}, u32[]{:S(2)}) collective-permute-start(bf16[16,128,128]{1,2,0:T(8,128)(2,1)} %fusion.47), channel_id=1, source_target_pairs={{0,8},{8,16},{16,24},{24,32},{32,40},{40,48},{48,56},{56,64},{64,7... | collective-permute-start | bytes 1572872 | tf_op jit(solution)/shard_map/ppermute | solution.py:42
  221.4 3.9 %convolution_convert_fusion.1 = bf16[2176,512]{0,1:T(8,128)(2,1)} fusion(bf16[2176,576]{0,1:T(8,128)(2,1)S(1)} %copy-done.15, bf16[512,2048]{1,0:T(8,128)(2,1)} %param.18), kind=kOutput, calls=%fused_computation.37 | convolution fusion | flops 1141964800 | bytes 4980736 | tf_op jit(solution)/shard_map/dot_general | solution.py:297
  225.3 6.1 %fusion.74 = bf16[128,4,128]{0,2,1:T(8,128)(2,1)S(1)} fusion(bf16[2176,4,128]{0,2,1:T(8,128)(2,1)} %bitcast.264, f32[128,4]{0,1:T(4,128)S(1)} %bitcast.268, f32[4,128,2176]{1,2,0:T(8,128)} %copy-done.16, pred[128,2176]{0,1:T(8,128)(4,1)S(1)} %compare_and_fusion), kind=kOutput, calls=%fused_computation.88 | convolution fusion | flops 288688768 | bytes 7096320 | tf_op jit(solution)/shard_map/hts,shv->thv/dot_general | solution.py:326
  (166 shorter events, 99.5 us)
Async XLA Ops:
  7.2 4.9 %copy-start.27 = (f32[128,16]{0,1:T(8,128)S(1)}, f32[128,16]{0,1:T(8,128)}, u32[]{:S(2)}) copy-start(f32[128,16]{0,1:T(8,128)} %param.14) | copy-start | bytes 24580
  7.2 5.0 %copy-start.24 = (bf16[128,2048]{1,0:T(8,128)(2,1)S(1)}, bf16[128,2048]{1,0:T(8,128)(2,1)}, u32[]{:S(2)}) copy-start(bf16[128,2048]{1,0:T(8,128)(2,1)} %param.12) | copy-start | bytes 1572868
  7.2 104.7 %all-gather.2.cloned.1.call-start = ((), (), s32[]{:S(2)}) async-start(), calls=%async_computation | async-start | bytes 4866048 | tf_op jit(solution)/shard_map/all_gather | solution.py:266
  38.0 9.6 %copy-start.3 = (f32[2,16,64,128]{3,2,1,0:T(8,128)}, f32[2,16,64,128]{3,2,1,0:T(8,128)S(1)}, u32[]{:S(2)}) copy-start(f32[2,16,64,128]{3,2,1,0:T(8,128)S(1)} %fusion.96) | copy-start | bytes 3145732
  39.9 4.7 %copy-start.5 = (f32[2,16,64,128]{3,2,1,0:T(8,128)}, f32[2,16,64,128]{3,2,1,0:T(8,128)S(1)}, u32[]{:S(2)}) copy-start(f32[2,16,64,128]{3,2,1,0:T(8,128)S(1)} %fusion.94) | copy-start | bytes 3145732
  44.6 7.1 %copy-start = (f32[2,16,128,128]{3,2,1,0:T(8,128)}, f32[2,16,128,128]{3,2,1,0:T(8,128)S(1)}, u32[]{:S(2)}) copy-start(f32[2,16,128,128]{3,2,1,0:T(8,128)S(1)} %multiply_subtract_fusion) | copy-start | bytes 6291460
  55.3 45.7 %collective-permute-start = (bf16[16,128,256]{1,2,0:T(8,128)(2,1)}, bf16[16,128,256]{1,2,0:T(8,128)(2,1)}, u32[]{:S(2)}, u32[]{:S(2)}) collective-permute-start(bf16[16,128,256]{1,2,0:T(8,128)(2,1)} %pad_maximum_fusion), channel_id=1, source_target_pairs={{0,8},{8,16},{16,24},{24,32},{32,40},{40,48},{48,56},{56,64},{64,7... | collective-permute-start | bytes 3145736 | tf_op jit(solution)/shard_map/ppermute | solution.py:42
  68.9 6.1 %copy-start.11 = (f32[2,16,64,128]{3,2,1,0:T(8,128)}, f32[2,16,64,128]{3,2,1,0:T(8,128)S(1)}, u32[]{:S(2)}) copy-start(f32[2,16,64,128]{3,2,1,0:T(8,128)S(1)} %convolution_subtract_fusion) | copy-start | bytes 3145732
  104.9 27.5 %collective-permute-start.1 = (bf16[16,128,256]{1,2,0:T(8,128)(2,1)}, bf16[16,128,256]{1,2,0:T(8,128)(2,1)}, u32[]{:S(2)}, u32[]{:S(2)}) collective-permute-start(bf16[16,128,256]{1,2,0:T(8,128)(2,1)} %pad_maximum_fusion.1), channel_id=1, source_target_pairs={{0,16},{8,24},{16,32},{24,40},{32,48},{40,56},{48,64},{56,72},{64,... | collective-permute-start | bytes 3145736 | tf_op jit(solution)/shard_map/ppermute | solution.py:42
  113.7 6.4 %copy-start.12 = (bf16[2176,576]{0,1:T(8,128)(2,1)}, bf16[2176,576]{0,1:T(8,128)(2,1)S(1)}, u32[]{:S(2)}) copy-start(bf16[2176,576]{0,1:T(8,128)(2,1)S(1)} %constant_dynamic-slice_fusion) | copy-start | bytes 7520260
  120.2 4.4 %copy-start.17 = (f32[4,128,2176]{1,2,0:T(8,128)}, f32[4,128,2176]{1,2,0:T(8,128)S(1)}, u32[]{:S(2)}) copy-start(f32[4,128,2176]{1,2,0:T(8,128)S(1)} %fusion.27) | copy-start | bytes 13369348
  134.8 5.2 %copy-start.13 = (bf16[2176,576]{0,1:T(8,128)(2,1)S(1)}, bf16[2176,576]{0,1:T(8,128)(2,1)}, u32[]{:S(2)}) copy-start(bf16[2176,576]{0,1:T(8,128)(2,1)} %copy-done.12) | copy-start | bytes 7520260
  137.1 23.7 %collective-permute-start.2 = (bf16[16,128,256]{1,2,0:T(8,128)(2,1)}, bf16[16,128,256]{1,2,0:T(8,128)(2,1)}, u32[]{:S(2)}, u32[]{:S(2)}) collective-permute-start(bf16[16,128,256]{1,2,0:T(8,128)(2,1)} %pad_maximum_fusion.2), channel_id=1, source_target_pairs={{0,32},{8,40},{16,48},{24,56},{32,64},{40,72},{48,80},{56,88},{64,... | collective-permute-start | bytes 3145736 | tf_op jit(solution)/shard_map/ppermute | solution.py:42
  146.0 4.4 %copy-start.18 = (f32[4,128,2176]{1,2,0:T(8,128)}, f32[4,128,2176]{1,2,0:T(8,128)S(1)}, u32[]{:S(2)}) copy-start(f32[4,128,2176]{1,2,0:T(8,128)S(1)} %fusion.24) | copy-start | bytes 13369348
  168.4 9.8 %copy-start.14 = (bf16[2176,576]{0,1:T(8,128)(2,1)S(1)}, bf16[2176,576]{0,1:T(8,128)(2,1)}, u32[]{:S(2)}) copy-start(bf16[2176,576]{0,1:T(8,128)(2,1)} %copy-done.12) | copy-start | bytes 7520260
  171.5 25.4 %collective-permute-start.3 = (bf16[16,128,128]{1,2,0:T(8,128)(2,1)}, bf16[16,128,128]{1,2,0:T(8,128)(2,1)}, u32[]{:S(2)}, u32[]{:S(2)}) collective-permute-start(bf16[16,128,128]{1,2,0:T(8,128)(2,1)} %get-tuple-element.36), channel_id=1, source_target_pairs={{0,64},{8,72},{16,80},{24,88},{32,96},{40,104},{48,112},{56,120},{... | collective-permute-start | bytes 1572872 | tf_op jit(solution)/shard_map/ppermute | solution.py:42
  190.2 6.7 %copy-start.10 = (f32[16,128,256]{2,1,0:T(8,128)S(1)}, f32[16,128,256]{2,1,0:T(8,128)}, u32[]{:S(2)}) copy-start(f32[16,128,256]{2,1,0:T(8,128)} %copy-done.9) | copy-start | bytes 6291460
  190.2 6.7 %copy-start.21 = (f32[16,128,128]{1,2,0:T(8,128)S(1)}, f32[16,128,128]{1,2,0:T(8,128)}, u32[]{:S(2)}) copy-start(f32[16,128,128]{1,2,0:T(8,128)} %get-tuple-element.37) | copy-start | bytes 3145732
  197.0 16.3 %copy-start.15 = (bf16[2176,576]{0,1:T(8,128)(2,1)S(1)}, bf16[2176,576]{0,1:T(8,128)(2,1)}, u32[]{:S(2)}) copy-start(bf16[2176,576]{0,1:T(8,128)(2,1)} %copy-done.12) | copy-start | bytes 7520260
  200.2 31.1 %collective-permute-start.4 = (bf16[16,128,128]{1,2,0:T(8,128)(2,1)}, bf16[16,128,128]{1,2,0:T(8,128)(2,1)S(1)}, u32[]{:S(2)}, u32[]{:S(2)}) collective-permute-start(bf16[16,128,128]{1,2,0:T(8,128)(2,1)} %fusion.47), channel_id=1, source_target_pairs={{0,8},{8,16},{16,24},{24,32},{32,40},{40,48},{48,56},{56,64},{64,7... | collective-permute-start | bytes 1572872 | tf_op jit(solution)/shard_map/ppermute | solution.py:42
  225.3 6.1 %slice-start = ((f32[2,16,64,128]{3,2,1,0:T(8,128)}), f32[1,16,64,128]{3,2,1,0:T(8,128)S(1)}, s32[]{:S(2)}) async-start(f32[2,16,64,128]{3,2,1,0:T(8,128)} %copy-done.11), calls=%async_computation.1 | async-start | bytes 1048576 | tf_op jit(solution)/shard_map/slice | solution.py:187
  225.3 6.1 %slice-start.1 = ((f32[2,16,64,128]{3,2,1,0:T(8,128)}), f32[1,16,64,128]{3,2,1,0:T(8,128)S(1)}, s32[]{:S(2)}) async-start(f32[2,16,64,128]{3,2,1,0:T(8,128)} %copy-done.20), calls=%async_computation.2 | async-start | bytes 1048576 | tf_op jit(solution)/shard_map/slice | solution.py:187
  225.3 6.1 %copy-start.22 = (f32[1,16,64,128]{3,2,1,0:T(8,128)S(1)}, f32[1,16,64,128]{3,2,1,0:T(8,128)}, u32[]{:S(2)}) copy-start(f32[1,16,64,128]{3,2,1,0:T(8,128)} %fusion.48) | copy-start | bytes 1572868
  225.3 6.1 %copy-start.23 = (f32[1,16,64,128]{3,2,1,0:T(8,128)S(1)}, f32[1,16,64,128]{3,2,1,0:T(8,128)}, u32[]{:S(2)}) copy-start(f32[1,16,64,128]{3,2,1,0:T(8,128)} %convolution_bitcast_fusion.9) | copy-start | bytes 1572868
  (13 other events, 32.7 us)
Sparse Core Ops, SparseCore 0:
  10.5 101.3 all-gather.1

commit v5 on v4

--- a/solution.py
+++ b/solution.py
@@ -142,6 +142,18 @@
     keyvec = unit_rows(kda_key.astype(jnp.float32).reshape(slab_rows, head_count, -1))
     valvec = kda_value.astype(jnp.float32).reshape(slab_rows, head_count, -1)
     logarithm_decay = log_decay.astype(jnp.float32).reshape(slab_rows, head_count, -1)
+    held, held_after = latents[None], []
+
+    def next_latents(held, stage):
+        if len(held_after) < len(latent_rounds(slab_rows)):
+            held = latent_round(held, slab_rows, len(held_after))
+            held, stage = lax.optimization_barrier((held, stage))
+            held_after.append(held.shape[0])
+        return held, stage
+
+    held, (query_unit, keyvec, valvec, logarithm_decay) = next_latents(
+        held, (query_unit, keyvec, valvec, logarithm_decay)
+    )
     block_count = slab_rows // BLOCK
     prevdocs = doc_of(first_row + jnp.arange(block_count, dtype=jnp.int32) * BLOCK - 1, doc_starts)
 
@@ -182,6 +194,7 @@
         )
         return ((map_after, increment_later), (eff_now, output_current))
 
+    held, block_outs = next_latents(held, block_outs)
     local_output, query_effective, handed_operator, handed_update = block_outs
     slab_pair = (handed_operator[0], handed_update[0])
     effective_blocks, output_blocks = [query_effective[0]], [local_output[0]]
@@ -194,8 +207,9 @@
         output_blocks.append(output_current)
     effective_everything = jnp.stack(effective_blocks)
     output_everything = jnp.stack(output_blocks)
+    held, slab_pair = next_latents(held, slab_pair)
     attend_group, group_count = latent_attention(
-        mla_query, latents, key_up, value_up, positions, docids, doc_starts, head_count
+        mla_query, held, held_after, key_up, value_up, positions, docids, doc_starts, head_count
     )
     carried_in, mla_parts = incoming_state(slab_pair, slab_rows, attend_group, group_count)
     delta_attention_complete = output_everything + jnp.einsum(
@@ -255,18 +269,34 @@
     return exchange(add_now, 1, step + 1), parts
 
 
+def latent_rounds(slab_rows):
+    reach = min(window_slabs_of(slab_rows), lax.axis_size("ctx") - 1)
+    plan, span = [], 1
+    while 2 * span <= reach:
+        plan.append((span, span))
+        span *= 2
+    if reach + 1 > span:
+        plan.append((1, reach + 1 - span))
+    return plan
+
+
+def latent_round(held, slab_rows, step):
+    distance, count = latent_rounds(slab_rows)[step]
+    return jnp.concatenate([shifted(held[:count], "ctx", distance), held], axis=0)
+
+
 def latent_attention(
-    mla_query, latents, key_up, value_up, positions, docids, doc_starts, head_count
+    mla_query, held, held_after, key_up, value_up, positions, docids, doc_starts, head_count
 ):
+    latents = held[-1]
     slab_rows = latents.shape[0]
     slabs = lax.axis_size("ctx")
-    reach = window_slabs_of(slab_rows)
-    window_slabs = min(reach + 1, slabs)
-    window_rows = window_slabs * slab_rows
-    everything = lax.all_gather(latents, "ctx", tiled=True)
-    first_slab = jnp.clip(lax.axis_index("ctx") - reach, 0, slabs - window_slabs)
-    key_first = first_slab * slab_rows
-    key_rows = lax.dynamic_slice_in_dim(everything, key_first, window_rows, 0)
+    reach = min(window_slabs_of(slab_rows), slabs - 1)
+    window_rows = (reach + 1) * slab_rows
+    for step in range(len(latent_rounds(slab_rows)) - len(held_after)):
+        held = latent_round(held, slab_rows, len(held_after) + step)
+    key_rows = held.reshape(window_rows, latents.shape[1])
+    key_first = (lax.axis_index("ctx") - reach) * slab_rows
     queries = mla_query.reshape(slab_rows, head_count, NOPE + ROPE)
     score_scale = 1.0 / math.sqrt(NOPE + ROPE)
     key_places = key_first + jnp.arange(window_rows, dtype=jnp.int32)

time: 247 us -> 330 us (1.34)
  the two profiles are of different devices: /device:TPU:4 before, /device:TPU:84 now
where the time goes in v5:
time: 330 us; the launch traced here: 326 us
  matrix products  124 us (38%)
  waiting for transfers between devices  69.9 us (21%)
  starting transfers between devices  62.7 us (19%)
  other arithmetic  38.2 us (12%)
  local copies, waits for them, and re-layouts  28.7 us (9%)
    ppermute x10, waiting for transfers between devices, shifted(): return lax.ppermute(block, axis, route)  69.9 us
    ppermute x10, starting transfers between devices, shifted(): return lax.ppermute(block, axis, route)  62.7 us
    dot_general x4, matrix products, attend_group(): jnp.einsum('hts,shv->thv', weights.astype(jnp.bfloat16), values, preferre...  23.9 us
    dot_general x4, matrix products, attend_group(): jnp.dot(latent_part, value_up[:, group * per_group * value_width:(group +...  16.2 us
    dot_general x4, matrix products, attend_group(): jnp.dot(latent_part, key_up[:, group * per_group * NOPE:(group + 1) * per...  14 us
    optimization_barrier x4, local copies, waits for them, and re-layouts, attend_group(): rows, _ = lax.optimization_barrier((key_rows, tie))  13.3 us
    another operation x1, other arithmetic, block_terms(): cumulative = jnp.cumsum(logarithm_decay, axis=0)  13.2 us
    dot_general x4, matrix products, product(): return jnp.einsum('hkj,hjl->hkl', left, right, precision=PRECISE_PRODUCT)  11 us
  transfers between devices with their start and end apart: 10, of which 4 were waited for; matrix products, arithmetic and copies ran while one was open for 48% of the time, Pallas kernels for 0%

profile of v5, /device:TPU:84, one launch (start us, length us, event | category | flops | bytes accessed | tf_op | source)
XLA Modules:
  0.0 325.7 jit_solution(9491553463879577136)
XLA Ops:
  16.5 13.2 %fusion.171 = f32[2,64,16,128]{3,2,1,0:T(8,128)S(1)} fusion(f32[2,64,16,128]{3,2,1,0:T(8,128)S(1)} %bitcast.238), kind=kOutput, calls=%fused_computation.231 | output fusion | flops 16515072 | bytes 2097152 | tf_op jit(solution)/shard_map/vmap(jit(cumsum))/reduce_window_sum | solution.py:69
  30.0 4.6 %collective-permute-start.1 = (bf16[2,128,576]{1,2,0:T(8,128)(2,1)S(1)}, bf16[2,128,576]{1,2,0:T(8,128)(2,1)S(1)}, u32[]{:S(2)}, u32[]{:S(2)}) collective-permute-start(bf16[2,128,576]{1,2,0:T(8,128)(2,1)S(1)} %pad_maximum_fusion.7), channel_id=1, source_target_pairs={{0,16},{8,24},{16,32},{24,40},{32,48},{40,56},{48,64},{56,72},{64,... | collective-permute-start | bytes 884744 | tf_op jit(solution)/shard_map/ppermute | solution.py:42
  59.0 3.9 %fusion.115 = f32[2,16,128,128]{3,2,1,0:T(8,128)S(1)} fusion(f32[2,16,64,128]{3,2,1,0:T(8,128)S(1)} %fusion.99, f32[2,64,16,128]{3,2,1,0:T(8,128)S(1)} %get-tuple-element.60), kind=kOutput, calls=%fused_computation.140 | convolution fusion | flops 402653184 | bytes 4194304 | tf_op jit(solution)/shard_map/vmap(omt,mor->mtr)/dot_general | solution.py:106
  62.9 4.0 %multiply_subtract_fusion = f32[2,16,128,128]{3,2,1,0:T(8,128)S(1)} fusion(f32[2,16,64,128]{3,2,1,0:T(8,128)S(1)} %fusion.97, f32[128,128]{1,0:T(8,128)S(1)} %fusion.154, f32[2,16,128]{2,1,0:T(8,128)S(1)} %bitcast.256, f32[2]{0:T(128)S(1)} %copy-done.29, f32[2,64,16,128]{3,2,1,0:T(8,128)S(1)} %get-tuple-element.60), kind=kOutput, calls=%fused_computation.53 | convolution fusion | flops 404226048 | bytes 4276232 | tf_op jit(solution)/shard_map/vmap(shk,hsj->hkj)/dot_general | solution.py:103
  69.2 5.0 %collective-permute-start.2 = (bf16[4,128,576]{1,2,0:T(8,128)(2,1)S(1)}, bf16[4,128,576]{1,2,0:T(8,128)(2,1)S(1)}, u32[]{:S(2)}, u32[]{:S(2)}) collective-permute-start(bf16[4,128,576]{1,2,0:T(8,128)(2,1)S(1)} %pad_maximum_fusion.5), channel_id=1, source_target_pairs={{0,32},{8,40},{16,48},{24,56},{32,64},{40,72},{48,80},{56,88},{64,... | collective-permute-start | bytes 1769480 | tf_op jit(solution)/shard_map/ppermute | solution.py:42
  76.7 9.5 %collective-permute-done.2 = bf16[4,128,576]{1,2,0:T(8,128)(2,1)S(1)} collective-permute-done((bf16[4,128,576]{1,2,0:T(8,128)(2,1)S(1)}, bf16[4,128,576]{1,2,0:T(8,128)(2,1)S(1)}, u32[]{:S(2)}, u32[]{:S(2)}) %collective-permute-start.2) | collective-permute-done | bytes 589856 | tf_op jit(solution)/shard_map/ppermute | solution.py:42
  88.8 4.0 %collective-permute-start.3 = (bf16[16,128,256]{2,1,0:T(8,128)(2,1)}, bf16[16,128,256]{2,1,0:T(8,128)(2,1)}, u32[]{:S(2)}, u32[]{:S(2)}) collective-permute-start(bf16[16,128,256]{2,1,0:T(8,128)(2,1)} %pad_maximum_fusion.2), channel_id=1, source_target_pairs={{0,8},{8,16},{16,24},{24,32},{32,40},{40,48},{48,56},{56,64},{64,7... | collective-permute-start | bytes 3145736 | tf_op jit(solution)/shard_map/ppermute | solution.py:42
  95.1 6.5 %collective-permute-start.5 = (bf16[8,128,576]{1,2,0:T(8,128)(2,1)}, bf16[8,128,576]{1,2,0:T(8,128)(2,1)S(1)}, u32[]{:S(2)}, u32[]{:S(2)}) collective-permute-start(bf16[8,128,576]{1,2,0:T(8,128)(2,1)} %pad_maximum_fusion.1), channel_id=1, source_target_pairs={{0,64},{8,72},{16,80},{24,88},{32,96},{40,104},{48,112},{56,120},{... | collective-permute-start | bytes 3538952 | tf_op jit(solution)/shard_map/ppermute | solution.py:42
  107.8 6.5 %collective-permute-done.3 = bf16[16,128,256]{2,1,0:T(8,128)(2,1)} collective-permute-done((bf16[16,128,256]{2,1,0:T(8,128)(2,1)}, bf16[16,128,256]{2,1,0:T(8,128)(2,1)}, u32[]{:S(2)}, u32[]{:S(2)}) %collective-permute-start.3) | collective-permute-done | bytes 1048608 | tf_op jit(solution)/shard_map/ppermute | solution.py:42
  116.6 33.7 %collective-permute-done.5 = bf16[8,128,576]{1,2,0:T(8,128)(2,1)S(1)} collective-permute-done((bf16[8,128,576]{1,2,0:T(8,128)(2,1)}, bf16[8,128,576]{1,2,0:T(8,128)(2,1)S(1)}, u32[]{:S(2)}, u32[]{:S(2)}) %collective-permute-start.5) | collective-permute-done | bytes 1179680 | tf_op jit(solution)/shard_map/ppermute | solution.py:42
  150.4 19.0 %collective-permute-start.6 = (bf16[1,128,576]{1,2,0:T(8,128)(2,1)S(1)}, bf16[1,128,576]{1,2,0:T(8,128)(2,1)S(1)}, u32[]{:S(2)}, u32[]{:S(2)}) collective-permute-start(bf16[1,128,576]{1,2,0:T(8,128)(2,1)S(1)} %slice.179), channel_id=1, source_target_pairs={{0,8},{8,16},{16,24},{24,32},{32,40},{40,48},{48,56},{56,64},{64,7... | collective-permute-start | bytes 442376 | tf_op jit(solution)/shard_map/ppermute | solution.py:42
  172.8 20.0 %collective-permute-done.6 = bf16[1,128,576]{1,2,0:T(8,128)(2,1)S(1)} collective-permute-done((bf16[1,128,576]{1,2,0:T(8,128)(2,1)S(1)}, bf16[1,128,576]{1,2,0:T(8,128)(2,1)S(1)}, u32[]{:S(2)}, u32[]{:S(2)}) %collective-permute-start.6) | collective-permute-done | bytes 147488 | tf_op jit(solution)/shard_map/ppermute | solution.py:42
  194.5 3.9 %copy.78 = bf16[17,128,576]{2,1,0:T(8,128)(2,1)S(1)} copy(bf16[17,128,576]{1,2,0:T(8,128)(2,1)} %pad_maximum_fusion) | data formatting | bytes 5013504 | tf_op jit(solution)/shard_map/concatenate | solution.py:285
  207.9 4.3 %convolution_convert_fusion.7 = bf16[2176,512]{0,1:T(8,128)(2,1)} fusion(bf16[2176,576]{1,0:T(8,128)(2,1)S(1)} %bitcast.220, bf16[512,2048]{1,0:T(8,128)(2,1)} %param.18), kind=kOutput, calls=%fused_computation.43 | convolution fusion | flops 1141964800 | bytes 4980736 | tf_op jit(solution)/shard_map/dot_general | solution.py:327
  213.6 5.9 %fusion.83 = bf16[128,4,128]{0,2,1:T(8,128)(2,1)S(1)} fusion(bf16[2176,4,128]{0,2,1:T(8,128)(2,1)} %bitcast.259, f32[128,4]{0,1:T(4,128)S(1)} %bitcast.263, f32[4,128,2176]{1,2,0:T(8,128)} %copy-done.14, pred[128,2176]{0,1:T(8,128)(4,1)S(1)} %compare_and_fusion), kind=kOutput, calls=%fused_computation.89 | convolution fusion | flops 288688768 | bytes 7096320 | tf_op jit(solution)/shard_map/hts,shv->thv/dot_general | solution.py:356
  238.8 4.3 %convolution_convert_fusion.5 = bf16[2176,512]{0,1:T(8,128)(2,1)} fusion(bf16[2176,576]{1,0:T(8,128)(2,1)S(1)} %bitcast.223, bf16[512,2048]{1,0:T(8,128)(2,1)} %param.18), kind=kOutput, calls=%fused_computation.41 | convolution fusion | flops 1141964800 | bytes 4980736 | tf_op jit(solution)/shard_map/dot_general | solution.py:327
  244.5 5.9 %fusion.80 = bf16[128,4,128]{0,2,1:T(8,128)(2,1)S(1)} fusion(bf16[2176,4,128]{0,2,1:T(8,128)(2,1)} %bitcast.260, f32[128,4]{0,1:T(4,128)S(1)} %bitcast.264, f32[4,128,2176]{1,2,0:T(8,128)} %copy-done.15, pred[128,2176]{0,1:T(8,128)(4,1)S(1)} %compare_and_fusion), kind=kOutput, calls=%fused_computation.88 | convolution fusion | flops 288688768 | bytes 7096320 | tf_op jit(solution)/shard_map/hts,shv->thv/dot_general | solution.py:356
  257.0 3.8 %convolution_convert_fusion.2 = bf16[2176,512]{0,1:T(8,128)(2,1)} fusion(bf16[2176,576]{1,0:T(8,128)(2,1)S(1)} %bitcast.224, bf16[512,2048]{1,0:T(8,128)(2,1)} %param.17), kind=kOutput, calls=%fused_computation.38 | convolution fusion | flops 1141964800 | bytes 4980736 | tf_op jit(solution)/shard_map/dot_general | solution.py:318
  270.5 3.9 %convolution_convert_fusion.3 = bf16[2176,512]{0,1:T(8,128)(2,1)} fusion(bf16[2176,576]{1,0:T(8,128)(2,1)S(1)} %bitcast.226, bf16[512,2048]{1,0:T(8,128)(2,1)} %param.18), kind=kOutput, calls=%fused_computation.39 | convolution fusion | flops 1141964800 | bytes 4980736 | tf_op jit(solution)/shard_map/dot_general | solution.py:327
  274.4 5.9 %fusion.77 = bf16[128,4,128]{0,2,1:T(8,128)(2,1)S(1)} fusion(bf16[2176,4,128]{0,2,1:T(8,128)(2,1)} %bitcast.261, f32[128,4]{0,1:T(4,128)S(1)} %bitcast.265, f32[4,128,2176]{1,2,0:T(8,128)} %copy-done.16, pred[128,2176]{0,1:T(8,128)(4,1)S(1)} %compare_and_fusion), kind=kOutput, calls=%fused_computation.87 | convolution fusion | flops 288688768 | bytes 7096320 | tf_op jit(solution)/shard_map/hts,shv->thv/dot_general | solution.py:356
  283.8 14.1 %collective-permute-start.9 = (bf16[16,128,128]{2,1,0:T(8,128)(2,1)}, bf16[16,128,128]{2,1,0:T(8,128)(2,1)}, u32[]{:S(2)}, u32[]{:S(2)}) collective-permute-start(bf16[16,128,128]{2,1,0:T(8,128)(2,1)} %fusion.47), channel_id=1, source_target_pairs={{0,8},{8,16},{16,24},{24,32},{32,40},{40,48},{48,56},{56,64},{64,7... | collective-permute-start | bytes 1572872 | tf_op jit(solution)/shard_map/ppermute | solution.py:42
  297.9 3.8 %convolution_convert_fusion = bf16[2176,512]{0,1:T(8,128)(2,1)} fusion(bf16[2176,576]{1,0:T(8,128)(2,1)S(1)} %bitcast.227, bf16[512,2048]{1,0:T(8,128)(2,1)} %param.17), kind=kOutput, calls=%fused_computation.36 | convolution fusion | flops 1141964800 | bytes 4980736 | tf_op jit(solution)/shard_map/dot_general | solution.py:318
  311.4 3.9 %convolution_convert_fusion.1 = bf16[2176,512]{0,1:T(8,128)(2,1)} fusion(bf16[2176,576]{1,0:T(8,128)(2,1)S(1)} %bitcast.229, bf16[512,2048]{1,0:T(8,128)(2,1)} %param.18), kind=kOutput, calls=%fused_computation.37 | convolution fusion | flops 1141964800 | bytes 4980736 | tf_op jit(solution)/shard_map/dot_general | solution.py:327
  315.3 6.1 %fusion.74 = bf16[128,4,128]{0,2,1:T(8,128)(2,1)S(1)} fusion(bf16[2176,4,128]{0,2,1:T(8,128)(2,1)} %bitcast.258, f32[128,4]{0,1:T(4,128)S(1)} %bitcast.262, f32[4,128,2176]{1,2,0:T(8,128)} %copy-done.13, pred[128,2176]{0,1:T(8,128)(4,1)S(1)} %compare_and_fusion), kind=kOutput, calls=%fused_computation.86 | convolution fusion | flops 288688768 | bytes 7096320 | tf_op jit(solution)/shard_map/hts,shv->thv/dot_general | solution.py:356
  (180 shorter events, 128.1 us)
Async XLA Ops:
  0.6 14.9 %collective-permute-start = (bf16[1,128,576]{1,2,0:T(8,128)(2,1)}, bf16[1,128,576]{1,2,0:T(8,128)(2,1)}, u32[]{:S(2)}, u32[]{:S(2)}) collective-permute-start(bf16[1,128,576]{1,2,0:T(8,128)(2,1)} %bitcast.254), channel_id=1, source_target_pairs={{0,8},{8,16},{16,24},{24,32},{32,40},{40,48},{48,56},{56,64},{64,7... | collective-permute-start | bytes 442376 | tf_op jit(solution)/shard_map/ppermute | solution.py:42
  14.8 19.9 %copy-start.24 = (f32[2,64]{1,0:T(2,128)S(1)}, f32[2,64]{1,0:T(2,128)}, u32[]{:S(2)}) copy-start(f32[2,64]{1,0:T(2,128)} %get-tuple-element.64) | copy-start | bytes 1540
  30.0 39.1 %collective-permute-start.1 = (bf16[2,128,576]{1,2,0:T(8,128)(2,1)S(1)}, bf16[2,128,576]{1,2,0:T(8,128)(2,1)S(1)}, u32[]{:S(2)}, u32[]{:S(2)}) collective-permute-start(bf16[2,128,576]{1,2,0:T(8,128)(2,1)S(1)} %pad_maximum_fusion.7), channel_id=1, source_target_pairs={{0,16},{8,24},{16,32},{24,40},{32,48},{40,56},{48,64},{56,72},{64,... | collective-permute-start | bytes 884744 | tf_op jit(solution)/shard_map/ppermute | solution.py:42
  62.9 12.5 %copy-start.8 = (f32[2,16,128,128]{3,2,1,0:T(8,128)}, f32[2,16,128,128]{3,2,1,0:T(8,128)S(1)}, u32[]{:S(2)}) copy-start(f32[2,16,128,128]{3,2,1,0:T(8,128)S(1)} %fusion.115) | copy-start | bytes 6291460
  69.2 17.0 %collective-permute-start.2 = (bf16[4,128,576]{1,2,0:T(8,128)(2,1)S(1)}, bf16[4,128,576]{1,2,0:T(8,128)(2,1)S(1)}, u32[]{:S(2)}, u32[]{:S(2)}) collective-permute-start(bf16[4,128,576]{1,2,0:T(8,128)(2,1)S(1)} %pad_maximum_fusion.5), channel_id=1, source_target_pairs={{0,32},{8,40},{16,48},{24,56},{32,64},{40,72},{48,80},{56,88},{64,... | collective-permute-start | bytes 1769480 | tf_op jit(solution)/shard_map/ppermute | solution.py:42
  75.4 12.0 %copy-start.6 = (f32[16,128,128]{2,1,0:T(8,128)}, f32[16,128,128]{2,1,0:T(8,128)S(1)}, u32[]{:S(2)}) copy-start(f32[16,128,128]{2,1,0:T(8,128)S(1)} %fusion.91) | copy-start | bytes 3145732
  76.7 92.7 %copy-start = (f32[16,128,128]{2,1,0:T(8,128)}, f32[16,128,128]{2,1,0:T(8,128)S(1)}, u32[]{:S(2)}) copy-start(f32[16,128,128]{2,1,0:T(8,128)S(1)} %convolution_add_fusion.1) | copy-start | bytes 3145732
  87.5 14.1 %copy-start.26 = (s32[128]{0:T(128)S(1)}, s32[128]{0:T(128)}, u32[]{:S(2)}) copy-start(s32[128]{0:T(128)} %copy-done.25) | copy-start | bytes 1540
  87.5 14.1 %copy-start.28 = (s32[128]{0:T(128)S(1)}, s32[128]{0:T(128)}, u32[]{:S(2)}) copy-start(s32[128]{0:T(128)} %copy-done.27) | copy-start | bytes 1540
  88.8 25.6 %collective-permute-start.3 = (bf16[16,128,256]{2,1,0:T(8,128)(2,1)}, bf16[16,128,256]{2,1,0:T(8,128)(2,1)}, u32[]{:S(2)}, u32[]{:S(2)}) collective-permute-start(bf16[16,128,256]{2,1,0:T(8,128)(2,1)} %pad_maximum_fusion.2), channel_id=1, source_target_pairs={{0,8},{8,16},{16,24},{24,32},{32,40},{40,48},{48,56},{56,64},{64,7... | collective-permute-start | bytes 3145736 | tf_op jit(solution)/shard_map/ppermute | solution.py:42
  95.1 10.9 %copy-start.9 = (f32[2,16,128,128]{3,2,1,0:T(8,128)S(1)}, f32[2,16,128,128]{3,2,1,0:T(8,128)}, u32[]{:S(2)}) copy-start(f32[2,16,128,128]{3,2,1,0:T(8,128)} %copy-done.8) | copy-start | bytes 6291460
  95.1 10.9 %copy-start.11 = (f32[2,16,64,128]{3,2,1,0:T(8,128)S(1)}, f32[2,16,64,128]{3,2,1,0:T(8,128)}, u32[]{:S(2)}) copy-start(f32[2,16,64,128]{3,2,1,0:T(8,128)} %convolution_subtract_fusion) | copy-start | bytes 3145732
  95.1 10.9 %copy-start.17 = (f32[2,16,64,128]{3,2,1,0:T(8,128)S(1)}, f32[2,16,64,128]{3,2,1,0:T(8,128)}, u32[]{:S(2)}) copy-start(f32[2,16,64,128]{3,2,1,0:T(8,128)} %fusion.177) | copy-start | bytes 3145732
  95.1 55.3 %collective-permute-start.5 = (bf16[8,128,576]{1,2,0:T(8,128)(2,1)}, bf16[8,128,576]{1,2,0:T(8,128)(2,1)S(1)}, u32[]{:S(2)}, u32[]{:S(2)}) collective-permute-start(bf16[8,128,576]{1,2,0:T(8,128)(2,1)} %pad_maximum_fusion.1), channel_id=1, source_target_pairs={{0,64},{8,72},{16,80},{24,88},{32,96},{40,104},{48,112},{56,120},{... | collective-permute-start | bytes 3538952 | tf_op jit(solution)/shard_map/ppermute | solution.py:42
  103.0 11.4 %copy-start.7 = (f32[16,128,128]{2,1,0:T(8,128)S(1)}, f32[16,128,128]{2,1,0:T(8,128)}, u32[]{:S(2)}) copy-start(f32[16,128,128]{2,1,0:T(8,128)} %copy-done.6) | copy-start | bytes 3145732
  116.6 54.2 %copy-start.2 = (f32[16,128,256]{2,1,0:T(8,128)}, f32[16,128,256]{2,1,0:T(8,128)S(1)}, u32[]{:S(2)}) copy-start(f32[16,128,256]{2,1,0:T(8,128)S(1)} %fusion.178) | copy-start | bytes 6291460
  150.4 42.4 %copy-start.12 = (bf16[8,128,576]{1,2,0:T(8,128)(2,1)S(1)}, bf16[8,128,576]{1,2,0:T(8,128)(2,1)}, u32[]{:S(2)}) copy-start(bf16[8,128,576]{1,2,0:T(8,128)(2,1)} %pad_maximum_fusion.1) | copy-start | bytes 3538948
  150.4 42.4 %collective-permute-start.6 = (bf16[1,128,576]{1,2,0:T(8,128)(2,1)S(1)}, bf16[1,128,576]{1,2,0:T(8,128)(2,1)S(1)}, u32[]{:S(2)}, u32[]{:S(2)}) collective-permute-start(bf16[1,128,576]{1,2,0:T(8,128)(2,1)S(1)} %slice.179), channel_id=1, source_target_pairs={{0,8},{8,16},{16,24},{24,32},{32,40},{40,48},{48,56},{56,64},{64,7... | collective-permute-start | bytes 442376 | tf_op jit(solution)/shard_map/ppermute | solution.py:42
  170.8 48.7 %collective-permute-start.4 = (bf16[16,128,256]{2,1,0:T(8,128)(2,1)}, bf16[16,128,256]{2,1,0:T(8,128)(2,1)}, u32[]{:S(2)}, u32[]{:S(2)}) collective-permute-start(bf16[16,128,256]{2,1,0:T(8,128)(2,1)} %pad_maximum_fusion.3), channel_id=1, source_target_pairs={{0,16},{8,24},{16,32},{24,40},{32,48},{40,56},{48,64},{56,72},{64,... | collective-permute-start | bytes 3145736 | tf_op jit(solution)/shard_map/ppermute | solution.py:42
  225.1 25.3 %collective-permute-start.7 = (bf16[16,128,256]{2,1,0:T(8,128)(2,1)}, bf16[16,128,256]{2,1,0:T(8,128)(2,1)}, u32[]{:S(2)}, u32[]{:S(2)}) collective-permute-start(bf16[16,128,256]{2,1,0:T(8,128)(2,1)} %pad_maximum_fusion.4), channel_id=1, source_target_pairs={{0,32},{8,40},{16,48},{24,56},{32,64},{40,72},{48,80},{56,88},{64,... | collective-permute-start | bytes 3145736 | tf_op jit(solution)/shard_map/ppermute | solution.py:42
  254.6 25.7 %collective-permute-start.8 = (bf16[16,128,128]{2,1,0:T(8,128)(2,1)}, bf16[16,128,128]{2,1,0:T(8,128)(2,1)}, u32[]{:S(2)}, u32[]{:S(2)}) collective-permute-start(bf16[16,128,128]{2,1,0:T(8,128)(2,1)} %fusion.145), channel_id=1, source_target_pairs={{0,64},{8,72},{16,80},{24,88},{32,96},{40,104},{48,112},{56,120},{... | collective-permute-start | bytes 1572872 | tf_op jit(solution)/shard_map/ppermute | solution.py:42
  283.8 37.6 %collective-permute-start.9 = (bf16[16,128,128]{2,1,0:T(8,128)(2,1)}, bf16[16,128,128]{2,1,0:T(8,128)(2,1)}, u32[]{:S(2)}, u32[]{:S(2)}) collective-permute-start(bf16[16,128,128]{2,1,0:T(8,128)(2,1)} %fusion.47), channel_id=1, source_target_pairs={{0,8},{8,16},{16,24},{24,32},{32,40},{40,48},{48,56},{56,64},{64,7... | collective-permute-start | bytes 1572872 | tf_op jit(solution)/shard_map/ppermute | solution.py:42
  315.3 6.1 %copy-start.18 = (f32[1,16,64,128]{3,2,1,0:T(8,128)S(1)}, f32[1,16,64,128]{3,2,1,0:T(8,128)}, u32[]{:S(2)}) copy-start(f32[1,16,64,128]{3,2,1,0:T(8,128)} %fusion.48) | copy-start | bytes 1572868
  315.3 6.1 %copy-start.19 = (f32[1,16,64,128]{3,2,1,0:T(8,128)S(1)}, f32[1,16,64,128]{3,2,1,0:T(8,128)}, u32[]{:S(2)}) copy-start(f32[1,16,64,128]{3,2,1,0:T(8,128)} %convolution_bitcast_fusion.9) | copy-start | bytes 1572868
  (19 other events, 57.0 us)

commit v6 on v4

--- a/solution.py
+++ b/solution.py
@@ -3,6 +3,8 @@
 import jax
 import jax.numpy as jnp
 from jax import lax
+from jax.experimental import pallas as pl
+from jax.experimental.pallas import tpu as pltpu
 from jax.sharding import PartitionSpec as P
 
 NOPE = 128
@@ -206,7 +208,7 @@
         .reshape(slab_rows, -1)
         .astype(jnp.bfloat16)
     )
-    mla_out = jnp.concatenate(mla_parts, axis=1).reshape(slab_rows, -1)
+    mla_out = jnp.concatenate(mla_parts, axis=1)
     return (kda_out, mla_out)
 
 
@@ -253,6 +255,49 @@
         distance, step = 2 * distance, step + 1
     add_now = product(map_now, exchange(add_now, distance, step)) + add_now
     return exchange(add_now, 1, step + 1), parts
+
+
+def attend_body(scale, qn_ref, qr_ref, kn_ref, kr_ref, v_ref, allowed_ref, out_ref):
+    allowed = allowed_ref[...] != 0
+    keys_rope = kr_ref[...]
+    for head in range(qn_ref.shape[0]):
+        columns = slice(head * NOPE, (head + 1) * NOPE)
+        contract = (((1,), (1,)), ((), ()))
+        scores = lax.dot_general(
+            qn_ref[head], kn_ref[:, columns], contract, preferred_element_type=jnp.float32
+        )
+        scores = (
+            scores
+            + lax.dot_general(
+                qr_ref[head], keys_rope, contract, preferred_element_type=jnp.float32
+            )
+        ) * scale
+        masked = jnp.where(allowed, scores, -1e30)
+        row_max = jnp.max(masked, axis=1, keepdims=True)
+        weights = jnp.where(allowed, jnp.exp(masked - row_max), 0.0)
+        row_total = jnp.sum(weights, axis=1, keepdims=True)
+        summed = jnp.dot(
+            weights.astype(jnp.bfloat16), v_ref[:, columns], preferred_element_type=jnp.float32
+        )
+        out_ref[:, columns] = (summed / row_total).astype(out_ref.dtype)
+
+
+def attend_kernel(query_nope, query_rope, keys_nope, keys_rope, values, allowed, scale):
+    heads, rows, _ = query_nope.shape
+    window = keys_nope.shape[0]
+    flops = 2 * heads * rows * window * (NOPE + ROPE + values.shape[1] // heads)
+    return pl.pallas_call(
+        lambda *refs: attend_body(scale, *refs),
+        out_shape=jax.ShapeDtypeStruct((rows, values.shape[1]), jnp.bfloat16),
+        in_specs=[pl.BlockSpec(memory_space=pltpu.VMEM)] * 6,
+        out_specs=pl.BlockSpec(memory_space=pltpu.VMEM),
+        cost_estimate=pl.CostEstimate(
+            flops=flops,
+            transcendentals=heads * rows * window,
+            bytes_accessed=2 * window * (keys_nope.shape[1] + values.shape[1] + ROPE)
+            + 4 * rows * window,
+        ),
+    )(query_nope, query_rope, keys_nope, keys_rope, values, allowed)
 
 
 def latent_attention(
@@ -274,6 +319,7 @@
     allowed = (key_places[None, :] <= positions[:, None]) & (
         key_docs[None, :] == docids[:, None]
     )
+    allowed_flags = allowed.astype(jnp.int32)
     value_width = value_up.shape[1] // head_count
     group_count = carry_rounds(slab_rows)
     while head_count % group_count:
@@ -304,32 +350,15 @@
             .astype(jnp.bfloat16)
             .reshape(window_rows, per_group, value_width)
         )
-        scores = jnp.einsum(
-            "thd,shd->hts",
-            queries[:, heads, :NOPE],
-            keys_nope,
-            preferred_element_type=jnp.float32,
-        )
-        scores = (
-            scores
-            + jnp.einsum(
-                "thr,sr->hts",
-                queries[:, heads, NOPE:],
-                rows[:, LATENT:],
-                preferred_element_type=jnp.float32,
-            )
-        ) * score_scale
-        masked = jnp.where(allowed[None], scores, -1e30)
-        row_max = jnp.max(masked, axis=2, keepdims=True)
-        weights = jnp.where(allowed[None], jnp.exp(masked - row_max), 0.0)
-        row_total = jnp.sum(weights, axis=2)
-        summed = jnp.einsum(
-            "hts,shv->thv",
-            weights.astype(jnp.bfloat16),
-            values,
-            preferred_element_type=jnp.float32,
-        )
-        return (summed / jnp.transpose(row_total)[:, :, None]).astype(jnp.bfloat16)
+        return attend_kernel(
+            jnp.transpose(queries[:, heads, :NOPE], (1, 0, 2)),
+            jnp.transpose(queries[:, heads, NOPE:], (1, 0, 2)),
+            keys_nope.reshape(window_rows, -1),
+            rows[:, LATENT:],
+            values.reshape(window_rows, -1),
+            allowed_flags,
+            score_scale,
+        )
 
     return attend_group, group_count
 

time: 247 us -> 262 us (1.061)
  the two profiles are of different devices: /device:TPU:4 before, /device:TPU:102 now
where the time goes in v6:
time: 262 us; the launch traced here: 258 us
  matrix products  101 us (39%)
  local copies, waits for them, and re-layouts  39.6 us (15%)
  waiting for transfers between devices  32.2 us (12%)
  Pallas kernels  29.4 us (11%)
  starting transfers between devices  24.8 us (9%)
  other arithmetic  15.5 us (6%)
  between operations  15 us (6%)
    ppermute x5, waiting for transfers between devices, shifted(): return lax.ppermute(block, axis, route)  32.1 us
    pallas_call x4, Pallas kernels, attend_kernel(): pl.pallas_call(lambda *refs: attend_body(scale, *refs), out_shape=jax.Sha...  29.4 us
    unnamed x78, local copies, waits for them, and re-layouts  24.9 us
    ppermute x5, starting transfers between devices, shifted(): return lax.ppermute(block, axis, route)  24.8 us
    dot_general x5, matrix products, unit_lower_inverse(): jnp.einsum('hij,hjk->hik', result, identity + power_term, precision=PRECI...  16.8 us
    dot_general x4, matrix products, attend_group(): jnp.dot(latent_part, key_up[:, group * per_group * NOPE:(group + 1) * per...  15.3 us
    dot_general x4, matrix products, attend_group(): jnp.dot(latent_part, value_up[:, group * per_group * value_width:(group +...  15.1 us
    dot_general x4, matrix products, product(): return jnp.einsum('hkj,hjl->hkl', left, right, precision=PRECISE_PRODUCT)  10.1 us
  transfers between devices with their start and end apart: 6, of which 3 were waited for; matrix products, arithmetic and copies ran while one was open for 52% of the time, Pallas kernels for 11%

profile of v6, /device:TPU:102, one launch (start us, length us, event | category | flops | bytes accessed | tf_op | source)
XLA Modules:
  0.0 257.5 jit_solution(10405447048044304163)
XLA Ops:
  34.0 12.0 %fusion.79 = f32[2,16,64,64]{3,2,1,0:T(8,128)S(1)} fusion(f32[2,16,64,64]{3,2,1,0:T(8,128)S(1)} %fusion.28, f32[2,16,64,64]{3,2,1,0:T(8,128)S(1)} %convolution_add_fusion.2), kind=kOutput, calls=%fused_computation.147 | convolution fusion | flops 100663296 | bytes 1572864 | tf_op jit(solution)/shard_map/vmap(hij,hjk->hik)/dot_general | solution.py:63
  49.4 4.7 %multiply_subtract_fusion = f32[2,16,128,128]{3,2,1,0:T(8,128)S(1)} fusion(f32[2,16,64,128]{3,2,1,0:T(8,128)S(1)} %fusion.22, f32[128,128]{1,0:T(8,128)S(1)} %fusion.63, f32[2,16,128]{2,1,0:T(8,128)S(1)} %bitcast.162, f32[2]{0:T(128)S(1)} %slice_reduce_fusion, f32[2,64,16,128]{3,2,1,0:T(8,128)S(1)} %fusion.16, f32[2,64,16,128]{3,2,1,0:T(8,128)S(1)} %bitcast.141, ...), kind=kOutput, calls=%fused_computation.8 | convolution fusion | flops 405274624 | bytes 5349896 | tf_op jit(solution)/shard_map/vmap(shk,hsj->hkj)/dot_general | solution.py:105
  57.0 4.2 %fusion.62 = f32[2,16,128,128]{2,3,1,0:T(8,128)S(1)} fusion(f32[2,16,64,128]{3,2,1,0:T(8,128)S(1)} %fusion.24, f32[2,64,16,128]{3,2,1,0:T(8,128)S(1)} %fusion.16, f32[2,64,16,128]{3,2,1,0:T(8,128)S(1)} %bitcast.142, f32[2,64]{1,0:T(2,128)S(1)} %get-tuple-element.40, f32[2,16,128]{2,1,0:T(8,128)S(1)} %slice_bitcast_fusion.14, f32[2,64,16]{1,2,0:T(8,128)S(1)} %copy.163), kind=kOutput, calls=%fused_computation.107 | convolution fusion | flops 403701760 | bytes 5267968 | tf_op jit(solution)/shard_map/vmap(omt,mor->mtr)/dot_general | solution.py:108
  64.8 4.9 %collective-permute-start = (bf16[16,128,256]{1,2,0:T(8,128)(2,1)}, bf16[16,128,256]{1,2,0:T(8,128)(2,1)}, u32[]{:S(2)}, u32[]{:S(2)}) collective-permute-start(bf16[16,128,256]{1,2,0:T(8,128)(2,1)} %pad_maximum_fusion), channel_id=1, source_target_pairs={{0,8},{8,16},{16,24},{24,32},{32,40},{40,48},{48,56},{56,64},{64,7... | collective-permute-start | bytes 3145736 | tf_op jit(solution)/shard_map/ppermute | solution.py:44
  83.3 4.1 %convolution_select_fusion.1 = f32[2,16,64,64]{3,2,1,0:T(8,128)S(1)} fusion(pred[2,64,64]{2,1,0:T(8,128)(4,1)S(1)} %get-tuple-element.41, f32[2,64,16,128]{3,2,1,0:T(8,128)} %bitcast.144, f32[2,64,16]{1,2,0:T(8,128)S(1)} %copy.159, f32[2,64,16,128]{3,2,1,0:T(8,128)S(1)} %fusion.16, f32[2,64,16,128]{3,2,1,0:T(8,128)S(1)} %bitcast.143, ...), kind=kOutput, calls=%fused_computation.25 | convolution fusion | flops 202768384 | bytes 3694592 | tf_op jit(solution)/shard_map/vmap(thk,shk->hts)/dot_general | solution.py:92
  93.8 17.2 %collective-permute-done = bf16[16,128,256]{1,2,0:T(8,128)(2,1)} collective-permute-done((bf16[16,128,256]{1,2,0:T(8,128)(2,1)}, bf16[16,128,256]{1,2,0:T(8,128)(2,1)}, u32[]{:S(2)}, u32[]{:S(2)}) %collective-permute-start) | collective-permute-done | bytes 1048608 | tf_op jit(solution)/shard_map/ppermute | solution.py:44
  120.1 3.9 %convolution_convert_fusion.7.refs_2_ = bf16[2176,512]{1,0:T(8,128)(2,1)} fusion(bf16[2176,576]{1,0:T(8,128)(2,1)S(1)} %constant_dynamic-slice_fusion, bf16[512,2048]{1,0:T(8,128)(2,1)} %param.17), kind=kOutput, calls=%fused_computation.7 | convolution fusion | flops 1141964800 | bytes 4980736 | tf_op jit(solution)/shard_map/dot_general | solution.py:334
  124.0 3.8 %convolution_convert_fusion.6.refs_4_ = bf16[2176,512]{1,0:T(8,128)(2,1)} fusion(bf16[2176,576]{1,0:T(8,128)(2,1)S(1)} %constant_dynamic-slice_fusion, bf16[512,2048]{1,0:T(8,128)(2,1)} %param.18), kind=kOutput, calls=%fused_computation.6 | convolution fusion | flops 1141964800 | bytes 4980736 | tf_op jit(solution)/shard_map/dot_general | solution.py:343
  127.8 7.3 %shard_map.113 = bf16[128,512]{1,0:T(8,128)(2,1)} custom-call(bf16[4,128,128]{2,1,0:T(8,128)(2,1)} %bitcast.153, bf16[4,128,64]{2,1,0:T(8,128)(2,1)} %bitcast.154, bf16[2176,512]{1,0:T(8,128)(2,1)} %convolution_convert_fusion.7.refs_2_, bf16[2176,64]{1,0:T(8,128)(2,1)} %slice.146.refs_3_, bf16[2176,512]{1,0:T(8,128)(2,1)} %convolution_convert_fusion.6.refs_4_, ...), custom_call_target="tpu_custom_call" | custom-call | flops 713031680 | bytes 5849088 | tf_op jit(solution)/shard_map/pallas_call | solution.py:289
  135.1 7.8 %collective-permute-done.1 = bf16[16,128,256]{1,2,0:T(8,128)(2,1)} collective-permute-done((bf16[16,128,256]{1,2,0:T(8,128)(2,1)}, bf16[16,128,256]{1,2,0:T(8,128)(2,1)}, u32[]{:S(2)}, u32[]{:S(2)}) %collective-permute-start.1) | collective-permute-done | bytes 1048608 | tf_op jit(solution)/shard_map/ppermute | solution.py:44
  146.6 4.0 %collective-permute-start.2 = (bf16[16,128,256]{1,2,0:T(8,128)(2,1)}, bf16[16,128,256]{1,2,0:T(8,128)(2,1)}, u32[]{:S(2)}, u32[]{:S(2)}) collective-permute-start(bf16[16,128,256]{1,2,0:T(8,128)(2,1)} %pad_maximum_fusion.2), channel_id=1, source_target_pairs={{0,32},{8,40},{16,48},{24,56},{32,64},{40,72},{48,80},{56,88},{64,... | collective-permute-start | bytes 3145736 | tf_op jit(solution)/shard_map/ppermute | solution.py:44
  159.7 4.6 %fusion.12 = f32[1,16,64,128]{3,2,1,0:T(8,128)} fusion(f32[2,16,128,128]{2,3,1,0:T(8,128)} %copy-done.12, f32[2,16,64,128]{3,2,1,0:T(8,128)} %fusion.80, f32[2,16,64,128]{3,2,1,0:T(8,128)} %convolution_subtract_fusion), kind=kOutput, calls=%fused_computation.33 | convolution fusion | flops 201457664 | bytes 2621440 | tf_op jit(solution)/shard_map/cor,crm->com/dot_general | solution.py:173
  166.2 3.8 %convolution_convert_fusion.5.refs_2_ = bf16[2176,512]{1,0:T(8,128)(2,1)} fusion(bf16[2176,576]{1,0:T(8,128)(2,1)S(1)} %copy-done.9, bf16[512,2048]{1,0:T(8,128)(2,1)} %param.17), kind=kOutput, calls=%fused_computation.5 | convolution fusion | flops 1141964800 | bytes 4980736 | tf_op jit(solution)/shard_map/dot_general | solution.py:334
  169.9 3.8 %convolution_convert_fusion.4.refs_4_ = bf16[2176,512]{1,0:T(8,128)(2,1)} fusion(bf16[2176,576]{1,0:T(8,128)(2,1)S(1)} %copy-done.9, bf16[512,2048]{1,0:T(8,128)(2,1)} %param.18), kind=kOutput, calls=%fused_computation.4 | convolution fusion | flops 1141964800 | bytes 4980736 | tf_op jit(solution)/shard_map/dot_general | solution.py:343
  173.7 7.3 %shard_map.114 = bf16[128,512]{1,0:T(8,128)(2,1)} custom-call(bf16[4,128,128]{2,1,0:T(8,128)(2,1)} %bitcast.159, bf16[4,128,64]{2,1,0:T(8,128)(2,1)} %bitcast.160, bf16[2176,512]{1,0:T(8,128)(2,1)} %convolution_convert_fusion.5.refs_2_, bf16[2176,64]{1,0:T(8,128)(2,1)} %slice.154.refs_3_, bf16[2176,512]{1,0:T(8,128)(2,1)} %convolution_convert_fusion.4.refs_4_, ...), custom_call_target="tpu_custom_call" | custom-call | flops 713031680 | bytes 5849088 | tf_op jit(solution)/shard_map/pallas_call | solution.py:289
  191.8 3.3 %collective-permute-start.3 = (bf16[16,128,128]{1,2,0:T(8,128)(2,1)}, bf16[16,128,128]{1,2,0:T(8,128)(2,1)}, u32[]{:S(2)}, u32[]{:S(2)}) collective-permute-start(bf16[16,128,128]{1,2,0:T(8,128)(2,1)} %get-tuple-element.26), channel_id=1, source_target_pairs={{0,64},{8,72},{16,80},{24,88},{32,96},{40,104},{48,112},{56,120},{... | collective-permute-start | bytes 1572872 | tf_op jit(solution)/shard_map/ppermute | solution.py:44
  195.1 3.8 %convolution_convert_fusion.3.refs_2_ = bf16[2176,512]{1,0:T(8,128)(2,1)} fusion(bf16[2176,576]{1,0:T(8,128)(2,1)S(1)} %copy-done.10, bf16[512,2048]{1,0:T(8,128)(2,1)} %param.17), kind=kOutput, calls=%fused_computation.3 | convolution fusion | flops 1141964800 | bytes 4980736 | tf_op jit(solution)/shard_map/dot_general | solution.py:334
  199.7 3.8 %convolution_convert_fusion.2.refs_4_ = bf16[2176,512]{1,0:T(8,128)(2,1)} fusion(bf16[2176,576]{1,0:T(8,128)(2,1)S(1)} %copy-done.10, bf16[512,2048]{1,0:T(8,128)(2,1)} %param.18), kind=kOutput, calls=%fused_computation.2 | convolution fusion | flops 1141964800 | bytes 4980736 | tf_op jit(solution)/shard_map/dot_general | solution.py:343
  203.5 7.4 %shard_map.115 = bf16[128,512]{1,0:T(8,128)(2,1)} custom-call(bf16[4,128,128]{2,1,0:T(8,128)(2,1)} %bitcast.157, bf16[4,128,64]{2,1,0:T(8,128)(2,1)} %bitcast.158, bf16[2176,512]{1,0:T(8,128)(2,1)} %convolution_convert_fusion.3.refs_2_, bf16[2176,64]{1,0:T(8,128)(2,1)} %slice.162.refs_3_, bf16[2176,512]{1,0:T(8,128)(2,1)} %convolution_convert_fusion.2.refs_4_, ...), custom_call_target="tpu_custom_call" | custom-call | flops 713031680 | bytes 5849088 | tf_op jit(solution)/shard_map/pallas_call | solution.py:289
  210.9 7.1 %collective-permute-done.3 = bf16[16,128,128]{1,2,0:T(8,128)(2,1)} collective-permute-done((bf16[16,128,128]{1,2,0:T(8,128)(2,1)}, bf16[16,128,128]{1,2,0:T(8,128)(2,1)}, u32[]{:S(2)}, u32[]{:S(2)}) %collective-permute-start.3) | collective-permute-done | bytes 524320 | tf_op jit(solution)/shard_map/ppermute | solution.py:44
  221.1 10.0 %collective-permute-start.4 = (bf16[16,128,128]{1,2,0:T(8,128)(2,1)}, bf16[16,128,128]{1,2,0:T(8,128)(2,1)S(1)}, u32[]{:S(2)}, u32[]{:S(2)}) collective-permute-start(bf16[16,128,128]{1,2,0:T(8,128)(2,1)} %fusion.11), channel_id=1, source_target_pairs={{0,8},{8,16},{16,24},{24,32},{32,40},{40,48},{48,56},{56,64},{64,7... | collective-permute-start | bytes 1572872 | tf_op jit(solution)/shard_map/ppermute | solution.py:44
  231.1 3.8 %convolution_convert_fusion.1.refs_2_ = bf16[2176,512]{1,0:T(8,128)(2,1)} fusion(bf16[2176,576]{1,0:T(8,128)(2,1)S(1)} %copy-done.11, bf16[512,2048]{1,0:T(8,128)(2,1)} %param.17), kind=kOutput, calls=%fused_computation.1 | convolution fusion | flops 1141964800 | bytes 4980736 | tf_op jit(solution)/shard_map/dot_general | solution.py:334
  235.8 3.8 %convolution_convert_fusion.refs_4_ = bf16[2176,512]{1,0:T(8,128)(2,1)} fusion(bf16[2176,576]{1,0:T(8,128)(2,1)S(1)} %copy-done.11, bf16[512,2048]{1,0:T(8,128)(2,1)} %param.18), kind=kOutput, calls=%fused_computation | convolution fusion | flops 1141964800 | bytes 4980736 | tf_op jit(solution)/shard_map/dot_general | solution.py:343
  239.5 7.4 %shard_map.116 = bf16[128,512]{1,0:T(8,128)(2,1)} custom-call(bf16[4,128,128]{2,1,0:T(8,128)(2,1)} %bitcast.155, bf16[4,128,64]{2,1,0:T(8,128)(2,1)} %bitcast.156, bf16[2176,512]{1,0:T(8,128)(2,1)} %convolution_convert_fusion.1.refs_2_, bf16[2176,64]{1,0:T(8,128)(2,1)} %slice.168.refs_3_, bf16[2176,512]{1,0:T(8,128)(2,1)} %convolution_convert_fusion.refs_4_, ...), custom_call_target="tpu_custom_call" | custom-call | flops 713031680 | bytes 5849088 | tf_op jit(solution)/shard_map/pallas_call | solution.py:289
  (170 shorter events, 98.8 us)
Async XLA Ops:
  7.2 109.9 %all-gather.2.cloned.1.call-start = ((), (), s32[]{:S(2)}) async-start(), calls=%async_computation | async-start | bytes 5406720 | tf_op jit(solution)/shard_map/all_gather | solution.py:311
  47.4 9.5 %copy-start.3 = (f32[2,16,64,128]{3,2,1,0:T(8,128)}, f32[2,16,64,128]{3,2,1,0:T(8,128)S(1)}, u32[]{:S(2)}) copy-start(f32[2,16,64,128]{3,2,1,0:T(8,128)S(1)} %fusion.24) | copy-start | bytes 3145732
  54.1 7.1 %copy-start = (f32[2,16,128,128]{3,2,1,0:T(8,128)}, f32[2,16,128,128]{3,2,1,0:T(8,128)S(1)}, u32[]{:S(2)}) copy-start(f32[2,16,128,128]{3,2,1,0:T(8,128)S(1)} %multiply_subtract_fusion) | copy-start | bytes 6291460
  61.2 11.1 %copy-start.12 = (f32[2,16,128,128]{2,3,1,0:T(8,128)}, f32[2,16,128,128]{2,3,1,0:T(8,128)S(1)}, u32[]{:S(2)}) copy-start(f32[2,16,128,128]{2,3,1,0:T(8,128)S(1)} %fusion.62) | copy-start | bytes 6291460
  61.2 8.6 %copy-start.19 = (bf16[128,2048]{1,0:T(8,128)(2,1)S(1)}, bf16[128,2048]{1,0:T(8,128)(2,1)}, u32[]{:S(2)}) copy-start(bf16[128,2048]{1,0:T(8,128)(2,1)} %param.10) | copy-start | bytes 1572868
  64.8 46.2 %collective-permute-start = (bf16[16,128,256]{1,2,0:T(8,128)(2,1)}, bf16[16,128,256]{1,2,0:T(8,128)(2,1)}, u32[]{:S(2)}, u32[]{:S(2)}) collective-permute-start(bf16[16,128,256]{1,2,0:T(8,128)(2,1)} %pad_maximum_fusion), channel_id=1, source_target_pairs={{0,8},{8,16},{16,24},{24,32},{32,40},{40,48},{48,56},{56,64},{64,7... | collective-permute-start | bytes 3145736 | tf_op jit(solution)/shard_map/ppermute | solution.py:44
  89.6 21.4 %copy-start.16 = (f32[16,128,128]{1,2,0:T(8,128)S(1)}, f32[16,128,128]{1,2,0:T(8,128)}, u32[]{:S(2)}) copy-start(f32[16,128,128]{1,2,0:T(8,128)} %get-tuple-element.44) | copy-start | bytes 3145732
  114.6 28.3 %collective-permute-start.1 = (bf16[16,128,256]{1,2,0:T(8,128)(2,1)}, bf16[16,128,256]{1,2,0:T(8,128)(2,1)}, u32[]{:S(2)}, u32[]{:S(2)}) collective-permute-start(bf16[16,128,256]{1,2,0:T(8,128)(2,1)} %pad_maximum_fusion.1), channel_id=1, source_target_pairs={{0,16},{8,24},{16,32},{24,40},{32,48},{40,56},{48,64},{56,72},{64,... | collective-permute-start | bytes 3145736 | tf_op jit(solution)/shard_map/ppermute | solution.py:44
  119.1 8.7 %copy-start.8 = (bf16[2176,576]{1,0:T(8,128)(2,1)}, bf16[2176,576]{1,0:T(8,128)(2,1)S(1)}, u32[]{:S(2)}) copy-start(bf16[2176,576]{1,0:T(8,128)(2,1)S(1)} %constant_dynamic-slice_fusion) | copy-start | bytes 7520260
  145.1 7.4 %copy-start.2 = (f32[16,128,256]{1,2,0:T(8,128)}, f32[16,128,256]{1,2,0:T(8,128)S(1)}, u32[]{:S(2)}) copy-start(f32[16,128,256]{1,2,0:T(8,128)S(1)} %fusion.40) | copy-start | bytes 6291460
  145.2 5.3 %copy-start.1 = (f32[2,16,128,128]{3,2,1,0:T(8,128)S(1)}, f32[2,16,128,128]{3,2,1,0:T(8,128)}, u32[]{:S(2)}) copy-start(f32[2,16,128,128]{3,2,1,0:T(8,128)} %copy-done) | copy-start | bytes 6291460
  145.2 5.3 %copy-start.15 = (f32[2,16,64,128]{3,2,1,0:T(8,128)S(1)}, f32[2,16,64,128]{3,2,1,0:T(8,128)}, u32[]{:S(2)}) copy-start(f32[2,16,64,128]{3,2,1,0:T(8,128)} %convolution_subtract_fusion) | copy-start | bytes 3145732
  146.6 34.4 %collective-permute-start.2 = (bf16[16,128,256]{1,2,0:T(8,128)(2,1)}, bf16[16,128,256]{1,2,0:T(8,128)(2,1)}, u32[]{:S(2)}, u32[]{:S(2)}) collective-permute-start(bf16[16,128,256]{1,2,0:T(8,128)(2,1)} %pad_maximum_fusion.2), channel_id=1, source_target_pairs={{0,32},{8,40},{16,48},{24,56},{32,64},{40,72},{48,80},{56,88},{64,... | collective-permute-start | bytes 3145736 | tf_op jit(solution)/shard_map/ppermute | solution.py:44
  159.7 6.5 %copy-start.9 = (bf16[2176,576]{1,0:T(8,128)(2,1)S(1)}, bf16[2176,576]{1,0:T(8,128)(2,1)}, u32[]{:S(2)}) copy-start(bf16[2176,576]{1,0:T(8,128)(2,1)} %copy-done.8) | copy-start | bytes 7520260
  188.6 6.5 %copy-start.10 = (bf16[2176,576]{1,0:T(8,128)(2,1)S(1)}, bf16[2176,576]{1,0:T(8,128)(2,1)}, u32[]{:S(2)}) copy-start(bf16[2176,576]{1,0:T(8,128)(2,1)} %copy-done.8) | copy-start | bytes 7520260
  191.8 26.3 %collective-permute-start.3 = (bf16[16,128,128]{1,2,0:T(8,128)(2,1)}, bf16[16,128,128]{1,2,0:T(8,128)(2,1)}, u32[]{:S(2)}, u32[]{:S(2)}) collective-permute-start(bf16[16,128,128]{1,2,0:T(8,128)(2,1)} %get-tuple-element.26), channel_id=1, source_target_pairs={{0,64},{8,72},{16,80},{24,88},{32,96},{40,104},{48,112},{56,120},{... | collective-permute-start | bytes 1572872 | tf_op jit(solution)/shard_map/ppermute | solution.py:44
  203.5 14.6 %copy-start.14 = (f32[16,128,256]{2,1,0:T(8,128)S(1)}, f32[16,128,256]{2,1,0:T(8,128)}, u32[]{:S(2)}) copy-start(f32[16,128,256]{2,1,0:T(8,128)} %copy-done.13) | copy-start | bytes 6291460
  203.5 14.6 %copy-start.17 = (f32[16,128,128]{1,2,0:T(8,128)S(1)}, f32[16,128,128]{1,2,0:T(8,128)}, u32[]{:S(2)}) copy-start(f32[16,128,128]{1,2,0:T(8,128)} %get-tuple-element.27) | copy-start | bytes 3145732
  210.9 20.2 %copy-start.11 = (bf16[2176,576]{1,0:T(8,128)(2,1)S(1)}, bf16[2176,576]{1,0:T(8,128)(2,1)}, u32[]{:S(2)}) copy-start(bf16[2176,576]{1,0:T(8,128)(2,1)} %copy-done.8) | copy-start | bytes 7520260
  221.1 25.9 %collective-permute-start.4 = (bf16[16,128,128]{1,2,0:T(8,128)(2,1)}, bf16[16,128,128]{1,2,0:T(8,128)(2,1)S(1)}, u32[]{:S(2)}, u32[]{:S(2)}) collective-permute-start(bf16[16,128,128]{1,2,0:T(8,128)(2,1)} %fusion.11), channel_id=1, source_target_pairs={{0,8},{8,16},{16,24},{24,32},{32,40},{40,48},{48,56},{56,64},{64,7... | collective-permute-start | bytes 1572872 | tf_op jit(solution)/shard_map/ppermute | solution.py:44
  239.5 7.5 %slice-start = ((f32[2,16,64,128]{3,2,1,0:T(8,128)}), f32[1,16,64,128]{3,2,1,0:T(8,128)S(1)}, s32[]{:S(2)}) async-start(f32[2,16,64,128]{3,2,1,0:T(8,128)} %convolution_subtract_fusion), calls=%async_computation.1 | async-start | bytes 1048576 | tf_op jit(solution)/shard_map/slice | solution.py:189
  239.5 7.5 %slice-start.1 = ((f32[2,16,64,128]{3,2,1,0:T(8,128)}), f32[1,16,64,128]{3,2,1,0:T(8,128)S(1)}, s32[]{:S(2)}) async-start(f32[2,16,64,128]{3,2,1,0:T(8,128)} %fusion.80), calls=%async_computation.2 | async-start | bytes 1048576 | tf_op jit(solution)/shard_map/slice | solution.py:189
  239.5 7.5 %copy-start.20 = (f32[1,16,64,128]{3,2,1,0:T(8,128)S(1)}, f32[1,16,64,128]{3,2,1,0:T(8,128)}, u32[]{:S(2)}) copy-start(f32[1,16,64,128]{3,2,1,0:T(8,128)} %fusion.12) | copy-start | bytes 1572868
  239.5 7.5 %copy-start.21 = (f32[1,16,64,128]{3,2,1,0:T(8,128)S(1)}, f32[1,16,64,128]{3,2,1,0:T(8,128)}, u32[]{:S(2)}) copy-start(f32[1,16,64,128]{3,2,1,0:T(8,128)} %convolution_bitcast_fusion.1) | copy-start | bytes 1572868
  (14 other events, 38.1 us)
Sparse Core Ops, SparseCore 0:
  11.2 100.0 all-gather.1

commit v7 on v6

--- a/solution.py
+++ b/solution.py
@@ -82,7 +82,7 @@
     strictly_lower = (
         jnp.where(strict[None], inner_prod, 0.0) * jnp.transpose(write_gain)[:, :, None]
     )
-    inverse = unit_lower_inverse(strictly_lower)
+    inverse = lax.optimization_barrier(unit_lower_inverse(strictly_lower))
     value_rhs = jnp.transpose(valvec * write_gain[:, :, None], (1, 0, 2))
     key_rhs = jnp.transpose(key_plus * (write_gain * follow[:, None])[:, :, None], (1, 0, 2))
     value_solution = jnp.einsum("hts,hsv->htv", inverse, value_rhs, precision=PRECISE_PRODUCT)
@@ -196,10 +196,12 @@
         output_blocks.append(output_current)
     effective_everything = jnp.stack(effective_blocks)
     output_everything = jnp.stack(output_blocks)
-    attend_group, group_count = latent_attention(
+    attend_group, group_count, latents_ready = latent_attention(
         mla_query, latents, key_up, value_up, positions, docids, doc_starts, head_count
     )
-    carried_in, mla_parts = incoming_state(slab_pair, slab_rows, attend_group, group_count)
+    carried_in, mla_parts = incoming_state(
+        slab_pair, slab_rows, attend_group, group_count, latents_ready
+    )
     delta_attention_complete = output_everything + jnp.einsum(
         "enzx,nxu->enzu", effective_everything, carried_in, precision=PRECISE_PRODUCT
     )
@@ -225,17 +227,20 @@
     return rounds
 
 
-def incoming_state(slab_pair, slab_rows, attend_group, group_count):
+def incoming_state(slab_pair, slab_rows, attend_group, group_count, latents_ready):
     map_now, add_now = slab_pair
     window = window_slabs_of(slab_rows)
     rounds = carry_rounds(slab_rows)
     groups_at = [[] for _ in range(rounds)]
     for group in range(group_count):
-        groups_at[rounds - group_count + group if rounds > group_count else group * rounds // group_count].append(group)
+        groups_at[group * rounds // group_count].append(group)
     parts = []
 
     def exchange(value, distance, step):
-        sent = lax.optimization_barrier(value.astype(jnp.bfloat16))
+        sent = value.astype(jnp.bfloat16)
+        if step == 0:
+            sent = latents_ready(sent)
+        sent = lax.optimization_barrier(sent)
         got = shifted(sent, "ctx", distance)
         done = [attend_group(group, sent) for group in groups_at[step]]
         got, done = lax.optimization_barrier((got, done))
@@ -360,7 +365,10 @@
             score_scale,
         )
 
-    return attend_group, group_count
+    def latents_ready(value):
+        return lax.optimization_barrier((key_rows, value))[1]
+
+    return attend_group, group_count, latents_ready
 
 
 def solution(mesh):

time: 262 us -> 258 us (0.985)
  the two profiles are of different devices: /device:TPU:102 before, /device:TPU:96 now
where the time goes in v7:
time: 258 us; the launch traced here: 254 us
  matrix products  102 us (40%)
  local copies, waits for them, and re-layouts  40.3 us (16%)
  waiting for transfers between devices  36.8 us (14%)
  Pallas kernels  29.3 us (11%)
  other arithmetic  15.5 us (6%)
  between operations  15.2 us (6%)
  starting transfers between devices  14.5 us (6%)
    pallas_call x4, Pallas kernels, attend_kernel(): pl.pallas_call(lambda *refs: attend_body(scale, *refs), out_shape=jax.Sha...  29.3 us
    unnamed x106, local copies, waits for them, and re-layouts  26.5 us
    ppermute x5, waiting for transfers between devices, shifted(): return lax.ppermute(block, axis, route)  20.4 us
    dot_general x5, matrix products, unit_lower_inverse(): jnp.einsum('hij,hjk->hik', result, identity + power_term, precision=PRECI...  18 us
    dot_general x4, matrix products, attend_group(): jnp.dot(latent_part, key_up[:, group * per_group * NOPE:(group + 1) * per...  16.9 us
    all_gather x1, waiting for transfers between devices, latent_attention(): everything = lax.all_gather(latents, 'ctx', tiled=True)  16.3 us
    dot_general x4, matrix products, attend_group(): jnp.dot(latent_part, value_up[:, group * per_group * value_width:(group +...  15 us
    ppermute x5, starting transfers between devices, shifted(): return lax.ppermute(block, axis, route)  14.4 us
  transfers between devices with their start and end apart: 6, of which 5 were waited for; matrix products, arithmetic and copies ran while one was open for 50% of the time, Pallas kernels for 12%

profile of v7, /device:TPU:96, one launch (start us, length us, event | category | flops | bytes accessed | tf_op | source)
XLA Modules:
  0.0 254.0 jit_solution(17701187369840622393)
XLA Ops:
  15.0 3.3 %fusion.9 = f32[2,16,64,64]{3,2,1,0:T(8,128)S(1)} fusion(f32[2,16,64]{2,1,0:T(8,128)S(1)} %get-tuple-element.39, pred[2,64,64]{2,1,0:T(8,128)(4,1)S(1)} %get-tuple-element.44, f32[2,64,16,128]{3,2,1,0:T(8,128)S(1)} %bitcast.139, f32[2,64,16]{1,2,0:T(8,128)S(1)} %copy.159, f32[2,64,16,128]{3,2,1,0:T(8,128)S(1)} %fusion.16), kind=kOutput, calls=%fused_computation.24 | convolution fusion | flops 202899456 | bytes 2646016 | tf_op jit(solution)/shard_map/vmap(thk,shk->hts)/dot_general | solution.py:81
  29.1 13.2 %fusion.79 = f32[2,16,64,64]{3,2,1,0:T(8,128)S(1)} fusion(f32[2,16,64,64]{3,2,1,0:T(8,128)S(1)} %fusion.28, f32[2,16,64,64]{3,2,1,0:T(8,128)S(1)} %convolution_add_fusion.2), kind=kOutput, calls=%fused_computation.147 | convolution fusion | flops 100663296 | bytes 1572864 | tf_op jit(solution)/shard_map/vmap(hij,hjk->hik)/dot_general | solution.py:63
  63.0 4.7 %multiply_subtract_fusion = f32[2,16,128,128]{3,2,1,0:T(8,128)S(1)} fusion(f32[2,16,64,128]{3,2,1,0:T(8,128)S(1)} %fusion.22, f32[128,128]{1,0:T(8,128)S(1)} %fusion.63, f32[2,16,128]{2,1,0:T(8,128)S(1)} %bitcast.162, f32[2]{0:T(128)S(1)} %slice_reduce_fusion, f32[2,64,16,128]{3,2,1,0:T(8,128)S(1)} %fusion.16, f32[2,64,16,128]{3,2,1,0:T(8,128)S(1)} %bitcast.141, ...), kind=kOutput, calls=%fused_computation.8 | convolution fusion | flops 405274624 | bytes 5349896 | tf_op jit(solution)/shard_map/vmap(shk,hsj->hkj)/dot_general | solution.py:105
  70.6 4.2 %fusion.62 = f32[2,16,128,128]{2,3,1,0:T(8,128)S(1)} fusion(f32[2,16,64,128]{3,2,1,0:T(8,128)S(1)} %fusion.24, f32[2,64,16,128]{3,2,1,0:T(8,128)S(1)} %fusion.16, f32[2,64,16,128]{3,2,1,0:T(8,128)S(1)} %bitcast.142, f32[2,64]{1,0:T(2,128)S(1)} %copy-done.35, f32[2,16,128]{2,1,0:T(8,128)S(1)} %slice_bitcast_fusion.14, f32[2,64,16]{1,2,0:T(8,128)S(1)} %copy.159), kind=kOutput, calls=%fused_computation.107 | convolution fusion | flops 403701760 | bytes 5267968 | tf_op jit(solution)/shard_map/vmap(omt,mor->mtr)/dot_general | solution.py:108
  74.9 3.5 %fusion.74 = (bf16[16,128,128]{1,2,0:T(8,128)(2,1)S(1)}, f32[16,128,128]{1,2,0:T(8,128)}) fusion(f32[2,16,128,128]{2,3,1,0:T(8,128)S(1)} %fusion.62, f32[2,16,128,128]{3,2,1,0:T(8,128)S(1)} %multiply_subtract_fusion), kind=kOutput, calls=%fused_computation.142 | convolution fusion | flops 403177472 | bytes 4718592 | tf_op jit(solution)/shard_map/ytn,yne->yte/dot_general | solution.py:180
  80.7 16.3 %all-gather.2.cloned.1.call-done = bf16[4096,576]{1,0:T(8,128)(2,1)} async-done(((bf16[128,576]{1,0:T(8,128)(2,1)}), bf16[4096,576]{1,0:T(8,128)(2,1)}) %all-gather.2.cloned.1.call-update) | async-done | bytes 4718608 | tf_op jit(solution)/shard_map/all_gather | solution.py:316
  101.3 3.7 %convolution_select_fusion.1 = f32[2,16,64,64]{3,2,1,0:T(8,128)} fusion(pred[2,64,64]{2,1,0:T(8,128)(4,1)S(1)} %get-tuple-element.43, f32[2,64,16,128]{3,2,1,0:T(8,128)S(1)} %bitcast.144, f32[2,64,16]{1,2,0:T(8,128)S(1)} %copy.155, f32[2,64,16,128]{3,2,1,0:T(8,128)S(1)} %fusion.16, f32[2,64,16,128]{3,2,1,0:T(8,128)S(1)} %bitcast.143, ...), kind=kOutput, calls=%fused_computation.25 | convolution fusion | flops 202768384 | bytes 3694592 | tf_op jit(solution)/shard_map/vmap(thk,shk->hts)/dot_general | solution.py:92
  105.8 3.8 %convolution_convert_fusion.7.refs_2_ = bf16[2176,512]{1,0:T(8,128)(2,1)} fusion(bf16[2176,576]{1,0:T(8,128)(2,1)S(1)} %constant_dynamic-slice_fusion, bf16[512,2048]{1,0:T(8,128)(2,1)} %param.17), kind=kOutput, calls=%fused_computation.7 | convolution fusion | flops 1141964800 | bytes 4980736 | tf_op jit(solution)/shard_map/dot_general | solution.py:339
  109.6 3.7 %convolution_convert_fusion.6.refs_4_ = bf16[2176,512]{1,0:T(8,128)(2,1)} fusion(bf16[2176,576]{1,0:T(8,128)(2,1)S(1)} %constant_dynamic-slice_fusion, bf16[512,2048]{1,0:T(8,128)(2,1)} %param.18), kind=kOutput, calls=%fused_computation.6 | convolution fusion | flops 1141964800 | bytes 4980736 | tf_op jit(solution)/shard_map/dot_general | solution.py:348
  113.4 7.3 %shard_map.113 = bf16[128,512]{1,0:T(8,128)(2,1)} custom-call(bf16[4,128,128]{2,1,0:T(8,128)(2,1)} %bitcast.153, bf16[4,128,64]{2,1,0:T(8,128)(2,1)} %bitcast.154, bf16[2176,512]{1,0:T(8,128)(2,1)} %convolution_convert_fusion.7.refs_2_, bf16[2176,64]{1,0:T(8,128)(2,1)} %slice.144.refs_3_, bf16[2176,512]{1,0:T(8,128)(2,1)} %convolution_convert_fusion.6.refs_4_, ...), custom_call_target="tpu_custom_call" | custom-call | flops 713031680 | bytes 5849088 | tf_op jit(solution)/shard_map/pallas_call | solution.py:294
  120.7 5.2 %collective-permute-done = bf16[16,128,256]{1,2,0:T(8,128)(2,1)} collective-permute-done((bf16[16,128,256]{1,2,0:T(8,128)(2,1)}, bf16[16,128,256]{1,2,0:T(8,128)(2,1)}, u32[]{:S(2)}, u32[]{:S(2)}) %collective-permute-start) | collective-permute-done | bytes 1048608 | tf_op jit(solution)/shard_map/ppermute | solution.py:44
  139.6 4.6 %convolution_convert_fusion.5.refs_2_ = bf16[2176,512]{1,0:T(8,128)(2,1)} fusion(bf16[2176,576]{1,0:T(8,128)(2,1)} %copy-done.14, bf16[512,2048]{1,0:T(8,128)(2,1)} %param.17), kind=kOutput, calls=%fused_computation.5 | convolution fusion | flops 1141964800 | bytes 4980736 | tf_op jit(solution)/shard_map/dot_general | solution.py:339
  144.2 3.7 %convolution_convert_fusion.4.refs_4_ = bf16[2176,512]{1,0:T(8,128)(2,1)} fusion(bf16[2176,576]{1,0:T(8,128)(2,1)S(1)} %copy-done.15, bf16[512,2048]{1,0:T(8,128)(2,1)} %param.18), kind=kOutput, calls=%fused_computation.4 | convolution fusion | flops 1141964800 | bytes 4980736 | tf_op jit(solution)/shard_map/dot_general | solution.py:348
  148.0 7.3 %shard_map.114 = bf16[128,512]{1,0:T(8,128)(2,1)} custom-call(bf16[4,128,128]{2,1,0:T(8,128)(2,1)} %bitcast.159, bf16[4,128,64]{2,1,0:T(8,128)(2,1)} %bitcast.160, bf16[2176,512]{1,0:T(8,128)(2,1)} %convolution_convert_fusion.5.refs_2_, bf16[2176,64]{1,0:T(8,128)(2,1)} %slice.152.refs_3_, bf16[2176,512]{1,0:T(8,128)(2,1)} %convolution_convert_fusion.4.refs_4_, ...), custom_call_target="tpu_custom_call" | custom-call | flops 713031680 | bytes 5849088 | tf_op jit(solution)/shard_map/pallas_call | solution.py:294
  160.8 5.8 %collective-permute-start.2 = (bf16[16,128,256]{1,2,0:T(8,128)(2,1)}, bf16[16,128,256]{1,2,0:T(8,128)(2,1)}, u32[]{:S(2)}, u32[]{:S(2)}) collective-permute-start(bf16[16,128,256]{1,2,0:T(8,128)(2,1)} %pad_maximum_fusion.2), channel_id=1, source_target_pairs={{0,32},{8,40},{16,48},{24,56},{32,64},{40,72},{48,80},{56,88},{64,... | collective-permute-start | bytes 3145736 | tf_op jit(solution)/shard_map/ppermute | solution.py:44
  175.5 4.6 %convolution_convert_fusion.3.refs_2_ = bf16[2176,512]{1,0:T(8,128)(2,1)} fusion(bf16[2176,576]{1,0:T(8,128)(2,1)} %copy-done.14, bf16[512,2048]{1,0:T(8,128)(2,1)} %param.17), kind=kOutput, calls=%fused_computation.3 | convolution fusion | flops 1141964800 | bytes 4980736 | tf_op jit(solution)/shard_map/dot_general | solution.py:339
  180.1 3.7 %convolution_convert_fusion.2.refs_4_ = bf16[2176,512]{1,0:T(8,128)(2,1)} fusion(bf16[2176,576]{1,0:T(8,128)(2,1)S(1)} %copy-done.16, bf16[512,2048]{1,0:T(8,128)(2,1)} %param.18), kind=kOutput, calls=%fused_computation.2 | convolution fusion | flops 1141964800 | bytes 4980736 | tf_op jit(solution)/shard_map/dot_general | solution.py:348
  183.8 7.3 %shard_map.115 = bf16[128,512]{1,0:T(8,128)(2,1)} custom-call(bf16[4,128,128]{2,1,0:T(8,128)(2,1)} %bitcast.157, bf16[4,128,64]{2,1,0:T(8,128)(2,1)} %bitcast.158, bf16[2176,512]{1,0:T(8,128)(2,1)} %convolution_convert_fusion.3.refs_2_, bf16[2176,64]{1,0:T(8,128)(2,1)} %slice.160.refs_3_, bf16[2176,512]{1,0:T(8,128)(2,1)} %convolution_convert_fusion.2.refs_4_, ...), custom_call_target="tpu_custom_call" | custom-call | flops 713031680 | bytes 5849088 | tf_op jit(solution)/shard_map/pallas_call | solution.py:294
  204.0 3.8 %convolution_convert_fusion.1.refs_2_ = bf16[2176,512]{1,0:T(8,128)(2,1)} fusion(bf16[2176,576]{1,0:T(8,128)(2,1)S(1)} %copy-done.17, bf16[512,2048]{1,0:T(8,128)(2,1)} %param.17), kind=kOutput, calls=%fused_computation.1 | convolution fusion | flops 1141964800 | bytes 4980736 | tf_op jit(solution)/shard_map/dot_general | solution.py:339
  208.6 3.8 %convolution_convert_fusion.refs_4_ = bf16[2176,512]{1,0:T(8,128)(2,1)} fusion(bf16[2176,576]{1,0:T(8,128)(2,1)S(1)} %copy-done.17, bf16[512,2048]{1,0:T(8,128)(2,1)} %param.18), kind=kOutput, calls=%fused_computation | convolution fusion | flops 1141964800 | bytes 4980736 | tf_op jit(solution)/shard_map/dot_general | solution.py:348
  212.4 7.4 %shard_map.116 = bf16[128,512]{1,0:T(8,128)(2,1)} custom-call(bf16[4,128,128]{2,1,0:T(8,128)(2,1)} %bitcast.155, bf16[4,128,64]{2,1,0:T(8,128)(2,1)} %bitcast.156, bf16[2176,512]{1,0:T(8,128)(2,1)} %convolution_convert_fusion.1.refs_2_, bf16[2176,64]{1,0:T(8,128)(2,1)} %slice.168.refs_3_, bf16[2176,512]{1,0:T(8,128)(2,1)} %convolution_convert_fusion.refs_4_, ...), custom_call_target="tpu_custom_call" | custom-call | flops 713031680 | bytes 5849088 | tf_op jit(solution)/shard_map/pallas_call | solution.py:294
  219.8 3.8 %collective-permute-done.3 = bf16[16,128,128]{1,2,0:T(8,128)(2,1)} collective-permute-done((bf16[16,128,128]{1,2,0:T(8,128)(2,1)}, bf16[16,128,128]{1,2,0:T(8,128)(2,1)}, u32[]{:S(2)}, u32[]{:S(2)}) %collective-permute-start.3) | collective-permute-done | bytes 524320 | tf_op jit(solution)/shard_map/ppermute | solution.py:44
  229.7 3.3 %fusion.12 = f32[1,16,64,128]{3,2,1,0:T(8,128)S(1)} fusion(f32[2,16,128,128]{2,3,1,0:T(8,128)S(1)} %copy-done.19, f32[2,16,64,128]{3,2,1,0:T(8,128)} %copy-done.24, f32[2,16,64,128]{3,2,1,0:T(8,128)S(1)} %copy-done.23), kind=kOutput, calls=%fused_computation.33 | convolution fusion | flops 201457664 | bytes 2621440 | tf_op jit(solution)/shard_map/cor,crm->com/dot_general | solution.py:173
  233.8 10.5 %collective-permute-done.4 = bf16[16,128,128]{1,2,0:T(8,128)(2,1)S(1)} collective-permute-done((bf16[16,128,128]{1,2,0:T(8,128)(2,1)S(1)}, bf16[16,128,128]{1,2,0:T(8,128)(2,1)S(1)}, u32[]{:S(2)}, u32[]{:S(2)}) %collective-permute-start.4) | collective-permute-done | bytes 524320 | tf_op jit(solution)/shard_map/ppermute | solution.py:44
  (198 shorter events, 100.0 us)
Async XLA Ops:
  7.2 89.9 %all-gather.2.cloned.1.call-start = ((), (), s32[]{:S(2)}) async-start(), calls=%async_computation | async-start | bytes 5406720 | tf_op jit(solution)/shard_map/all_gather | solution.py:316
  29.1 13.3 %copy-start.27 = (bf16[128,2048]{1,0:T(8,128)(2,1)S(1)}, bf16[128,2048]{1,0:T(8,128)(2,1)}, u32[]{:S(2)}) copy-start(bf16[128,2048]{1,0:T(8,128)(2,1)} %param.12) | copy-start | bytes 1572868
  48.3 9.1 %copy-start.33 = (f32[2,64]{1,0:T(2,128)S(1)}, f32[2,64]{1,0:T(2,128)}, u32[]{:S(2)}) copy-start(f32[2,64]{1,0:T(2,128)} %copy-done.32) | copy-start | bytes 1540
  48.3 9.3 %copy-start.42 = (s32[8]{0:T(128)S(1)}, s32[8]{0:T(128)}, u32[]{:S(2)}) copy-start(s32[8]{0:T(128)} %copy-done.41) | copy-start | bytes 100
  60.4 10.2 %copy-start.6 = (f32[2,16,64,128]{3,2,1,0:T(8,128)}, f32[2,16,64,128]{3,2,1,0:T(8,128)S(1)}, u32[]{:S(2)}) copy-start(f32[2,16,64,128]{3,2,1,0:T(8,128)S(1)} %fusion.24) | copy-start | bytes 3145732
  67.7 7.1 %copy-start = (f32[2,16,128,128]{3,2,1,0:T(8,128)}, f32[2,16,128,128]{3,2,1,0:T(8,128)S(1)}, u32[]{:S(2)}) copy-start(f32[2,16,128,128]{3,2,1,0:T(8,128)S(1)} %multiply_subtract_fusion) | copy-start | bytes 6291460
  80.7 20.5 %copy-start.10 = (f32[16,8,16,128]{3,2,1,0:T(8,128)S(1)}, f32[16,8,16,128]{3,2,1,0:T(8,128)}, u32[]{:S(2)}) copy-start(f32[16,8,16,128]{3,2,1,0:T(8,128)} %copy.217) | copy-start | bytes 3145732
  99.1 10.6 %copy-start.14 = (bf16[2176,576]{1,0:T(8,128)(2,1)}, bf16[2176,576]{1,0:T(8,128)(2,1)S(1)}, u32[]{:S(2)}) copy-start(bf16[2176,576]{1,0:T(8,128)(2,1)S(1)} %constant_dynamic-slice_fusion) | copy-start | bytes 7520260
  99.1 26.8 %collective-permute-start = (bf16[16,128,256]{1,2,0:T(8,128)(2,1)}, bf16[16,128,256]{1,2,0:T(8,128)(2,1)}, u32[]{:S(2)}, u32[]{:S(2)}) collective-permute-start(bf16[16,128,256]{1,2,0:T(8,128)(2,1)} %pad_maximum_fusion), channel_id=1, source_target_pairs={{0,8},{8,16},{16,24},{24,32},{32,40},{40,48},{48,56},{56,64},{64,7... | collective-permute-start | bytes 3145736 | tf_op jit(solution)/shard_map/ppermute | solution.py:44
  129.9 26.2 %collective-permute-start.1 = (bf16[16,128,256]{1,2,0:T(8,128)(2,1)}, bf16[16,128,256]{1,2,0:T(8,128)(2,1)}, u32[]{:S(2)}, u32[]{:S(2)}) collective-permute-start(bf16[16,128,256]{1,2,0:T(8,128)(2,1)} %pad_maximum_fusion.1), channel_id=1, source_target_pairs={{0,16},{8,24},{16,32},{24,40},{32,48},{40,56},{48,64},{56,72},{64,... | collective-permute-start | bytes 3145736 | tf_op jit(solution)/shard_map/ppermute | solution.py:44
  158.4 8.1 %copy-start.9 = (f32[2,16,64,64]{3,2,1,0:T(8,128)S(1)}, f32[2,16,64,64]{3,2,1,0:T(8,128)}, u32[]{:S(2)}) copy-start(f32[2,16,64,64]{3,2,1,0:T(8,128)} %convolution_select_fusion.1) | copy-start | bytes 1572868
  158.4 8.1 %copy-start.11 = (f32[16,8,16,128]{3,2,1,0:T(8,128)S(1)}, f32[16,8,16,128]{3,2,1,0:T(8,128)}, u32[]{:S(2)}) copy-start(f32[16,8,16,128]{3,2,1,0:T(8,128)} %copy.217) | copy-start | bytes 3145732
  158.5 8.1 %copy-start.13 = (f32[2,16,64,128]{3,2,1,0:T(8,128)S(1)}, f32[2,16,64,128]{3,2,1,0:T(8,128)}, u32[]{:S(2)}) copy-start(f32[2,16,64,128]{3,2,1,0:T(8,128)} %copy-done.12) | copy-start | bytes 3145732
  158.5 8.1 %copy-start.34 = (f32[2,64]{1,0:T(2,128)S(1)}, f32[2,64]{1,0:T(2,128)}, u32[]{:S(2)}) copy-start(f32[2,64]{1,0:T(2,128)} %copy-done.32) | copy-start | bytes 1540
  160.8 30.4 %collective-permute-start.2 = (bf16[16,128,256]{1,2,0:T(8,128)(2,1)}, bf16[16,128,256]{1,2,0:T(8,128)(2,1)}, u32[]{:S(2)}, u32[]{:S(2)}) collective-permute-start(bf16[16,128,256]{1,2,0:T(8,128)(2,1)} %pad_maximum_fusion.2), channel_id=1, source_target_pairs={{0,32},{8,40},{16,48},{24,56},{32,64},{40,72},{48,80},{56,88},{64,... | collective-permute-start | bytes 3145736 | tf_op jit(solution)/shard_map/ppermute | solution.py:44
  201.8 21.8 %collective-permute-start.3 = (bf16[16,128,128]{1,2,0:T(8,128)(2,1)}, bf16[16,128,128]{1,2,0:T(8,128)(2,1)}, u32[]{:S(2)}, u32[]{:S(2)}) collective-permute-start(bf16[16,128,128]{1,2,0:T(8,128)(2,1)} %get-tuple-element.28), channel_id=1, source_target_pairs={{0,64},{8,72},{16,80},{24,88},{32,96},{40,104},{48,112},{56,120},{... | collective-permute-start | bytes 1572872 | tf_op jit(solution)/shard_map/ppermute | solution.py:44
  212.4 11.3 %copy-start.21 = (f32[16,128,256]{2,1,0:T(8,128)S(1)}, f32[16,128,256]{2,1,0:T(8,128)}, u32[]{:S(2)}) copy-start(f32[16,128,256]{2,1,0:T(8,128)} %copy-done.20) | copy-start | bytes 6291460
  219.8 8.7 %copy-start.1 = (f32[2,16,128,128]{3,2,1,0:T(8,128)S(1)}, f32[2,16,128,128]{3,2,1,0:T(8,128)}, u32[]{:S(2)}) copy-start(f32[2,16,128,128]{3,2,1,0:T(8,128)} %copy-done) | copy-start | bytes 6291460
  219.8 8.7 %copy-start.23 = (f32[2,16,64,128]{3,2,1,0:T(8,128)S(1)}, f32[2,16,64,128]{3,2,1,0:T(8,128)}, u32[]{:S(2)}) copy-start(f32[2,16,64,128]{3,2,1,0:T(8,128)} %copy-done.22) | copy-start | bytes 3145732
  226.4 6.6 %copy-start.28 = (bf16[128,512]{1,0:T(8,128)(2,1)S(1)}, bf16[128,512]{1,0:T(8,128)(2,1)}, u32[]{:S(2)}) copy-start(bf16[128,512]{1,0:T(8,128)(2,1)} %shard_map.113) | copy-start | bytes 393220
  226.4 6.6 %copy-start.29 = (bf16[128,512]{1,0:T(8,128)(2,1)S(1)}, bf16[128,512]{1,0:T(8,128)(2,1)}, u32[]{:S(2)}) copy-start(bf16[128,512]{1,0:T(8,128)(2,1)} %shard_map.114) | copy-start | bytes 393220
  226.4 17.9 %collective-permute-start.4 = (bf16[16,128,128]{1,2,0:T(8,128)(2,1)S(1)}, bf16[16,128,128]{1,2,0:T(8,128)(2,1)S(1)}, u32[]{:S(2)}, u32[]{:S(2)}) collective-permute-start(bf16[16,128,128]{1,2,0:T(8,128)(2,1)S(1)} %fusion.11), channel_id=1, source_target_pairs={{0,8},{8,16},{16,24},{24,32},{32,40},{40,48},{48,56},{56,64},{64,7... | collective-permute-start | bytes 1572872 | tf_op jit(solution)/shard_map/ppermute | solution.py:44
  229.6 14.7 %slice-start = ((f32[2,16,64,128]{3,2,1,0:T(8,128)}), f32[1,16,64,128]{3,2,1,0:T(8,128)S(1)}, s32[]{:S(2)}) async-start(f32[2,16,64,128]{3,2,1,0:T(8,128)} %copy-done.22), calls=%async_computation.1 | async-start | bytes 1048576 | tf_op jit(solution)/shard_map/slice | solution.py:189
  229.7 14.7 %slice-start.1 = ((f32[2,16,64,128]{3,2,1,0:T(8,128)}), f32[1,16,64,128]{3,2,1,0:T(8,128)S(1)}, s32[]{:S(2)}) async-start(f32[2,16,64,128]{3,2,1,0:T(8,128)} %copy-done.24), calls=%async_computation.2 | async-start | bytes 1048576 | tf_op jit(solution)/shard_map/slice | solution.py:189
  (28 other events, 92.6 us)
Sparse Core Ops, SparseCore 0:
  11.2 85.8 all-gather.1

commit v8 on v4

--- a/solution.py
+++ b/solution.py
@@ -199,7 +199,7 @@
     )
     carried_in, mla_parts = incoming_state(slab_pair, slab_rows, attend_group, group_count)
     delta_attention_complete = output_everything + jnp.einsum(
-        "enzx,nxu->enzu", effective_everything, carried_in, precision=PRECISE_PRODUCT
+        "enzx,nxu->enzu", effective_everything, carried_in, precision=lax.Precision.HIGH
     )
     kda_out = (
         jnp.transpose(delta_attention_complete, (0, 2, 1, 3))
@@ -241,7 +241,7 @@
         return got.astype(jnp.float32)
 
     def product(left, right):
-        return jnp.einsum("hkj,hjl->hkl", left, right, precision=PRECISE_PRODUCT)
+        return jnp.einsum("hkj,hjl->hkl", left, right, precision=lax.Precision.HIGH)
 
     value_dim = add_now.shape[2]
     distance, step = 1, 0

time: 247 us -> 249 us (level)
  the two profiles are of different devices: /device:TPU:4 before, /device:TPU:78 now
where the time goes in v8:
time: 249 us; the launch traced here: 244 us
  matrix products  131 us (53%)
  other arithmetic  26.4 us (11%)
  waiting for transfers between devices  25.8 us (10%)
  starting transfers between devices  24.7 us (10%)
  local copies, waits for them, and re-layouts  20.9 us (8%)
  between operations  15.1 us (6%)
    dot_general x4, matrix products, attend_group(): jnp.einsum('hts,shv->thv', weights.astype(jnp.bfloat16), values, preferre...  25.3 us
    ppermute x5, waiting for transfers between devices, shifted(): return lax.ppermute(block, axis, route)  25.1 us
    ppermute x5, starting transfers between devices, shifted(): return lax.ppermute(block, axis, route)  24.7 us
    dot_general x5, matrix products, unit_lower_inverse(): jnp.einsum('hij,hjk->hik', result, identity + power_term, precision=PRECI...  16.8 us
    dot_general x4, matrix products, attend_group(): jnp.dot(latent_part, value_up[:, group * per_group * value_width:(group +...  16.5 us
    unnamed x68, local copies, waits for them, and re-layouts  14.2 us
    dot_general x4, matrix products, attend_group(): jnp.dot(latent_part, key_up[:, group * per_group * NOPE:(group + 1) * per...  10.4 us
    dot_general x4, matrix products, product(): return jnp.einsum('hkj,hjl->hkl', left, right, precision=lax.Precision.HIGH)  9.27 us
  transfers between devices with their start and end apart: 6, of which 4 were waited for; matrix products, arithmetic and copies ran while one was open for 64% of the time, Pallas kernels for 0%

profile of v8, /device:TPU:78, one launch (start us, length us, event | category | flops | bytes accessed | tf_op | source)
XLA Modules:
  0.0 243.9 jit_solution(14221033886436032275)
XLA Ops:
  19.6 3.3 %fusion.45 = f32[2,16,64,64]{3,2,1,0:T(8,128)S(1)} fusion(f32[2,16,64]{2,1,0:T(8,128)S(1)} %get-tuple-element.39, pred[2,64,64]{2,1,0:T(8,128)(4,1)S(1)} %get-tuple-element.44, f32[2,64,16,128]{3,2,1,0:T(8,128)S(1)} %bitcast.236, f32[2,64,16]{1,2,0:T(8,128)S(1)} %copy.187, f32[2,64,16,128]{3,2,1,0:T(8,128)S(1)} %fusion.88), kind=kOutput, calls=%fused_computation.68 | convolution fusion | flops 202899456 | bytes 2646016 | tf_op jit(solution)/shard_map/vmap(thk,shk->hts)/dot_general | solution.py:79
  35.0 12.0 %fusion.177 = f32[2,16,64,64]{3,2,1,0:T(8,128)S(1)} fusion(f32[2,16,64,64]{3,2,1,0:T(8,128)S(1)} %fusion.100, f32[2,16,64,64]{3,2,1,0:T(8,128)S(1)} %convolution_add_fusion.2), kind=kOutput, calls=%fused_computation.229 | convolution fusion | flops 100663296 | bytes 1572864 | tf_op jit(solution)/shard_map/vmap(hij,hjk->hik)/dot_general | solution.py:61
  50.3 4.7 %multiply_subtract_fusion = f32[2,16,128,128]{3,2,1,0:T(8,128)S(1)} fusion(f32[2,16,64,128]{3,2,1,0:T(8,128)S(1)} %fusion.94, f32[128,128]{1,0:T(8,128)S(1)} %fusion.151, f32[2,16,128]{2,1,0:T(8,128)S(1)} %bitcast.262, f32[2]{0:T(128)S(1)} %slice_reduce_fusion, f32[2,64,16,128]{3,2,1,0:T(8,128)S(1)} %fusion.88, f32[2,64,16,128]{3,2,1,0:T(8,128)S(1)} %bitcast.238, ...), kind=kOutput, calls=%fused_computation.52 | convolution fusion | flops 405274624 | bytes 5349896 | tf_op jit(solution)/shard_map/vmap(shk,hsj->hkj)/dot_general | solution.py:103
  55.0 2.9 %fusion.167 = (bf16[16,128,128]{1,2,0:T(8,128)(2,1)S(1)}, f32[16,128,128]{1,2,0:T(8,128)}) fusion(f32[2,16,128,128]{3,2,1,0:T(8,128)S(1)} %multiply_subtract_fusion), kind=kOutput, calls=%fused_computation.219 | convolution fusion | flops 402915328 | bytes 3670016 | tf_op jit(solution)/shard_map/hkj,hjl->hkl/dot_general | solution.py:174
  57.9 4.2 %fusion.146 = f32[2,16,128,128]{2,3,1,0:T(8,128)S(1)} fusion(f32[2,16,64,128]{3,2,1,0:T(8,128)S(1)} %fusion.96, f32[2,64,16,128]{3,2,1,0:T(8,128)S(1)} %fusion.88, f32[2,64,16,128]{3,2,1,0:T(8,128)S(1)} %bitcast.239, f32[2,64]{1,0:T(2,128)S(1)} %get-tuple-element.42, f32[2,16,128]{2,1,0:T(8,128)S(1)} %slice_bitcast_fusion.14, f32[2,64,16]{1,2,0:T(8,128)S(1)} %copy.187), kind=kOutput, calls=%fused_computation.175 | convolution fusion | flops 403701760 | bytes 5267968 | tf_op jit(solution)/shard_map/vmap(omt,mor->mtr)/dot_general | solution.py:106
  65.8 3.7 %collective-permute-start = (bf16[16,128,256]{1,2,0:T(8,128)(2,1)}, bf16[16,128,256]{1,2,0:T(8,128)(2,1)}, u32[]{:S(2)}, u32[]{:S(2)}) collective-permute-start(bf16[16,128,256]{1,2,0:T(8,128)(2,1)} %pad_maximum_fusion), channel_id=1, source_target_pairs={{0,8},{8,16},{16,24},{24,32},{32,40},{40,48},{48,56},{56,64},{64,7... | collective-permute-start | bytes 3145736 | tf_op jit(solution)/shard_map/ppermute | solution.py:42
  75.0 2.9 %convolution_select_fusion.1 = f32[2,16,64,64]{3,2,1,0:T(8,128)S(1)} fusion(pred[2,64,64]{2,1,0:T(8,128)(4,1)S(1)} %get-tuple-element.43, f32[2,64,16,128]{3,2,1,0:T(8,128)S(1)} %bitcast.241, f32[2,64,16]{1,2,0:T(8,128)S(1)} %copy.183, f32[2,64,16,128]{3,2,1,0:T(8,128)S(1)} %fusion.88, f32[2,64,16,128]{3,2,1,0:T(8,128)S(1)} %bitcast.240, ...), kind=kOutput, calls=%fused_computation.69 | convolution fusion | flops 202768384 | bytes 3694592 | tf_op jit(solution)/shard_map/vmap(thk,shk->hts)/dot_general | solution.py:90
  83.1 2.9 %fusion.48 = f32[1,16,64,128]{3,2,1,0:T(8,128)} fusion(f32[2,16,128,128]{2,3,1,0:T(8,128)S(1)} %copy-done.8, f32[2,16,64,128]{3,2,1,0:T(8,128)S(1)} %fusion.178, f32[2,16,64,128]{3,2,1,0:T(8,128)S(1)} %convolution_subtract_fusion), kind=kOutput, calls=%fused_computation.77 | convolution fusion | flops 201457664 | bytes 2621440 | tf_op jit(solution)/shard_map/cor,crm->com/dot_general | solution.py:171
  89.9 16.4 %collective-permute-done = bf16[16,128,256]{1,2,0:T(8,128)(2,1)} collective-permute-done((bf16[16,128,256]{1,2,0:T(8,128)(2,1)}, bf16[16,128,256]{1,2,0:T(8,128)(2,1)}, u32[]{:S(2)}, u32[]{:S(2)}) %collective-permute-start) | collective-permute-done | bytes 1048608 | tf_op jit(solution)/shard_map/ppermute | solution.py:42
  109.8 3.1 %collective-permute-start.1 = (bf16[16,128,256]{1,2,0:T(8,128)(2,1)}, bf16[16,128,256]{1,2,0:T(8,128)(2,1)}, u32[]{:S(2)}, u32[]{:S(2)}) collective-permute-start(bf16[16,128,256]{1,2,0:T(8,128)(2,1)} %pad_maximum_fusion.1), channel_id=1, source_target_pairs={{0,16},{8,24},{16,32},{24,40},{32,48},{40,56},{48,64},{56,72},{64,... | collective-permute-start | bytes 3145736 | tf_op jit(solution)/shard_map/ppermute | solution.py:42
  114.9 2.9 %convolution_convert_fusion.6 = bf16[2176,512]{0,1:T(8,128)(2,1)S(1)} fusion(bf16[2176,576]{0,1:T(8,128)(2,1)S(1)} %constant_dynamic-slice_fusion, bf16[512,2048]{1,0:T(8,128)(2,1)} %param.17), kind=kOutput, calls=%fused_computation.42 | convolution fusion | flops 1141964800 | bytes 4980736 | tf_op jit(solution)/shard_map/dot_general | solution.py:288
  121.4 4.3 %convolution_convert_fusion.7 = bf16[2176,512]{0,1:T(8,128)(2,1)} fusion(bf16[2176,576]{0,1:T(8,128)(2,1)S(1)} %constant_dynamic-slice_fusion, bf16[512,2048]{1,0:T(8,128)(2,1)} %param.18), kind=kOutput, calls=%fused_computation.43 | convolution fusion | flops 1141964800 | bytes 4980736 | tf_op jit(solution)/shard_map/dot_general | solution.py:297
  127.7 5.9 %fusion.83 = bf16[128,4,128]{0,2,1:T(8,128)(2,1)S(1)} fusion(bf16[2176,4,128]{0,2,1:T(8,128)(2,1)} %bitcast.265, f32[128,4]{0,1:T(4,128)} %bitcast.269, f32[4,128,2176]{1,2,0:T(8,128)} %copy-done.17, pred[128,2176]{0,1:T(8,128)(4,1)S(1)} %compare_and_fusion), kind=kOutput, calls=%fused_computation.91 | convolution fusion | flops 288688768 | bytes 7096320 | tf_op jit(solution)/shard_map/hts,shv->thv/dot_general | solution.py:326
  133.6 4.1 %collective-permute-done.1 = bf16[16,128,256]{1,2,0:T(8,128)(2,1)} collective-permute-done((bf16[16,128,256]{1,2,0:T(8,128)(2,1)}, bf16[16,128,256]{1,2,0:T(8,128)(2,1)}, u32[]{:S(2)}, u32[]{:S(2)}) %collective-permute-start.1) | collective-permute-done | bytes 1048608 | tf_op jit(solution)/shard_map/ppermute | solution.py:42
  142.0 3.6 %collective-permute-start.2 = (bf16[16,128,256]{1,2,0:T(8,128)(2,1)}, bf16[16,128,256]{1,2,0:T(8,128)(2,1)}, u32[]{:S(2)}, u32[]{:S(2)}) collective-permute-start(bf16[16,128,256]{1,2,0:T(8,128)(2,1)} %pad_maximum_fusion.2), channel_id=1, source_target_pairs={{0,32},{8,40},{16,48},{24,56},{32,64},{40,72},{48,80},{56,88},{64,... | collective-permute-start | bytes 3145736 | tf_op jit(solution)/shard_map/ppermute | solution.py:42
  151.7 4.3 %convolution_convert_fusion.5 = bf16[2176,512]{0,1:T(8,128)(2,1)} fusion(bf16[2176,576]{0,1:T(8,128)(2,1)S(1)} %copy-done.13, bf16[512,2048]{1,0:T(8,128)(2,1)} %param.18), kind=kOutput, calls=%fused_computation.41 | convolution fusion | flops 1141964800 | bytes 4980736 | tf_op jit(solution)/shard_map/dot_general | solution.py:297
  158.1 6.6 %fusion.80 = bf16[128,4,128]{0,2,1:T(8,128)(2,1)} fusion(bf16[2176,4,128]{0,2,1:T(8,128)(2,1)} %bitcast.266, f32[128,4]{0,1:T(4,128)} %bitcast.270, f32[4,128,2176]{1,2,0:T(8,128)} %copy-done.18, pred[128,2176]{0,1:T(8,128)(4,1)S(1)} %compare_and_fusion), kind=kOutput, calls=%fused_computation.90 | convolution fusion | flops 288688768 | bytes 7096320 | tf_op jit(solution)/shard_map/hts,shv->thv/dot_general | solution.py:326
  174.8 3.1 %fusion.165 = (bf16[16,128,128]{1,2,0:T(8,128)(2,1)}, f32[16,128,128]{1,2,0:T(8,128)}) fusion(f32[16,128,128]{1,2,0:T(8,128)} %copy.250, f32[16,128,128]{1,2,0:T(8,128)S(1)} %get-tuple-element.48, f32[16,128,256]{1,2,0:T(8,128)S(1)} %fusion.179, f32[16,128,256]{1,2,0:T(8,128)} %copy-done.2), kind=kLoop, calls=%fused_computation.218 | loop fusion | flops 1048576 | bytes 5767168 | tf_op jit(solution)/shard_map/convert_element_type | solution.py:236
  177.9 7.9 %collective-permute-start.3 = (bf16[16,128,128]{1,2,0:T(8,128)(2,1)}, bf16[16,128,128]{1,2,0:T(8,128)(2,1)}, u32[]{:S(2)}, u32[]{:S(2)}) collective-permute-start(bf16[16,128,128]{1,2,0:T(8,128)(2,1)} %get-tuple-element.36), channel_id=1, source_target_pairs={{0,64},{8,72},{16,80},{24,88},{32,96},{40,104},{48,112},{56,120},{... | collective-permute-start | bytes 1572872 | tf_op jit(solution)/shard_map/ppermute | solution.py:42
  193.9 3.9 %convolution_convert_fusion.3 = bf16[2176,512]{0,1:T(8,128)(2,1)} fusion(bf16[2176,576]{0,1:T(8,128)(2,1)S(1)} %copy-done.14, bf16[512,2048]{1,0:T(8,128)(2,1)} %param.18), kind=kOutput, calls=%fused_computation.39 | convolution fusion | flops 1141964800 | bytes 4980736 | tf_op jit(solution)/shard_map/dot_general | solution.py:297
  197.9 6.7 %fusion.77 = bf16[128,4,128]{0,2,1:T(8,128)(2,1)} fusion(bf16[2176,4,128]{0,2,1:T(8,128)(2,1)} %bitcast.267, f32[128,4]{0,1:T(4,128)} %bitcast.271, f32[4,128,2176]{1,2,0:T(8,128)} %copy-done.19, pred[128,2176]{0,1:T(8,128)(4,1)S(1)} %compare_and_fusion), kind=kOutput, calls=%fused_computation.89 | convolution fusion | flops 288688768 | bytes 7096320 | tf_op jit(solution)/shard_map/hts,shv->thv/dot_general | solution.py:326
  209.2 6.3 %collective-permute-start.4 = (bf16[16,128,128]{1,2,0:T(8,128)(2,1)}, bf16[16,128,128]{1,2,0:T(8,128)(2,1)S(1)}, u32[]{:S(2)}, u32[]{:S(2)}) collective-permute-start(bf16[16,128,128]{1,2,0:T(8,128)(2,1)} %fusion.47), channel_id=1, source_target_pairs={{0,8},{8,16},{16,24},{24,32},{32,40},{40,48},{48,56},{56,64},{64,7... | collective-permute-start | bytes 1572872 | tf_op jit(solution)/shard_map/ppermute | solution.py:42
  223.6 3.9 %convolution_convert_fusion.1 = bf16[2176,512]{0,1:T(8,128)(2,1)} fusion(bf16[2176,576]{0,1:T(8,128)(2,1)S(1)} %copy-done.15, bf16[512,2048]{1,0:T(8,128)(2,1)} %param.18), kind=kOutput, calls=%fused_computation.37 | convolution fusion | flops 1141964800 | bytes 4980736 | tf_op jit(solution)/shard_map/dot_general | solution.py:297
  227.5 6.1 %fusion.74 = bf16[128,4,128]{0,2,1:T(8,128)(2,1)S(1)} fusion(bf16[2176,4,128]{0,2,1:T(8,128)(2,1)} %bitcast.264, f32[128,4]{0,1:T(4,128)S(1)} %bitcast.268, f32[4,128,2176]{1,2,0:T(8,128)} %copy-done.16, pred[128,2176]{0,1:T(8,128)(4,1)S(1)} %compare_and_fusion), kind=kOutput, calls=%fused_computation.88 | convolution fusion | flops 288688768 | bytes 7096320 | tf_op jit(solution)/shard_map/hts,shv->thv/dot_general | solution.py:326
  (166 shorter events, 102.9 us)
Async XLA Ops:
  7.2 4.9 %copy-start.27 = (f32[128,16]{0,1:T(8,128)S(1)}, f32[128,16]{0,1:T(8,128)}, u32[]{:S(2)}) copy-start(f32[128,16]{0,1:T(8,128)} %param.14) | copy-start | bytes 24580
  7.2 5.0 %copy-start.24 = (bf16[128,2048]{1,0:T(8,128)(2,1)S(1)}, bf16[128,2048]{1,0:T(8,128)(2,1)}, u32[]{:S(2)}) copy-start(bf16[128,2048]{1,0:T(8,128)(2,1)} %param.12) | copy-start | bytes 1572868
  7.2 105.8 %all-gather.2.cloned.1.call-start = ((), (), s32[]{:S(2)}) async-start(), calls=%async_computation | async-start | bytes 4866048 | tf_op jit(solution)/shard_map/all_gather | solution.py:266
  48.4 9.6 %copy-start.3 = (f32[2,16,64,128]{3,2,1,0:T(8,128)}, f32[2,16,64,128]{3,2,1,0:T(8,128)S(1)}, u32[]{:S(2)}) copy-start(f32[2,16,64,128]{3,2,1,0:T(8,128)S(1)} %fusion.96) | copy-start | bytes 3145732
  50.3 4.7 %copy-start.5 = (f32[2,16,64,128]{3,2,1,0:T(8,128)}, f32[2,16,64,128]{3,2,1,0:T(8,128)S(1)}, u32[]{:S(2)}) copy-start(f32[2,16,64,128]{3,2,1,0:T(8,128)S(1)} %fusion.94) | copy-start | bytes 3145732
  55.0 7.1 %copy-start = (f32[2,16,128,128]{3,2,1,0:T(8,128)}, f32[2,16,128,128]{3,2,1,0:T(8,128)S(1)}, u32[]{:S(2)}) copy-start(f32[2,16,128,128]{3,2,1,0:T(8,128)S(1)} %multiply_subtract_fusion) | copy-start | bytes 6291460
  65.8 40.5 %collective-permute-start = (bf16[16,128,256]{1,2,0:T(8,128)(2,1)}, bf16[16,128,256]{1,2,0:T(8,128)(2,1)}, u32[]{:S(2)}, u32[]{:S(2)}) collective-permute-start(bf16[16,128,256]{1,2,0:T(8,128)(2,1)} %pad_maximum_fusion), channel_id=1, source_target_pairs={{0,8},{8,16},{16,24},{24,32},{32,40},{40,48},{48,56},{56,64},{64,7... | collective-permute-start | bytes 3145736 | tf_op jit(solution)/shard_map/ppermute | solution.py:42
  80.0 6.1 %copy-start.11 = (f32[2,16,64,128]{3,2,1,0:T(8,128)}, f32[2,16,64,128]{3,2,1,0:T(8,128)S(1)}, u32[]{:S(2)}) copy-start(f32[2,16,64,128]{3,2,1,0:T(8,128)S(1)} %convolution_subtract_fusion) | copy-start | bytes 3145732
  109.8 27.8 %collective-permute-start.1 = (bf16[16,128,256]{1,2,0:T(8,128)(2,1)}, bf16[16,128,256]{1,2,0:T(8,128)(2,1)}, u32[]{:S(2)}, u32[]{:S(2)}) collective-permute-start(bf16[16,128,256]{1,2,0:T(8,128)(2,1)} %pad_maximum_fusion.1), channel_id=1, source_target_pairs={{0,16},{8,24},{16,32},{24,40},{32,48},{40,56},{48,64},{56,72},{64,... | collective-permute-start | bytes 3145736 | tf_op jit(solution)/shard_map/ppermute | solution.py:42
  114.9 6.4 %copy-start.12 = (bf16[2176,576]{0,1:T(8,128)(2,1)}, bf16[2176,576]{0,1:T(8,128)(2,1)S(1)}, u32[]{:S(2)}) copy-start(bf16[2176,576]{0,1:T(8,128)(2,1)S(1)} %constant_dynamic-slice_fusion) | copy-start | bytes 7520260
  121.4 4.4 %copy-start.17 = (f32[4,128,2176]{1,2,0:T(8,128)}, f32[4,128,2176]{1,2,0:T(8,128)S(1)}, u32[]{:S(2)}) copy-start(f32[4,128,2176]{1,2,0:T(8,128)S(1)} %fusion.27) | copy-start | bytes 13369348
  139.7 5.9 %copy-start.13 = (bf16[2176,576]{0,1:T(8,128)(2,1)S(1)}, bf16[2176,576]{0,1:T(8,128)(2,1)}, u32[]{:S(2)}) copy-start(bf16[2176,576]{0,1:T(8,128)(2,1)} %copy-done.12) | copy-start | bytes 7520260
  142.0 25.4 %collective-permute-start.2 = (bf16[16,128,256]{1,2,0:T(8,128)(2,1)}, bf16[16,128,256]{1,2,0:T(8,128)(2,1)}, u32[]{:S(2)}, u32[]{:S(2)}) collective-permute-start(bf16[16,128,256]{1,2,0:T(8,128)(2,1)} %pad_maximum_fusion.2), channel_id=1, source_target_pairs={{0,32},{8,40},{16,48},{24,56},{32,64},{40,72},{48,80},{56,88},{64,... | collective-permute-start | bytes 3145736 | tf_op jit(solution)/shard_map/ppermute | solution.py:42
  151.7 4.4 %copy-start.18 = (f32[4,128,2176]{1,2,0:T(8,128)}, f32[4,128,2176]{1,2,0:T(8,128)S(1)}, u32[]{:S(2)}) copy-start(f32[4,128,2176]{1,2,0:T(8,128)S(1)} %fusion.24) | copy-start | bytes 13369348
  174.8 11.1 %copy-start.14 = (bf16[2176,576]{0,1:T(8,128)(2,1)S(1)}, bf16[2176,576]{0,1:T(8,128)(2,1)}, u32[]{:S(2)}) copy-start(bf16[2176,576]{0,1:T(8,128)(2,1)} %copy-done.12) | copy-start | bytes 7520260
  177.9 28.6 %collective-permute-start.3 = (bf16[16,128,128]{1,2,0:T(8,128)(2,1)}, bf16[16,128,128]{1,2,0:T(8,128)(2,1)}, u32[]{:S(2)}, u32[]{:S(2)}) collective-permute-start(bf16[16,128,128]{1,2,0:T(8,128)(2,1)} %get-tuple-element.36), channel_id=1, source_target_pairs={{0,64},{8,72},{16,80},{24,88},{32,96},{40,104},{48,112},{56,120},{... | collective-permute-start | bytes 1572872 | tf_op jit(solution)/shard_map/ppermute | solution.py:42
  197.9 8.6 %copy-start.10 = (f32[16,128,256]{2,1,0:T(8,128)S(1)}, f32[16,128,256]{2,1,0:T(8,128)}, u32[]{:S(2)}) copy-start(f32[16,128,256]{2,1,0:T(8,128)} %copy-done.9) | copy-start | bytes 6291460
  197.9 8.6 %copy-start.21 = (f32[16,128,128]{1,2,0:T(8,128)S(1)}, f32[16,128,128]{1,2,0:T(8,128)}, u32[]{:S(2)}) copy-start(f32[16,128,128]{1,2,0:T(8,128)} %get-tuple-element.37) | copy-start | bytes 3145732
  204.6 10.9 %copy-start.15 = (bf16[2176,576]{0,1:T(8,128)(2,1)S(1)}, bf16[2176,576]{0,1:T(8,128)(2,1)}, u32[]{:S(2)}) copy-start(bf16[2176,576]{0,1:T(8,128)(2,1)} %copy-done.12) | copy-start | bytes 7520260
  209.2 24.3 %collective-permute-start.4 = (bf16[16,128,128]{1,2,0:T(8,128)(2,1)}, bf16[16,128,128]{1,2,0:T(8,128)(2,1)S(1)}, u32[]{:S(2)}, u32[]{:S(2)}) collective-permute-start(bf16[16,128,128]{1,2,0:T(8,128)(2,1)} %fusion.47), channel_id=1, source_target_pairs={{0,8},{8,16},{16,24},{24,32},{32,40},{40,48},{48,56},{56,64},{64,7... | collective-permute-start | bytes 1572872 | tf_op jit(solution)/shard_map/ppermute | solution.py:42
  227.5 6.1 %slice-start = ((f32[2,16,64,128]{3,2,1,0:T(8,128)}), f32[1,16,64,128]{3,2,1,0:T(8,128)S(1)}, s32[]{:S(2)}) async-start(f32[2,16,64,128]{3,2,1,0:T(8,128)} %copy-done.11), calls=%async_computation.1 | async-start | bytes 1048576 | tf_op jit(solution)/shard_map/slice | solution.py:187
  227.5 6.1 %slice-start.1 = ((f32[2,16,64,128]{3,2,1,0:T(8,128)}), f32[1,16,64,128]{3,2,1,0:T(8,128)S(1)}, s32[]{:S(2)}) async-start(f32[2,16,64,128]{3,2,1,0:T(8,128)} %copy-done.20), calls=%async_computation.2 | async-start | bytes 1048576 | tf_op jit(solution)/shard_map/slice | solution.py:187
  227.5 6.1 %copy-start.22 = (f32[1,16,64,128]{3,2,1,0:T(8,128)S(1)}, f32[1,16,64,128]{3,2,1,0:T(8,128)}, u32[]{:S(2)}) copy-start(f32[1,16,64,128]{3,2,1,0:T(8,128)} %fusion.48) | copy-start | bytes 1572868
  227.5 6.1 %copy-start.23 = (f32[1,16,64,128]{3,2,1,0:T(8,128)S(1)}, f32[1,16,64,128]{3,2,1,0:T(8,128)}, u32[]{:S(2)}) copy-start(f32[1,16,64,128]{3,2,1,0:T(8,128)} %convolution_bitcast_fusion.9) | copy-start | bytes 1572868
  (13 other events, 31.9 us)
Sparse Core Ops, SparseCore 0:
  10.5 101.8 all-gather.1

commit v9 on v4

--- a/solution.py
+++ b/solution.py
@@ -284,28 +284,24 @@
         rows, _ = lax.optimization_barrier((key_rows, tie))
         heads = slice(group * per_group, (group + 1) * per_group)
         latent_part = rows[:, :LATENT]
-        keys_nope = (
-            jnp.dot(
-                latent_part,
-                key_up[:, group * per_group * NOPE : (group + 1) * per_group * NOPE],
-                preferred_element_type=jnp.float32,
-            )
-            .astype(jnp.bfloat16)
-            .reshape(window_rows, per_group, NOPE)
-        )
-        values = (
-            jnp.dot(
-                latent_part,
-                value_up[
-                    :, group * per_group * value_width : (group + 1) * per_group * value_width
-                ],
-                preferred_element_type=jnp.float32,
-            )
-            .astype(jnp.bfloat16)
-            .reshape(window_rows, per_group, value_width)
-        )
+        keys_nope = jnp.einsum(
+            "sl,lhd->hsd",
+            latent_part,
+            key_up[:, group * per_group * NOPE : (group + 1) * per_group * NOPE].reshape(
+                LATENT, per_group, NOPE
+            ),
+            preferred_element_type=jnp.float32,
+        ).astype(jnp.bfloat16)
+        values = jnp.einsum(
+            "sl,lhv->hsv",
+            latent_part,
+            value_up[
+                :, group * per_group * value_width : (group + 1) * per_group * value_width
+            ].reshape(LATENT, per_group, value_width),
+            preferred_element_type=jnp.float32,
+        ).astype(jnp.bfloat16)
         scores = jnp.einsum(
-            "thd,shd->hts",
+            "thd,hsd->hts",
             queries[:, heads, :NOPE],
             keys_nope,
             preferred_element_type=jnp.float32,
@@ -324,7 +320,7 @@
         weights = jnp.where(allowed[None], jnp.exp(masked - row_max), 0.0)
         row_total = jnp.sum(weights, axis=2)
         summed = jnp.einsum(
-            "hts,shv->thv",
+            "hts,hsv->thv",
             weights.astype(jnp.bfloat16),
             values,
             preferred_element_type=jnp.float32,

time: 247 us -> 258 us (1.045)
  the two profiles are of different devices: /device:TPU:4 before, /device:TPU:102 now
where the time goes in v9:
time: 258 us; the launch traced here: 254 us
  matrix products  135 us (52%)
  local copies, waits for them, and re-layouts  37.8 us (15%)
  starting transfers between devices  28.8 us (11%)
  waiting for transfers between devices  19.7 us (8%)
  other arithmetic  16.8 us (7%)
  between operations  15 us (6%)
    ppermute x5, starting transfers between devices, shifted(): return lax.ppermute(block, axis, route)  28.8 us
    sub x4, matrix products, attend_group(): weights = jnp.where(allowed[None], jnp.exp(masked - row_max), 0.0)  26.7 us
    unnamed x83, local copies, waits for them, and re-layouts  26.7 us
    dot_general x4, matrix products, attend_group(): jnp.einsum('thd,hsd->hts', queries[:, heads, :NOPE], keys_nope, preferred...  22.7 us
    dot_general x4, matrix products, attend_group(): jnp.einsum('hts,hsv->thv', weights.astype(jnp.bfloat16), values, preferre...  19.9 us
    ppermute x5, waiting for transfers between devices, shifted(): return lax.ppermute(block, axis, route)  19.7 us
    dot_general x5, matrix products, unit_lower_inverse(): jnp.einsum('hij,hjk->hik', result, identity + power_term, precision=PRECI...  16.6 us
    dot_general x4, matrix products, product(): return jnp.einsum('hkj,hjl->hkl', left, right, precision=PRECISE_PRODUCT)  10.4 us
  transfers between devices with their start and end apart: 6, of which 4 were waited for; matrix products, arithmetic and copies ran while one was open for 65% of the time, Pallas kernels for 0%

profile of v9, /device:TPU:102, one launch (start us, length us, event | category | flops | bytes accessed | tf_op | source)
XLA Modules:
  0.0 253.6 jit_solution(6648846014336414688)
XLA Ops:
  19.9 3.3 %fusion.69 = f32[2,16,64,64]{3,2,1,0:T(8,128)S(1)} fusion(f32[2,16,64]{2,1,0:T(8,128)S(1)} %get-tuple-element.49, pred[2,64,64]{2,1,0:T(8,128)(4,1)S(1)} %get-tuple-element.54, f32[2,64,16,128]{3,2,1,0:T(8,128)S(1)} %bitcast.364, f32[2,64,16]{1,2,0:T(8,128)S(1)} %copy.270, f32[2,64,16,128]{3,2,1,0:T(8,128)S(1)} %fusion.144), kind=kOutput, calls=%fused_computation.84 | convolution fusion | flops 202899456 | bytes 2646016 | tf_op jit(solution)/shard_map/vmap(thk,shk->hts)/dot_general | solution.py:79
  34.0 11.8 %fusion.235 = f32[2,16,64,64]{3,2,1,0:T(8,128)S(1)} fusion(f32[2,16,64,64]{3,2,1,0:T(8,128)S(1)} %fusion.156, f32[2,16,64,64]{3,2,1,0:T(8,128)S(1)} %convolution_add_fusion.2), kind=kOutput, calls=%fused_computation.231 | convolution fusion | flops 100663296 | bytes 1572864 | tf_op jit(solution)/shard_map/vmap(hij,hjk->hik)/dot_general | solution.py:61
  49.2 4.7 %multiply_subtract_fusion = f32[2,16,128,128]{3,2,1,0:T(8,128)S(1)} fusion(f32[2,16,64,128]{3,2,1,0:T(8,128)S(1)} %fusion.150, f32[128,128]{1,0:T(8,128)S(1)} %fusion.199, f32[2,16,128]{2,1,0:T(8,128)S(1)} %bitcast.394, f32[2]{0:T(128)S(1)} %slice_reduce_fusion, f32[2,64,16,128]{3,2,1,0:T(8,128)S(1)} %fusion.144, f32[2,64,16,128]{3,2,1,0:T(8,128)S(1)} %bitcast.366, ...), kind=kOutput, calls=%fused_computation.68 | convolution fusion | flops 405274624 | bytes 5349896 | tf_op jit(solution)/shard_map/vmap(shk,hsj->hkj)/dot_general | solution.py:103
  56.8 4.2 %fusion.194 = f32[2,16,128,128]{2,3,1,0:T(8,128)S(1)} fusion(f32[2,16,64,128]{3,2,1,0:T(8,128)S(1)} %fusion.152, f32[2,64,16,128]{3,2,1,0:T(8,128)S(1)} %fusion.144, f32[2,64,16,128]{3,2,1,0:T(8,128)S(1)} %bitcast.367, f32[2,64]{1,0:T(2,128)S(1)} %get-tuple-element.52, f32[2,16,128]{2,1,0:T(8,128)S(1)} %slice_bitcast_fusion.14, f32[2,64,16]{1,2,0:T(8,128)S(1)} %copy.270), kind=kOutput, calls=%fused_computation.183 | convolution fusion | flops 403701760 | bytes 5267968 | tf_op jit(solution)/shard_map/vmap(omt,mor->mtr)/dot_general | solution.py:106
  64.6 4.9 %collective-permute-start = (bf16[16,128,256]{1,2,0:T(8,128)(2,1)}, bf16[16,128,256]{1,2,0:T(8,128)(2,1)}, u32[]{:S(2)}, u32[]{:S(2)}) collective-permute-start(bf16[16,128,256]{1,2,0:T(8,128)(2,1)} %pad_maximum_fusion), channel_id=1, source_target_pairs={{0,8},{8,16},{16,24},{24,32},{32,40},{40,48},{48,56},{56,64},{64,7... | collective-permute-start | bytes 3145736 | tf_op jit(solution)/shard_map/ppermute | solution.py:42
  104.1 6.4 %collective-permute-done = bf16[16,128,256]{1,2,0:T(8,128)(2,1)} collective-permute-done((bf16[16,128,256]{1,2,0:T(8,128)(2,1)}, bf16[16,128,256]{1,2,0:T(8,128)(2,1)}, u32[]{:S(2)}, u32[]{:S(2)}) %collective-permute-start) | collective-permute-done | bytes 1048608 | tf_op jit(solution)/shard_map/ppermute | solution.py:42
  116.8 3.5 %constant_dynamic-slice_fusion = bf16[2176,576]{1,0:T(8,128)(2,1)} fusion(bf16[4096,576]{1,0:T(8,128)(2,1)} %all-gather.2.cloned.1.call-done, s32[]{:T(128)S(6)} %select_n.37), kind=kLoop, calls=%fused_computation.214 | loop fusion | bytes 5013508 | tf_op jit(solution)/shard_map/dynamic_slice | solution.py:269
  120.3 5.7 %convolution_bitcast_fusion.7 = f32[4,128,2176]{1,2,0:T(8,128)} fusion(bf16[512,4,128]{0,2,1:T(8,128)(2,1)} %bitcast.391, bf16[2176,576]{1,0:T(8,128)(2,1)} %constant_dynamic-slice_fusion, bf16[128,16,192]{0,2,1:T(8,128)(2,1)} %bitcast.377), kind=kOutput, calls=%fused_computation.35 | convolution fusion | flops 1427177472 | bytes 7340032 | tf_op jit(solution)/shard_map/thd,hsd->hts/dot_general | solution.py:303
  126.0 6.7 %fusion.211 = (f32[4,128]{1,0:T(4,128)}, bf16[4,128,2176]{1,2,0:T(8,128)(2,1)}) fusion(pred[128,2176]{0,1:T(8,128)(4,1)S(1)} %compare_and_fusion, f32[4,128,2176]{1,2,0:T(8,128)} %convolution_bitcast_fusion.7, bf16[2176,576]{1,0:T(8,128)(2,1)} %constant_dynamic-slice_fusion, bf16[128,16,192]{0,2,1:T(8,128)(2,1)} %bitcast.378), kind=kOutput, calls=%fused_computation.223 | convolution fusion | flops 150407296 | bytes 7866368 | tf_op jit(solution)/shard_map/sub | solution.py:320
  132.7 4.5 %fusion.137 = bf16[128,4,128]{0,2,1:T(8,128)(2,1)S(1)} fusion(bf16[4,128,2176]{1,2,0:T(8,128)(2,1)} %get-tuple-element.60, bf16[512,4,128]{0,2,1:T(8,128)(2,1)} %bitcast.392, bf16[2176,576]{1,0:T(8,128)(2,1)} %constant_dynamic-slice_fusion, f32[128,4]{0,1:T(4,128)} %bitcast.397), kind=kOutput, calls=%fused_computation.107 | convolution fusion | flops 1427308544 | bytes 5113856 | tf_op jit(solution)/shard_map/hts,hsv->thv/dot_general | solution.py:322
  137.2 5.6 %collective-permute-done.1 = bf16[16,128,256]{1,2,0:T(8,128)(2,1)} collective-permute-done((bf16[16,128,256]{1,2,0:T(8,128)(2,1)}, bf16[16,128,256]{1,2,0:T(8,128)(2,1)}, u32[]{:S(2)}, u32[]{:S(2)}) %collective-permute-start.1) | collective-permute-done | bytes 1048608 | tf_op jit(solution)/shard_map/ppermute | solution.py:42
  147.4 4.0 %collective-permute-start.2 = (bf16[16,128,256]{1,2,0:T(8,128)(2,1)}, bf16[16,128,256]{1,2,0:T(8,128)(2,1)}, u32[]{:S(2)}, u32[]{:S(2)}) collective-permute-start(bf16[16,128,256]{1,2,0:T(8,128)(2,1)} %pad_maximum_fusion.2), channel_id=1, source_target_pairs={{0,32},{8,40},{16,48},{24,56},{32,64},{40,72},{48,80},{56,88},{64,... | collective-permute-start | bytes 3145736 | tf_op jit(solution)/shard_map/ppermute | solution.py:42
  151.4 5.7 %convolution_bitcast_fusion.5 = f32[4,128,2176]{1,2,0:T(8,128)} fusion(bf16[512,4,128]{0,2,1:T(8,128)(2,1)} %bitcast.389, bf16[2176,576]{1,0:T(8,128)(2,1)} %constant_dynamic-slice_fusion, bf16[128,16,192]{0,2,1:T(8,128)(2,1)} %bitcast.379), kind=kOutput, calls=%fused_computation.30 | convolution fusion | flops 1427177472 | bytes 7340032 | tf_op jit(solution)/shard_map/thd,hsd->hts/dot_general | solution.py:303
  157.1 6.7 %fusion.212 = (f32[4,128]{1,0:T(4,128)}, bf16[4,128,2176]{1,2,0:T(8,128)(2,1)}) fusion(pred[128,2176]{0,1:T(8,128)(4,1)S(1)} %compare_and_fusion, f32[4,128,2176]{1,2,0:T(8,128)} %convolution_bitcast_fusion.5, bf16[2176,576]{1,0:T(8,128)(2,1)} %constant_dynamic-slice_fusion, bf16[128,16,192]{0,2,1:T(8,128)(2,1)} %bitcast.380), kind=kOutput, calls=%fused_computation.224 | convolution fusion | flops 150407296 | bytes 7866368 | tf_op jit(solution)/shard_map/sub | solution.py:320
  163.8 5.1 %fusion.127 = bf16[128,4,128]{0,2,1:T(8,128)(2,1)} fusion(bf16[4,128,2176]{1,2,0:T(8,128)(2,1)} %get-tuple-element.62, bf16[512,4,128]{0,2,1:T(8,128)(2,1)} %bitcast.390, bf16[2176,576]{1,0:T(8,128)(2,1)} %constant_dynamic-slice_fusion, f32[128,4]{0,1:T(4,128)} %bitcast.398), kind=kOutput, calls=%fused_computation.105 | convolution fusion | flops 1427308544 | bytes 5113856 | tf_op jit(solution)/shard_map/hts,hsv->thv/dot_general | solution.py:322
  168.9 4.5 %collective-permute-done.2 = bf16[16,128,256]{1,2,0:T(8,128)(2,1)} collective-permute-done((bf16[16,128,256]{1,2,0:T(8,128)(2,1)}, bf16[16,128,256]{1,2,0:T(8,128)(2,1)}, u32[]{:S(2)}, u32[]{:S(2)}) %collective-permute-start.2) | collective-permute-done | bytes 1048608 | tf_op jit(solution)/shard_map/ppermute | solution.py:42
  183.9 4.2 %collective-permute-start.3 = (bf16[16,128,128]{1,2,0:T(8,128)(2,1)}, bf16[16,128,128]{1,2,0:T(8,128)(2,1)}, u32[]{:S(2)}, u32[]{:S(2)}) collective-permute-start(bf16[16,128,128]{1,2,0:T(8,128)(2,1)} %get-tuple-element.38), channel_id=1, source_target_pairs={{0,64},{8,72},{16,80},{24,88},{32,96},{40,104},{48,112},{56,120},{... | collective-permute-start | bytes 1572872 | tf_op jit(solution)/shard_map/ppermute | solution.py:42
  188.2 5.7 %convolution_bitcast_fusion.3 = f32[4,128,2176]{1,2,0:T(8,128)} fusion(bf16[512,4,128]{0,2,1:T(8,128)(2,1)} %bitcast.387, bf16[2176,576]{1,0:T(8,128)(2,1)} %constant_dynamic-slice_fusion, bf16[128,16,192]{0,2,1:T(8,128)(2,1)} %bitcast.381), kind=kOutput, calls=%fused_computation.25 | convolution fusion | flops 1427177472 | bytes 7340032 | tf_op jit(solution)/shard_map/thd,hsd->hts/dot_general | solution.py:303
  193.9 6.7 %fusion.213 = (f32[4,128]{1,0:T(4,128)}, bf16[4,128,2176]{1,2,0:T(8,128)(2,1)}) fusion(pred[128,2176]{0,1:T(8,128)(4,1)S(1)} %compare_and_fusion, f32[4,128,2176]{1,2,0:T(8,128)} %convolution_bitcast_fusion.3, bf16[2176,576]{1,0:T(8,128)(2,1)} %constant_dynamic-slice_fusion, bf16[128,16,192]{0,2,1:T(8,128)(2,1)} %bitcast.382), kind=kOutput, calls=%fused_computation.225 | convolution fusion | flops 150407296 | bytes 7866368 | tf_op jit(solution)/shard_map/sub | solution.py:320
  200.5 5.3 %fusion.117 = bf16[128,4,128]{0,2,1:T(8,128)(2,1)} fusion(bf16[4,128,2176]{1,2,0:T(8,128)(2,1)} %get-tuple-element.64, bf16[512,4,128]{0,2,1:T(8,128)(2,1)} %bitcast.388, bf16[2176,576]{1,0:T(8,128)(2,1)} %constant_dynamic-slice_fusion, f32[128,4]{0,1:T(4,128)} %bitcast.399), kind=kOutput, calls=%fused_computation.103 | convolution fusion | flops 1427308544 | bytes 5113856 | tf_op jit(solution)/shard_map/hts,hsv->thv/dot_general | solution.py:322
  212.0 13.3 %collective-permute-start.4 = (bf16[16,128,128]{1,2,0:T(8,128)(2,1)}, bf16[16,128,128]{1,2,0:T(8,128)(2,1)S(1)}, u32[]{:S(2)}, u32[]{:S(2)}) collective-permute-start(bf16[16,128,128]{1,2,0:T(8,128)(2,1)} %fusion.71), channel_id=1, source_target_pairs={{0,8},{8,16},{16,24},{24,32},{32,40},{40,48},{48,56},{56,64},{64,7... | collective-permute-start | bytes 1572872 | tf_op jit(solution)/shard_map/ppermute | solution.py:42
  225.3 5.7 %convolution_bitcast_fusion.1 = f32[4,128,2176]{1,2,0:T(8,128)} fusion(bf16[512,4,128]{0,2,1:T(8,128)(2,1)} %bitcast.385, bf16[2176,576]{1,0:T(8,128)(2,1)} %constant_dynamic-slice_fusion, bf16[128,16,192]{0,2,1:T(8,128)(2,1)} %bitcast.383), kind=kOutput, calls=%fused_computation.20 | convolution fusion | flops 1427177472 | bytes 7340032 | tf_op jit(solution)/shard_map/thd,hsd->hts/dot_general | solution.py:303
  231.0 6.7 %fusion.214 = (f32[4,128]{1,0:T(4,128)}, bf16[4,128,2176]{1,2,0:T(8,128)(2,1)}) fusion(pred[128,2176]{0,1:T(8,128)(4,1)S(1)} %compare_and_fusion, f32[4,128,2176]{1,2,0:T(8,128)} %convolution_bitcast_fusion.1, bf16[2176,576]{1,0:T(8,128)(2,1)} %constant_dynamic-slice_fusion, bf16[128,16,192]{0,2,1:T(8,128)(2,1)} %bitcast.384), kind=kOutput, calls=%fused_computation.226 | convolution fusion | flops 150407296 | bytes 7866368 | tf_op jit(solution)/shard_map/sub | solution.py:320
  237.8 5.1 %fusion.107 = bf16[128,4,128]{0,2,1:T(8,128)(2,1)} fusion(bf16[4,128,2176]{1,2,0:T(8,128)(2,1)} %get-tuple-element.66, bf16[512,4,128]{0,2,1:T(8,128)(2,1)S(1)} %bitcast.386, bf16[2176,576]{1,0:T(8,128)(2,1)} %constant_dynamic-slice_fusion, f32[128,4]{0,1:T(4,128)} %bitcast.396), kind=kOutput, calls=%fused_computation.101 | convolution fusion | flops 1427308544 | bytes 5113856 | tf_op jit(solution)/shard_map/hts,hsv->thv/dot_general | solution.py:322
  (171 shorter events, 98.7 us)
Async XLA Ops:
  7.2 109.6 %all-gather.2.cloned.1.call-start = ((), (), s32[]{:S(2)}) async-start(), calls=%async_computation | async-start | bytes 5406720 | tf_op jit(solution)/shard_map/all_gather | solution.py:266
  47.3 9.5 %copy-start.3 = (f32[2,16,64,128]{3,2,1,0:T(8,128)}, f32[2,16,64,128]{3,2,1,0:T(8,128)S(1)}, u32[]{:S(2)}) copy-start(f32[2,16,64,128]{3,2,1,0:T(8,128)S(1)} %fusion.152) | copy-start | bytes 3145732
  49.2 4.7 %copy-start.5 = (f32[2,16,64,128]{3,2,1,0:T(8,128)}, f32[2,16,64,128]{3,2,1,0:T(8,128)S(1)}, u32[]{:S(2)}) copy-start(f32[2,16,64,128]{3,2,1,0:T(8,128)S(1)} %fusion.150) | copy-start | bytes 3145732
  53.9 7.1 %copy-start = (f32[2,16,128,128]{3,2,1,0:T(8,128)}, f32[2,16,128,128]{3,2,1,0:T(8,128)S(1)}, u32[]{:S(2)}) copy-start(f32[2,16,128,128]{3,2,1,0:T(8,128)S(1)} %multiply_subtract_fusion) | copy-start | bytes 6291460
  64.6 46.0 %collective-permute-start = (bf16[16,128,256]{1,2,0:T(8,128)(2,1)}, bf16[16,128,256]{1,2,0:T(8,128)(2,1)}, u32[]{:S(2)}, u32[]{:S(2)}) collective-permute-start(bf16[16,128,256]{1,2,0:T(8,128)(2,1)} %pad_maximum_fusion), channel_id=1, source_target_pairs={{0,8},{8,16},{16,24},{24,32},{32,40},{40,48},{48,56},{56,64},{64,7... | collective-permute-start | bytes 3145736 | tf_op jit(solution)/shard_map/ppermute | solution.py:42
  80.0 9.9 %copy-start.11 = (f32[2,16,64,128]{3,2,1,0:T(8,128)}, f32[2,16,64,128]{3,2,1,0:T(8,128)S(1)}, u32[]{:S(2)}) copy-start(f32[2,16,64,128]{3,2,1,0:T(8,128)S(1)} %convolution_subtract_fusion) | copy-start | bytes 3145732
  83.1 6.7 %copy-start.12 = (f32[2,16,64,128]{3,2,1,0:T(8,128)}, f32[2,16,64,128]{3,2,1,0:T(8,128)S(1)}, u32[]{:S(2)}) copy-start(f32[2,16,64,128]{3,2,1,0:T(8,128)S(1)} %fusion.236) | copy-start | bytes 3145732
  89.9 4.5 %copy-start.24 = (bf16[512,512]{1,0:T(8,128)(2,1)S(1)}, bf16[512,512]{1,0:T(8,128)(2,1)}, u32[]{:S(2)}) copy-start(bf16[512,512]{1,0:T(8,128)(2,1)} %get-tuple-element.45) | copy-start | bytes 1572868
  89.9 5.5 %copy-start.23 = (bf16[512,512]{1,0:T(8,128)(2,1)S(1)}, bf16[512,512]{1,0:T(8,128)(2,1)}, u32[]{:S(2)}) copy-start(bf16[512,512]{1,0:T(8,128)(2,1)} %get-tuple-element.46) | copy-start | bytes 1572868
  92.3 6.3 %copy-start.22 = (bf16[512,512]{1,0:T(8,128)(2,1)S(1)}, bf16[512,512]{1,0:T(8,128)(2,1)}, u32[]{:S(2)}) copy-start(bf16[512,512]{1,0:T(8,128)(2,1)} %get-tuple-element.40) | copy-start | bytes 1572868
  94.4 5.2 %copy-start.21 = (bf16[512,512]{1,0:T(8,128)(2,1)S(1)}, bf16[512,512]{1,0:T(8,128)(2,1)}, u32[]{:S(2)}) copy-start(bf16[512,512]{1,0:T(8,128)(2,1)} %get-tuple-element.41) | copy-start | bytes 1572868
  95.4 5.2 %copy-start.20 = (bf16[512,512]{1,0:T(8,128)(2,1)S(1)}, bf16[512,512]{1,0:T(8,128)(2,1)}, u32[]{:S(2)}) copy-start(bf16[512,512]{1,0:T(8,128)(2,1)} %get-tuple-element.42) | copy-start | bytes 1572868
  96.4 5.2 %copy-start.19 = (bf16[512,512]{1,0:T(8,128)(2,1)S(1)}, bf16[512,512]{1,0:T(8,128)(2,1)}, u32[]{:S(2)}) copy-start(bf16[512,512]{1,0:T(8,128)(2,1)} %get-tuple-element.43) | copy-start | bytes 1572868
  114.4 28.3 %collective-permute-start.1 = (bf16[16,128,256]{1,2,0:T(8,128)(2,1)}, bf16[16,128,256]{1,2,0:T(8,128)(2,1)}, u32[]{:S(2)}, u32[]{:S(2)}) collective-permute-start(bf16[16,128,256]{1,2,0:T(8,128)(2,1)} %pad_maximum_fusion.1), channel_id=1, source_target_pairs={{0,16},{8,24},{16,32},{24,40},{32,48},{40,56},{48,64},{56,72},{64,... | collective-permute-start | bytes 3145736 | tf_op jit(solution)/shard_map/ppermute | solution.py:42
  147.4 25.9 %collective-permute-start.2 = (bf16[16,128,256]{1,2,0:T(8,128)(2,1)}, bf16[16,128,256]{1,2,0:T(8,128)(2,1)}, u32[]{:S(2)}, u32[]{:S(2)}) collective-permute-start(bf16[16,128,256]{1,2,0:T(8,128)(2,1)} %pad_maximum_fusion.2), channel_id=1, source_target_pairs={{0,32},{8,40},{16,48},{24,56},{32,64},{40,72},{48,80},{56,88},{64,... | collective-permute-start | bytes 3145736 | tf_op jit(solution)/shard_map/ppermute | solution.py:42
  183.9 25.0 %collective-permute-start.3 = (bf16[16,128,128]{1,2,0:T(8,128)(2,1)}, bf16[16,128,128]{1,2,0:T(8,128)(2,1)}, u32[]{:S(2)}, u32[]{:S(2)}) collective-permute-start(bf16[16,128,128]{1,2,0:T(8,128)(2,1)} %get-tuple-element.38), channel_id=1, source_target_pairs={{0,64},{8,72},{16,80},{24,88},{32,96},{40,104},{48,112},{56,120},{... | collective-permute-start | bytes 1572872 | tf_op jit(solution)/shard_map/ppermute | solution.py:42
  200.5 8.5 %copy-start.10 = (f32[16,128,256]{2,1,0:T(8,128)S(1)}, f32[16,128,256]{2,1,0:T(8,128)}, u32[]{:S(2)}) copy-start(f32[16,128,256]{2,1,0:T(8,128)} %copy-done.9) | copy-start | bytes 6291460
  200.5 8.5 %copy-start.13 = (f32[16,128,128]{1,2,0:T(8,128)S(1)}, f32[16,128,128]{1,2,0:T(8,128)}, u32[]{:S(2)}) copy-start(f32[16,128,128]{1,2,0:T(8,128)} %get-tuple-element.39) | copy-start | bytes 3145732
  212.0 30.8 %collective-permute-start.4 = (bf16[16,128,128]{1,2,0:T(8,128)(2,1)}, bf16[16,128,128]{1,2,0:T(8,128)(2,1)S(1)}, u32[]{:S(2)}, u32[]{:S(2)}) collective-permute-start(bf16[16,128,128]{1,2,0:T(8,128)(2,1)} %fusion.71), channel_id=1, source_target_pairs={{0,8},{8,16},{16,24},{24,32},{32,40},{40,48},{48,56},{56,64},{64,7... | collective-permute-start | bytes 1572872 | tf_op jit(solution)/shard_map/ppermute | solution.py:42
  231.0 6.7 %copy-start.26 = (bf16[512,512]{0,1:T(8,128)(2,1)S(1)}, bf16[512,512]{0,1:T(8,128)(2,1)}, u32[]{:S(2)}) copy-start(bf16[512,512]{0,1:T(8,128)(2,1)} %copy.378) | copy-start | bytes 1572868
  237.7 5.1 %slice-start = ((f32[2,16,64,128]{3,2,1,0:T(8,128)}), f32[1,16,64,128]{3,2,1,0:T(8,128)S(1)}, s32[]{:S(2)}) async-start(f32[2,16,64,128]{3,2,1,0:T(8,128)} %copy-done.11), calls=%async_computation.1 | async-start | bytes 1048576 | tf_op jit(solution)/shard_map/slice | solution.py:187
  237.7 5.1 %slice-start.1 = ((f32[2,16,64,128]{3,2,1,0:T(8,128)}), f32[1,16,64,128]{3,2,1,0:T(8,128)S(1)}, s32[]{:S(2)}) async-start(f32[2,16,64,128]{3,2,1,0:T(8,128)} %copy-done.12), calls=%async_computation.2 | async-start | bytes 1048576 | tf_op jit(solution)/shard_map/slice | solution.py:187
  237.7 5.1 %copy-start.17 = (f32[1,16,64,128]{3,2,1,0:T(8,128)S(1)}, f32[1,16,64,128]{3,2,1,0:T(8,128)}, u32[]{:S(2)}) copy-start(f32[1,16,64,128]{3,2,1,0:T(8,128)} %fusion.72) | copy-start | bytes 1572868
  237.8 5.1 %copy-start.18 = (f32[1,16,64,128]{3,2,1,0:T(8,128)S(1)}, f32[1,16,64,128]{3,2,1,0:T(8,128)}, u32[]{:S(2)}) copy-start(f32[1,16,64,128]{3,2,1,0:T(8,128)} %convolution_bitcast_fusion.9) | copy-start | bytes 1572868
  (16 other events, 42.0 us)
Sparse Core Ops, SparseCore 0:
  10.6 99.8 all-gather.1

commit v10 on v4

--- a/solution.py
+++ b/solution.py
@@ -58,8 +58,8 @@
     power_term = strictly_lower
     for level_index in range(length.bit_length() - 2):
         power_term = jnp.einsum("hij,hjk->hik", power_term, power_term, precision=PRECISE_PRODUCT)
-        result = jnp.einsum(
-            "hij,hjk->hik", result, identity + power_term, precision=PRECISE_PRODUCT
+        result = result + jnp.einsum(
+            "hij,hjk->hik", result, power_term, precision=PRECISE_PRODUCT
         )
     return result
 

time: 247 us -> 247 us (level)
  no operation moved by 1% of the time
where the time goes in v10:
time: 247 us; the launch traced here: 242 us
  matrix products  122 us (49%)
  waiting for transfers between devices  29.4 us (12%)
  starting transfers between devices  28 us (11%)
  other arithmetic  26.4 us (11%)
  local copies, waits for them, and re-layouts  20.8 us (8%)
  between operations  15.1 us (6%)
    ppermute x5, starting transfers between devices, shifted(): return lax.ppermute(block, axis, route)  28 us
    dot_general x4, matrix products, attend_group(): jnp.einsum('hts,shv->thv', weights.astype(jnp.bfloat16), values, preferre...  25.3 us
    ppermute x5, waiting for transfers between devices, shifted(): return lax.ppermute(block, axis, route)  23.9 us
    dot_general x4, matrix products, attend_group(): jnp.dot(latent_part, value_up[:, group * per_group * value_width:(group +...  16.5 us
    unnamed x68, local copies, waits for them, and re-layouts  14.2 us
    dot_general x4, matrix products, product(): return jnp.einsum('hkj,hjl->hkl', left, right, precision=PRECISE_PRODUCT)  10.6 us
    dot_general x4, matrix products, attend_group(): jnp.dot(latent_part, key_up[:, group * per_group * NOPE:(group + 1) * per...  10.4 us
    sub x4, other arithmetic, attend_group(): weights = jnp.where(allowed[None], jnp.exp(masked - row_max), 0.0)  7.39 us
  transfers between devices with their start and end apart: 6, of which 3 were waited for; matrix products, arithmetic and copies ran while one was open for 61% of the time, Pallas kernels for 0%

profile of v10, /device:TPU:4, one launch (start us, length us, event | category | flops | bytes accessed | tf_op | source)
XLA Modules:
  0.0 242.0 jit_solution(16872617383104804996)
XLA Ops:
  19.6 3.1 %fusion.45 = f32[2,16,64,64]{3,2,1,0:T(8,128)S(1)} fusion(f32[2,16,64]{2,1,0:T(8,128)S(1)} %get-tuple-element.39, pred[2,64,64]{2,1,0:T(8,128)(4,1)S(1)} %get-tuple-element.44, f32[2,64,16,128]{3,2,1,0:T(8,128)S(1)} %bitcast.240, f32[2,64,16]{1,2,0:T(8,128)S(1)} %copy.187, f32[2,64,16,128]{3,2,1,0:T(8,128)S(1)} %fusion.88), kind=kOutput, calls=%fused_computation.72 | convolution fusion | flops 202899456 | bytes 2646016 | tf_op jit(solution)/shard_map/vmap(thk,shk->hts)/dot_general | solution.py:79
  39.9 4.7 %multiply_subtract_fusion = f32[2,16,128,128]{3,2,1,0:T(8,128)S(1)} fusion(f32[2,16,64,128]{3,2,1,0:T(8,128)S(1)} %fusion.94, f32[128,128]{1,0:T(8,128)S(1)} %fusion.140, f32[2,16,128]{2,1,0:T(8,128)S(1)} %bitcast.266, f32[2]{0:T(128)S(1)} %slice_reduce_fusion, f32[2,64,16,128]{3,2,1,0:T(8,128)S(1)} %fusion.88, f32[2,64,16,128]{3,2,1,0:T(8,128)S(1)} %bitcast.242, ...), kind=kOutput, calls=%fused_computation.52 | convolution fusion | flops 405274624 | bytes 5349896 | tf_op jit(solution)/shard_map/vmap(shk,hsj->hkj)/dot_general | solution.py:103
  44.6 2.9 %fusion.156 = (bf16[16,128,128]{1,2,0:T(8,128)(2,1)S(1)}, f32[16,128,128]{1,2,0:T(8,128)}) fusion(f32[2,16,128,128]{3,2,1,0:T(8,128)S(1)} %multiply_subtract_fusion), kind=kOutput, calls=%fused_computation.212 | convolution fusion | flops 402915328 | bytes 3670016 | tf_op jit(solution)/shard_map/hkj,hjl->hkl/dot_general | solution.py:174
  47.6 4.2 %fusion.135 = f32[2,16,128,128]{2,3,1,0:T(8,128)S(1)} fusion(f32[2,16,64,128]{3,2,1,0:T(8,128)S(1)} %fusion.96, f32[2,64,16,128]{3,2,1,0:T(8,128)S(1)} %fusion.88, f32[2,64,16,128]{3,2,1,0:T(8,128)S(1)} %bitcast.243, f32[2,64]{1,0:T(2,128)S(1)} %get-tuple-element.42, f32[2,16,128]{2,1,0:T(8,128)S(1)} %slice_bitcast_fusion.14, f32[2,64,16]{1,2,0:T(8,128)S(1)} %copy.187), kind=kOutput, calls=%fused_computation.168 | convolution fusion | flops 403701760 | bytes 5267968 | tf_op jit(solution)/shard_map/vmap(omt,mor->mtr)/dot_general | solution.py:106
  55.4 3.1 %collective-permute-start = (bf16[16,128,256]{1,2,0:T(8,128)(2,1)}, bf16[16,128,256]{1,2,0:T(8,128)(2,1)}, u32[]{:S(2)}, u32[]{:S(2)}) collective-permute-start(bf16[16,128,256]{1,2,0:T(8,128)(2,1)} %pad_maximum_fusion), channel_id=1, source_target_pairs={{0,8},{8,16},{16,24},{24,32},{32,40},{40,48},{48,56},{56,64},{64,7... | collective-permute-start | bytes 3145736 | tf_op jit(solution)/shard_map/ppermute | solution.py:42
  63.9 2.9 %convolution_select_fusion.1 = f32[2,16,64,64]{3,2,1,0:T(8,128)S(1)} fusion(pred[2,64,64]{2,1,0:T(8,128)(4,1)S(1)} %get-tuple-element.43, f32[2,64,16,128]{3,2,1,0:T(8,128)S(1)} %bitcast.245, f32[2,64,16]{1,2,0:T(8,128)S(1)} %copy.183, f32[2,64,16,128]{3,2,1,0:T(8,128)S(1)} %fusion.88, f32[2,64,16,128]{3,2,1,0:T(8,128)S(1)} %bitcast.244, ...), kind=kOutput, calls=%fused_computation.73 | convolution fusion | flops 202768384 | bytes 3694592 | tf_op jit(solution)/shard_map/vmap(thk,shk->hts)/dot_general | solution.py:90
  72.0 2.9 %fusion.48 = f32[1,16,64,128]{3,2,1,0:T(8,128)} fusion(f32[2,16,128,128]{2,3,1,0:T(8,128)S(1)} %copy-done.8, f32[2,16,64,128]{3,2,1,0:T(8,128)S(1)} %fusion.167, f32[2,16,64,128]{3,2,1,0:T(8,128)S(1)} %convolution_subtract_fusion), kind=kOutput, calls=%fused_computation.81 | convolution fusion | flops 201457664 | bytes 2621440 | tf_op jit(solution)/shard_map/cor,crm->com/dot_general | solution.py:171
  78.8 22.3 %collective-permute-done = bf16[16,128,256]{1,2,0:T(8,128)(2,1)} collective-permute-done((bf16[16,128,256]{1,2,0:T(8,128)(2,1)}, bf16[16,128,256]{1,2,0:T(8,128)(2,1)}, u32[]{:S(2)}, u32[]{:S(2)}) %collective-permute-start) | collective-permute-done | bytes 1048608 | tf_op jit(solution)/shard_map/ppermute | solution.py:42
  107.1 4.8 %all-gather.2.cloned.1.call-done = bf16[4096,576]{0,1:T(8,128)(2,1)} async-done(((bf16[128,576]{0,1:T(8,128)(2,1)}), bf16[4096,576]{0,1:T(8,128)(2,1)}) %all-gather.2.cloned.1.call-update) | async-done | bytes 4718608 | tf_op jit(solution)/shard_map/all_gather | solution.py:266
  113.8 2.9 %convolution_convert_fusion.6 = bf16[2176,512]{0,1:T(8,128)(2,1)S(1)} fusion(bf16[2176,576]{0,1:T(8,128)(2,1)S(1)} %constant_dynamic-slice_fusion, bf16[512,2048]{1,0:T(8,128)(2,1)} %param.17), kind=kOutput, calls=%fused_computation.42 | convolution fusion | flops 1141964800 | bytes 4980736 | tf_op jit(solution)/shard_map/dot_general | solution.py:288
  120.2 4.3 %convolution_convert_fusion.7 = bf16[2176,512]{0,1:T(8,128)(2,1)} fusion(bf16[2176,576]{0,1:T(8,128)(2,1)S(1)} %constant_dynamic-slice_fusion, bf16[512,2048]{1,0:T(8,128)(2,1)} %param.18), kind=kOutput, calls=%fused_computation.43 | convolution fusion | flops 1141964800 | bytes 4980736 | tf_op jit(solution)/shard_map/dot_general | solution.py:297
  126.5 5.9 %fusion.83 = bf16[128,4,128]{0,2,1:T(8,128)(2,1)S(1)} fusion(bf16[2176,4,128]{0,2,1:T(8,128)(2,1)} %bitcast.269, f32[128,4]{0,1:T(4,128)} %bitcast.273, f32[4,128,2176]{1,2,0:T(8,128)} %copy-done.17, pred[128,2176]{0,1:T(8,128)(4,1)S(1)} %compare_and_fusion), kind=kOutput, calls=%fused_computation.95 | convolution fusion | flops 288688768 | bytes 7096320 | tf_op jit(solution)/shard_map/hts,shv->thv/dot_general | solution.py:326
  137.1 3.1 %collective-permute-start.2 = (bf16[16,128,256]{1,2,0:T(8,128)(2,1)}, bf16[16,128,256]{1,2,0:T(8,128)(2,1)}, u32[]{:S(2)}, u32[]{:S(2)}) collective-permute-start(bf16[16,128,256]{1,2,0:T(8,128)(2,1)} %pad_maximum_fusion.2), channel_id=1, source_target_pairs={{0,32},{8,40},{16,48},{24,56},{32,64},{40,72},{48,80},{56,88},{64,... | collective-permute-start | bytes 3145736 | tf_op jit(solution)/shard_map/ppermute | solution.py:42
  146.2 4.3 %convolution_convert_fusion.5 = bf16[2176,512]{0,1:T(8,128)(2,1)} fusion(bf16[2176,576]{0,1:T(8,128)(2,1)S(1)} %copy-done.13, bf16[512,2048]{1,0:T(8,128)(2,1)} %param.18), kind=kOutput, calls=%fused_computation.41 | convolution fusion | flops 1141964800 | bytes 4980736 | tf_op jit(solution)/shard_map/dot_general | solution.py:297
  152.6 6.6 %fusion.80 = bf16[128,4,128]{0,2,1:T(8,128)(2,1)} fusion(bf16[2176,4,128]{0,2,1:T(8,128)(2,1)} %bitcast.270, f32[128,4]{0,1:T(4,128)} %bitcast.274, f32[4,128,2176]{1,2,0:T(8,128)} %copy-done.18, pred[128,2176]{0,1:T(8,128)(4,1)S(1)} %compare_and_fusion), kind=kOutput, calls=%fused_computation.94 | convolution fusion | flops 288688768 | bytes 7096320 | tf_op jit(solution)/shard_map/hts,shv->thv/dot_general | solution.py:326
  160.8 2.6 %fusion.102 = f32[16,128,256]{2,1,0:T(8,128)S(1)} fusion(bf16[16,128,256]{1,2,0:T(8,128)(2,1)} %collective-permute-done.2, f32[16,128,256]{1,2,0:T(8,128)} %copy-done.2), kind=kOutput, calls=%fused_computation.129 | convolution fusion | flops 805306368 | bytes 4194304 | tf_op jit(solution)/shard_map/hkj,hjl->hkl/dot_general | solution.py:244
  168.4 3.1 %fusion.154 = (bf16[16,128,128]{1,2,0:T(8,128)(2,1)}, f32[16,128,128]{1,2,0:T(8,128)}) fusion(f32[16,128,128]{1,2,0:T(8,128)} %copy.250, f32[16,128,128]{1,2,0:T(8,128)S(1)} %get-tuple-element.48, f32[16,128,256]{1,2,0:T(8,128)S(1)} %fusion.168, f32[16,128,256]{1,2,0:T(8,128)} %copy-done.2), kind=kLoop, calls=%fused_computation.211 | loop fusion | flops 1048576 | bytes 5767168 | tf_op jit(solution)/shard_map/convert_element_type | solution.py:236
  171.5 6.7 %collective-permute-start.3 = (bf16[16,128,128]{1,2,0:T(8,128)(2,1)}, bf16[16,128,128]{1,2,0:T(8,128)(2,1)}, u32[]{:S(2)}, u32[]{:S(2)}) collective-permute-start(bf16[16,128,128]{1,2,0:T(8,128)(2,1)} %get-tuple-element.36), channel_id=1, source_target_pairs={{0,64},{8,72},{16,80},{24,88},{32,96},{40,104},{48,112},{56,120},{... | collective-permute-start | bytes 1572872 | tf_op jit(solution)/shard_map/ppermute | solution.py:42
  186.3 3.9 %convolution_convert_fusion.3 = bf16[2176,512]{0,1:T(8,128)(2,1)} fusion(bf16[2176,576]{0,1:T(8,128)(2,1)S(1)} %copy-done.14, bf16[512,2048]{1,0:T(8,128)(2,1)} %param.18), kind=kOutput, calls=%fused_computation.39 | convolution fusion | flops 1141964800 | bytes 4980736 | tf_op jit(solution)/shard_map/dot_general | solution.py:297
  190.2 6.7 %fusion.77 = bf16[128,4,128]{0,2,1:T(8,128)(2,1)} fusion(bf16[2176,4,128]{0,2,1:T(8,128)(2,1)} %bitcast.271, f32[128,4]{0,1:T(4,128)} %bitcast.275, f32[4,128,2176]{1,2,0:T(8,128)} %copy-done.19, pred[128,2176]{0,1:T(8,128)(4,1)S(1)} %compare_and_fusion), kind=kOutput, calls=%fused_computation.93 | convolution fusion | flops 288688768 | bytes 7096320 | tf_op jit(solution)/shard_map/hts,shv->thv/dot_general | solution.py:326
  197.0 3.2 %fusion.47 = bf16[16,128,128]{1,2,0:T(8,128)(2,1)} fusion(f32[16,128,128]{1,2,0:T(8,128)S(1)} %copy-done.21, bf16[16,128,128]{1,2,0:T(8,128)(2,1)} %collective-permute-done.3, f32[16,128,256]{2,1,0:T(8,128)S(1)} %copy-done.10), kind=kOutput, calls=%fused_computation.79 | convolution fusion | flops 403177472 | bytes 3145728 | tf_op jit(solution)/shard_map/hkj,hjl->hkl/dot_general | solution.py:244
  200.2 13.0 %collective-permute-start.4 = (bf16[16,128,128]{1,2,0:T(8,128)(2,1)}, bf16[16,128,128]{1,2,0:T(8,128)(2,1)S(1)}, u32[]{:S(2)}, u32[]{:S(2)}) collective-permute-start(bf16[16,128,128]{1,2,0:T(8,128)(2,1)} %fusion.47), channel_id=1, source_target_pairs={{0,8},{8,16},{16,24},{24,32},{32,40},{40,48},{48,56},{56,64},{64,7... | collective-permute-start | bytes 1572872 | tf_op jit(solution)/shard_map/ppermute | solution.py:42
  221.3 3.9 %convolution_convert_fusion.1 = bf16[2176,512]{0,1:T(8,128)(2,1)} fusion(bf16[2176,576]{0,1:T(8,128)(2,1)S(1)} %copy-done.15, bf16[512,2048]{1,0:T(8,128)(2,1)} %param.18), kind=kOutput, calls=%fused_computation.37 | convolution fusion | flops 1141964800 | bytes 4980736 | tf_op jit(solution)/shard_map/dot_general | solution.py:297
  225.2 6.1 %fusion.74 = bf16[128,4,128]{0,2,1:T(8,128)(2,1)S(1)} fusion(bf16[2176,4,128]{0,2,1:T(8,128)(2,1)} %bitcast.268, f32[128,4]{0,1:T(4,128)S(1)} %bitcast.272, f32[4,128,2176]{1,2,0:T(8,128)} %copy-done.16, pred[128,2176]{0,1:T(8,128)(4,1)S(1)} %compare_and_fusion), kind=kOutput, calls=%fused_computation.92 | convolution fusion | flops 288688768 | bytes 7096320 | tf_op jit(solution)/shard_map/hts,shv->thv/dot_general | solution.py:326
  (166 shorter events, 99.5 us)
Async XLA Ops:
  7.2 4.9 %copy-start.27 = (f32[128,16]{0,1:T(8,128)S(1)}, f32[128,16]{0,1:T(8,128)}, u32[]{:S(2)}) copy-start(f32[128,16]{0,1:T(8,128)} %param.14) | copy-start | bytes 24580
  7.2 5.0 %copy-start.24 = (bf16[128,2048]{1,0:T(8,128)(2,1)S(1)}, bf16[128,2048]{1,0:T(8,128)(2,1)}, u32[]{:S(2)}) copy-start(bf16[128,2048]{1,0:T(8,128)(2,1)} %param.12) | copy-start | bytes 1572868
  7.2 104.7 %all-gather.2.cloned.1.call-start = ((), (), s32[]{:S(2)}) async-start(), calls=%async_computation | async-start | bytes 4866048 | tf_op jit(solution)/shard_map/all_gather | solution.py:266
  38.0 9.6 %copy-start.3 = (f32[2,16,64,128]{3,2,1,0:T(8,128)}, f32[2,16,64,128]{3,2,1,0:T(8,128)S(1)}, u32[]{:S(2)}) copy-start(f32[2,16,64,128]{3,2,1,0:T(8,128)S(1)} %fusion.96) | copy-start | bytes 3145732
  39.9 4.7 %copy-start.5 = (f32[2,16,64,128]{3,2,1,0:T(8,128)}, f32[2,16,64,128]{3,2,1,0:T(8,128)S(1)}, u32[]{:S(2)}) copy-start(f32[2,16,64,128]{3,2,1,0:T(8,128)S(1)} %fusion.94) | copy-start | bytes 3145732
  44.6 7.1 %copy-start = (f32[2,16,128,128]{3,2,1,0:T(8,128)}, f32[2,16,128,128]{3,2,1,0:T(8,128)S(1)}, u32[]{:S(2)}) copy-start(f32[2,16,128,128]{3,2,1,0:T(8,128)S(1)} %multiply_subtract_fusion) | copy-start | bytes 6291460
  55.4 45.8 %collective-permute-start = (bf16[16,128,256]{1,2,0:T(8,128)(2,1)}, bf16[16,128,256]{1,2,0:T(8,128)(2,1)}, u32[]{:S(2)}, u32[]{:S(2)}) collective-permute-start(bf16[16,128,256]{1,2,0:T(8,128)(2,1)} %pad_maximum_fusion), channel_id=1, source_target_pairs={{0,8},{8,16},{16,24},{24,32},{32,40},{40,48},{48,56},{56,64},{64,7... | collective-permute-start | bytes 3145736 | tf_op jit(solution)/shard_map/ppermute | solution.py:42
  68.9 6.1 %copy-start.11 = (f32[2,16,64,128]{3,2,1,0:T(8,128)}, f32[2,16,64,128]{3,2,1,0:T(8,128)S(1)}, u32[]{:S(2)}) copy-start(f32[2,16,64,128]{3,2,1,0:T(8,128)S(1)} %convolution_subtract_fusion) | copy-start | bytes 3145732
  104.9 27.5 %collective-permute-start.1 = (bf16[16,128,256]{1,2,0:T(8,128)(2,1)}, bf16[16,128,256]{1,2,0:T(8,128)(2,1)}, u32[]{:S(2)}, u32[]{:S(2)}) collective-permute-start(bf16[16,128,256]{1,2,0:T(8,128)(2,1)} %pad_maximum_fusion.1), channel_id=1, source_target_pairs={{0,16},{8,24},{16,32},{24,40},{32,48},{40,56},{48,64},{56,72},{64,... | collective-permute-start | bytes 3145736 | tf_op jit(solution)/shard_map/ppermute | solution.py:42
  113.7 6.4 %copy-start.12 = (bf16[2176,576]{0,1:T(8,128)(2,1)}, bf16[2176,576]{0,1:T(8,128)(2,1)S(1)}, u32[]{:S(2)}) copy-start(bf16[2176,576]{0,1:T(8,128)(2,1)S(1)} %constant_dynamic-slice_fusion) | copy-start | bytes 7520260
  120.2 4.4 %copy-start.17 = (f32[4,128,2176]{1,2,0:T(8,128)}, f32[4,128,2176]{1,2,0:T(8,128)S(1)}, u32[]{:S(2)}) copy-start(f32[4,128,2176]{1,2,0:T(8,128)S(1)} %fusion.27) | copy-start | bytes 13369348
  134.8 5.4 %copy-start.13 = (bf16[2176,576]{0,1:T(8,128)(2,1)S(1)}, bf16[2176,576]{0,1:T(8,128)(2,1)}, u32[]{:S(2)}) copy-start(bf16[2176,576]{0,1:T(8,128)(2,1)} %copy-done.12) | copy-start | bytes 7520260
  137.1 23.7 %collective-permute-start.2 = (bf16[16,128,256]{1,2,0:T(8,128)(2,1)}, bf16[16,128,256]{1,2,0:T(8,128)(2,1)}, u32[]{:S(2)}, u32[]{:S(2)}) collective-permute-start(bf16[16,128,256]{1,2,0:T(8,128)(2,1)} %pad_maximum_fusion.2), channel_id=1, source_target_pairs={{0,32},{8,40},{16,48},{24,56},{32,64},{40,72},{48,80},{56,88},{64,... | collective-permute-start | bytes 3145736 | tf_op jit(solution)/shard_map/ppermute | solution.py:42
  146.2 4.4 %copy-start.18 = (f32[4,128,2176]{1,2,0:T(8,128)}, f32[4,128,2176]{1,2,0:T(8,128)S(1)}, u32[]{:S(2)}) copy-start(f32[4,128,2176]{1,2,0:T(8,128)S(1)} %fusion.24) | copy-start | bytes 13369348
  168.4 9.8 %copy-start.14 = (bf16[2176,576]{0,1:T(8,128)(2,1)S(1)}, bf16[2176,576]{0,1:T(8,128)(2,1)}, u32[]{:S(2)}) copy-start(bf16[2176,576]{0,1:T(8,128)(2,1)} %copy-done.12) | copy-start | bytes 7520260
  171.5 25.4 %collective-permute-start.3 = (bf16[16,128,128]{1,2,0:T(8,128)(2,1)}, bf16[16,128,128]{1,2,0:T(8,128)(2,1)}, u32[]{:S(2)}, u32[]{:S(2)}) collective-permute-start(bf16[16,128,128]{1,2,0:T(8,128)(2,1)} %get-tuple-element.36), channel_id=1, source_target_pairs={{0,64},{8,72},{16,80},{24,88},{32,96},{40,104},{48,112},{56,120},{... | collective-permute-start | bytes 1572872 | tf_op jit(solution)/shard_map/ppermute | solution.py:42
  190.2 6.7 %copy-start.10 = (f32[16,128,256]{2,1,0:T(8,128)S(1)}, f32[16,128,256]{2,1,0:T(8,128)}, u32[]{:S(2)}) copy-start(f32[16,128,256]{2,1,0:T(8,128)} %copy-done.9) | copy-start | bytes 6291460
  190.2 6.7 %copy-start.21 = (f32[16,128,128]{1,2,0:T(8,128)S(1)}, f32[16,128,128]{1,2,0:T(8,128)}, u32[]{:S(2)}) copy-start(f32[16,128,128]{1,2,0:T(8,128)} %get-tuple-element.37) | copy-start | bytes 3145732
  196.9 16.3 %copy-start.15 = (bf16[2176,576]{0,1:T(8,128)(2,1)S(1)}, bf16[2176,576]{0,1:T(8,128)(2,1)}, u32[]{:S(2)}) copy-start(bf16[2176,576]{0,1:T(8,128)(2,1)} %copy-done.12) | copy-start | bytes 7520260
  200.2 31.1 %collective-permute-start.4 = (bf16[16,128,128]{1,2,0:T(8,128)(2,1)}, bf16[16,128,128]{1,2,0:T(8,128)(2,1)S(1)}, u32[]{:S(2)}, u32[]{:S(2)}) collective-permute-start(bf16[16,128,128]{1,2,0:T(8,128)(2,1)} %fusion.47), channel_id=1, source_target_pairs={{0,8},{8,16},{16,24},{24,32},{32,40},{40,48},{48,56},{56,64},{64,7... | collective-permute-start | bytes 1572872 | tf_op jit(solution)/shard_map/ppermute | solution.py:42
  225.2 6.1 %slice-start = ((f32[2,16,64,128]{3,2,1,0:T(8,128)}), f32[1,16,64,128]{3,2,1,0:T(8,128)S(1)}, s32[]{:S(2)}) async-start(f32[2,16,64,128]{3,2,1,0:T(8,128)} %copy-done.11), calls=%async_computation.1 | async-start | bytes 1048576 | tf_op jit(solution)/shard_map/slice | solution.py:187
  225.2 6.1 %slice-start.1 = ((f32[2,16,64,128]{3,2,1,0:T(8,128)}), f32[1,16,64,128]{3,2,1,0:T(8,128)S(1)}, s32[]{:S(2)}) async-start(f32[2,16,64,128]{3,2,1,0:T(8,128)} %copy-done.20), calls=%async_computation.2 | async-start | bytes 1048576 | tf_op jit(solution)/shard_map/slice | solution.py:187
  225.2 6.1 %copy-start.22 = (f32[1,16,64,128]{3,2,1,0:T(8,128)S(1)}, f32[1,16,64,128]{3,2,1,0:T(8,128)}, u32[]{:S(2)}) copy-start(f32[1,16,64,128]{3,2,1,0:T(8,128)} %fusion.48) | copy-start | bytes 1572868
  225.2 6.1 %copy-start.23 = (f32[1,16,64,128]{3,2,1,0:T(8,128)S(1)}, f32[1,16,64,128]{3,2,1,0:T(8,128)}, u32[]{:S(2)}) copy-start(f32[1,16,64,128]{3,2,1,0:T(8,128)} %convolution_bitcast_fusion.9) | copy-start | bytes 1572868
  (13 other events, 32.6 us)
Sparse Core Ops, SparseCore 0:
  10.5 101.3 all-gather.1
